TPU v7x, 256 devices: a whole 4x4x8 slice. The times are simulated.
256 devices in a mesh: sec: 16 (over y_lo, x, core), tile: 16 (over y_hi, z).
Axes of the slice: x: 4, y: 4 (y_hi: 2, y_lo: 2; y = y_hi * 2 + y_lo), z: 8, core: 2. Of those that a mesh axis runs over, the one named last changes fastest.
Arguments:
- displacement: float32 [2, 32, 128, 2048], P(None, 'sec', 'tile'), may hold values from -6 to 6
- velocity: float32 [2, 32, 128, 2048], P(None, 'sec', 'tile'), may hold values from -10 to 10
- frac: bfloat16 [2, 4, 32, 128, 2048], P(None, None, 'sec', 'tile'), may hold values from 0 to 1
- offsets: int32 [4, 32, 16, 2], P(None, 'sec', 'tile'), may hold values from -2 to 2
- fixed: int32 [32, 128, 2048], P('sec', 'tile'), may hold values 0 or 1
- trans: float32 [32, 2], P('sec'), may hold values from -0.3 to 0.3
Outputs:
- new_displacement: float32 [2, 32, 128, 2048], P(None, 'sec', 'tile')
- new_velocity: float32 [2, 32, 128, 2048], P(None, 'sec', 'tile')
All inputs are finite; a program needn't handle non-finite values. No bound on the sum of `fixed` on one device may be relied on, other than what follows from the above.
Results may differ from a plain program's by a relative error of at most 0.0003.
Values sent between devices are 32-bit elements; how exact they have to be, the bound alone decides.
No kernel may reach another device: no remote copies, remote signals or barrier semaphores. Data moves between devices by JAX's collectives and lax.ppermute only.
A program may use at most 64 MiB of HBM per device.

v0:
```python
import jax
import jax.numpy as jnp
from jax import lax
from jax.sharding import Mesh
from jax.sharding import PartitionSpec as P

ITERS = 3
SEC = ("sec_0", "sec_1", "sec_2")
TILE = ("tile_0", "tile_1")
SEC_TILE = ("sec_0", "sec_1", "sec_2", "tile_0", "tile_1")


in_stiff = 1.0
anchor_stiff = 0.25
cross_stiff = (0.25, 0.5, 0.5, 0.25)
reaches = (-2, -1, 1, 2)


def sent_to_all(shard, axis):
    count = lax.axis_size(axis)
    return lax.all_to_all(
        jnp.broadcast_to(shard[None], (count, *shard.shape)), axis, 0, 0, tiled=True
    )


def joined_by_halves(pieces, combine):
    while len(jax.tree.leaves(pieces)[0]) > 1:
        pieces = jax.vmap(combine)(*(pieces[side::2] for side in (0, 1)))
    return pieces[0]


def prefix(shard, axis, combine, identity):
    count, place = (lax.axis_size(axis), lax.axis_index(axis))
    passed = jnp.arange(count) < place

    def kept(part, zero, own):
        part = jnp.where(
            passed.reshape(-1, *(1 for _ in own.shape)), part, jnp.asarray(zero, own.dtype)
        )
        return part

    pieces = sent_to_all(shard, axis)
    return joined_by_halves(kept(pieces, identity, shard), combine)


def padded(cells, sides, width):
    for axis, dim in sides:
        count = lax.axis_size(axis)
        ends = count - 1
        head = lax.slice_in_dim(cells, 0, width, axis=dim)
        tail = lax.slice_in_dim(cells, cells.shape[dim] - width, cells.shape[dim], axis=dim)
        cells = jnp.concatenate(
            [
                lax.ppermute(tail, axis, [(i, (i + 1) % count) for i in range(ends)]),
                cells,
                lax.ppermute(head, axis, [((i + 1) % count, i) for i in range(ends)]),
            ],
            axis=dim,
        )
    return cells


def by_axis(shard, axes):
    for axis in axes:
        shard = lax.psum(shard, axis)
    return shard


def spring_force(ext, frac, offsets, fixed, anchor, sec_first, row_first, sections, rows):
    count = fixed.shape[0]
    height = fixed.shape[1]
    width = fixed.shape[2]
    centre = ext[:, 2 : count + 2, 3 : height + 3, :]
    grow = row_first + jnp.arange(height, dtype=jnp.int32)
    gcol = jnp.arange(width, dtype=jnp.int32)
    gsec = sec_first + jnp.arange(count, dtype=jnp.int32)
    above = ext[:, 2 : count + 2, 2 : height + 2, :]
    below = ext[:, 2 : count + 2, 4 : height + 4, :]
    left = jnp.roll(centre, 1, axis=3)
    right = jnp.roll(centre, -1, axis=3)
    force = jnp.where((grow > 0)[:, None], above - centre, 0.0)
    force = force + jnp.where((grow < rows - 1)[:, None], below - centre, 0.0)
    force = force + jnp.where((gcol > 0)[None, :], left - centre, 0.0)
    force = force + jnp.where((gcol < width - 1)[None, :], right - centre, 0.0)
    force = in_stiff * force + anchor_stiff * (jnp.transpose(anchor)[:, :, None, None] - centre)
    for index in range(4):
        reach = reaches[index]
        stiff = cross_stiff[index]
        source = ext[:, 2 + reach : 2 + reach + count]

        def pull(block, frow, fcol, shift, own, section):
            frow = frow.astype(jnp.float32)
            fcol = fcol.astype(jnp.float32)
            part_rows = lax.dynamic_slice_in_dim(block, 3 + shift[0], height + 1, 1)
            first = jnp.roll(part_rows, -shift[1], axis=2)
            second = jnp.roll(part_rows, -shift[1] - 1, axis=2)
            match = (1.0 - frow) * ((1.0 - fcol) * first[:, :height] + fcol * second[:, :height])
            match = match + frow * ((1.0 - fcol) * first[:, 1:] + fcol * second[:, 1:])
            flow = jnp.stack(
                [shift[0].astype(jnp.float32) + frow, shift[1].astype(jnp.float32) + fcol]
            )
            gap = match + flow - own
            row_ok = (grow + shift[0] >= 0) & (grow + shift[0] + 1 <= rows - 1)
            col_ok = (gcol + shift[1] >= 0) & (gcol + shift[1] + 1 <= width - 1)
            sec_ok = (section + reach >= 0) & (section + reach < sections)
            valid = row_ok[:, None] & col_ok[None, :] & sec_ok
            return jnp.where(valid, stiff * gap, 0.0)

        force = force + jax.vmap(pull, in_axes=(1, 0, 0, 0, 1, 0), out_axes=1)(
            source, frac[0, index], frac[1, index], offsets[index], centre, gsec
        )
    return force * (1 - fixed).astype(jnp.float32)[None]


def add_pair(earlier, later):
    return earlier + later


def shards(displacement, velocity, frac, offsets, fixed, trans):
    count = displacement.shape[1]
    height = displacement.shape[2]
    sections = count * lax.axis_size(SEC)
    rows = height * lax.axis_size(TILE)
    sec_first = lax.axis_index(SEC) * count
    row_first = lax.axis_index(TILE) * height
    local = jnp.cumsum(trans, 0)
    before = prefix(local[-1], SEC, add_pair, jnp.zeros((2,), jnp.float32))
    anchor = local + before[None, :]
    tile_shift = offsets[:, :, 0, :]
    keep = (1 - fixed).astype(jnp.float32)
    moving = velocity * keep[None]
    shifted = displacement
    for step in range(ITERS):
        alpha = 0.1 * 0.99**step
        delta = 0.25 * 1.1**step
        taller = padded(shifted, ((TILE, 2),), 3)
        ext = padded(taller, ((SEC, 1),), 2)
        force = spring_force(
            ext, frac, tile_shift, fixed, anchor, sec_first, row_first, sections, rows
        )
        ff, vv = (
            by_axis(jnp.sum(force * force), SEC_TILE),
            by_axis(jnp.sum(moving * moving), SEC_TILE),
        )
        ratio = jnp.sqrt(vv / (ff + 1e-06))
        moving = (1.0 - alpha) * moving + alpha * ratio * force
        moving = moving + delta * force
        shifted = shifted + delta * moving
    return (shifted, moving)


def solution(mesh):
    torus = Mesh(
        mesh.devices.reshape(2, 4, 2, 2, 8), ("sec_0", "sec_1", "sec_2", "tile_0", "tile_1")
    )
    in_specs = (
        P(None, SEC, TILE, None),
        P(None, SEC, TILE, None),
        P(None, None, SEC, TILE, None),
        P(None, SEC, TILE, None),
        P(SEC, TILE, None),
        P(SEC, None),
    )
    out_specs = (P(None, SEC, TILE, None), P(None, SEC, TILE, None))
    return jax.shard_map(
        shards, mesh=torus, in_specs=in_specs, out_specs=out_specs, check_vma=False
    )
```

profile of v0, /device:TPU:1, one launch (start us, length us, event | category | flops | bytes accessed | tf_op | source)
XLA Modules:
  0.0 454.6 jit_solution(6087241552105703784)
XLA Ops:
  8.1 6.3 %all-to-all-start = ((f32[16,1,2]{2,1,0:T(1,128)}), f32[16,1,2]{2,1,0:T(1,128)S(1)}, u32[]{:S(2)}, u32[]{:S(2)}) async-start(f32[16,1,2]{2,1,0:T(1,128)} %broadcast_in_dim.131), calls=%async_computation | async-start | bytes 16384 | tf_op jit(solution)/shard_map/all_to_all | solution.py:21
  49.9 6.7 %while.50 = (s32[]{:T(128)}, f32[2,2,9,4096]{3,2,1,0:T(8,128)S(1)}, s32[2,4]{1,0:T(2,128)}, f32[2,2,9,2048]{3,2,0,1:T(8,128)}, s32[]{:T(128)}) while((s32[]{:T(128)}, f32[2,2,9,4096]{3,2,1,0:T(8,128)S(1)}, s32[2,4]{1,0:T(2,128)}, f32[2,2,9,2048]{3,2,0,1:T(8,128)}, s32[]{:T(128)}) %tuple.539), condition=%wide.while_cond.clone.1, body=%wide.while_body.clone.1.sunk | while | flops 2 | bytes 411405 | solution.py:95
  57.4 6.7 %while.51 = (s32[]{:T(128)}, f32[2,2,9,4096]{3,2,1,0:T(8,128)S(1)}, s32[2,4]{1,0:T(2,128)}, f32[2,2,9,2048]{3,2,0,1:T(8,128)}, s32[]{:T(128)}) while((s32[]{:T(128)}, f32[2,2,9,4096]{3,2,1,0:T(8,128)S(1)}, s32[2,4]{1,0:T(2,128)}, f32[2,2,9,2048]{3,2,0,1:T(8,128)}, s32[]{:T(128)}) %tuple.600), condition=%wide.while_cond.clone.2, body=%wide.while_body.clone.2.sunk | while | flops 2 | bytes 411405 | solution.py:96
  67.1 5.6 %while.52 = (s32[]{:T(128)}, f32[2,2,9,4096]{3,2,1,0:T(8,128)S(1)}, s32[2,4]{1,0:T(2,128)S(1)}, f32[2,2,9,2048]{3,2,0,1:T(8,128)}, s32[]{:T(128)}) while((s32[]{:T(128)}, f32[2,2,9,4096]{3,2,1,0:T(8,128)S(1)}, s32[2,4]{1,0:T(2,128)S(1)}, f32[2,2,9,2048]{3,2,0,1:T(8,128)}, s32[]{:T(128)}) %tuple.618), condition=%wide.while_cond.clone.3, body=%wide.while_body.clone.3.sunk | while | flops 2 | bytes 411249 | solution.py:95
  73.5 5.6 %while.53 = (s32[]{:T(128)}, f32[2,2,9,4096]{3,2,1,0:T(8,128)S(1)}, s32[2,4]{1,0:T(2,128)S(1)}, f32[2,2,9,2048]{3,2,0,1:T(8,128)}, s32[]{:T(128)}) while((s32[]{:T(128)}, f32[2,2,9,4096]{3,2,1,0:T(8,128)S(1)}, s32[2,4]{1,0:T(2,128)S(1)}, f32[2,2,9,2048]{3,2,0,1:T(8,128)}, s32[]{:T(128)}) %tuple.616), condition=%wide.while_cond.clone.4, body=%wide.while_body.clone.4.sunk | while | flops 2 | bytes 411249 | solution.py:96
  115.7 11.1 %all-reduce.6 = (f32[]{:T(128)}, f32[]{:T(128)}) all-reduce(f32[]{:T(128)} %get-tuple-element.799, f32[]{:T(128)} %get-tuple-element.800), channel_id=1, replica_groups=mesh['sec_0'=2,'sec_1'=4,'sec_2'=2,'tile_0'=2,'tile_1'=8] {'sec_1'}, use_global_device_ids=true, to_apply=%region_2.3 | all-reduce | flops 2 | bytes 16 | tf_op jit(solution)/shard_map/psum | solution.py:65
  129.8 10.8 %all-reduce.9 = (f32[]{:T(128)}, f32[]{:T(128)}) all-reduce(f32[]{:T(128)} %get-tuple-element.793, f32[]{:T(128)} %get-tuple-element.794), channel_id=1, replica_groups=mesh['sec_0'=2,'sec_1'=4,'sec_2'=2,'tile_0'=2,'tile_1'=8] {'tile_0'}, use_global_device_ids=true, to_apply=%region_4.5 | all-reduce | flops 2 | bytes 16 | tf_op jit(solution)/shard_map/psum | solution.py:65
  140.6 13.0 %all-reduce.3 = (f32[]{:T(128)}, f32[]{:T(128)}) all-reduce(f32[]{:T(128)} %get-tuple-element.787, f32[]{:T(128)} %get-tuple-element.788), channel_id=1, replica_groups=mesh['sec_0'=2,'sec_1'=4,'sec_2'=2,'tile_0'=2,'tile_1'=8] {'tile_1'}, use_global_device_ids=true, to_apply=%region_5.6 | all-reduce | flops 2 | bytes 16 | tf_op jit(solution)/shard_map/psum | solution.py:65
  163.3 8.3 %collective-permute-start.6 = (f32[2,2,14,2048]{3,2,1,0:T(8,128)S(1)}, f32[2,2,14,2048]{3,2,1,0:T(8,128)S(1)}, u32[]{:S(2)}, u32[]{:S(2)}) collective-permute-start(f32[2,2,14,2048]{3,2,1,0:T(8,128)S(1)} %pad_maximum_fusion.24), channel_id=1, source_target_pairs={{0,16},{16,32},{32,48},{48,64},{64,80},{80,96},{96,112},{112,128},... | collective-permute-start | bytes 1376264 | tf_op jit(solution)/shard_map/ppermute | solution.py:54
  186.1 5.6 %while.58 = (s32[]{:T(128)}, f32[2,2,9,4096]{3,2,1,0:T(8,128)S(1)}, s32[2,4]{1,0:T(2,128)S(1)}, f32[2,2,9,2048]{3,2,0,1:T(8,128)}, s32[]{:T(128)}) while((s32[]{:T(128)}, f32[2,2,9,4096]{3,2,1,0:T(8,128)S(1)}, s32[2,4]{1,0:T(2,128)S(1)}, f32[2,2,9,2048]{3,2,0,1:T(8,128)}, s32[]{:T(128)}) %tuple.622), condition=%wide.while_cond.clone.9, body=%wide.while_body.clone.9.sunk | while | flops 2 | bytes 411249 | solution.py:95
  192.5 5.6 %while.59 = (s32[]{:T(128)}, f32[2,2,9,4096]{3,2,1,0:T(8,128)S(1)}, s32[2,4]{1,0:T(2,128)S(1)}, f32[2,2,9,2048]{3,2,0,1:T(8,128)}, s32[]{:T(128)}) while((s32[]{:T(128)}, f32[2,2,9,4096]{3,2,1,0:T(8,128)S(1)}, s32[2,4]{1,0:T(2,128)S(1)}, f32[2,2,9,2048]{3,2,0,1:T(8,128)}, s32[]{:T(128)}) %tuple.620), condition=%wide.while_cond.clone.10, body=%wide.while_body.clone.10.sunk | while | flops 2 | bytes 411249 | solution.py:96
  201.9 6.9 %while.60 = (s32[]{:T(128)}, f32[2,2,9,4096]{3,2,1,0:T(8,128)S(1)}, s32[2,4]{1,0:T(2,128)}, f32[2,2,9,2048]{3,2,0,1:T(8,128)}, s32[]{:T(128)}) while((s32[]{:T(128)}, f32[2,2,9,4096]{3,2,1,0:T(8,128)S(1)}, s32[2,4]{1,0:T(2,128)}, f32[2,2,9,2048]{3,2,0,1:T(8,128)}, s32[]{:T(128)}) %tuple.557), condition=%wide.while_cond.clone.11, body=%wide.while_body.clone.11.sunk | while | flops 2 | bytes 411249 | solution.py:95
  209.7 6.6 %while.61 = (s32[]{:T(128)}, f32[2,2,9,4096]{3,2,1,0:T(8,128)S(1)}, s32[2,4]{1,0:T(2,128)}, f32[2,2,9,2048]{3,2,0,1:T(8,128)}, s32[]{:T(128)}) while((s32[]{:T(128)}, f32[2,2,9,4096]{3,2,1,0:T(8,128)S(1)}, s32[2,4]{1,0:T(2,128)}, f32[2,2,9,2048]{3,2,0,1:T(8,128)}, s32[]{:T(128)}) %tuple.605), condition=%wide.while_cond.clone.12, body=%wide.while_body.clone.12.sunk | while | flops 2 | bytes 411249 | solution.py:96
  220.1 6.8 %while.56 = (s32[]{:T(128)}, f32[2,2,9,4096]{3,2,1,0:T(8,128)S(1)}, s32[2,4]{1,0:T(2,128)}, f32[2,2,9,2048]{3,2,0,1:T(8,128)}, s32[]{:T(128)}) while((s32[]{:T(128)}, f32[2,2,9,4096]{3,2,1,0:T(8,128)S(1)}, s32[2,4]{1,0:T(2,128)}, f32[2,2,9,2048]{3,2,0,1:T(8,128)}, s32[]{:T(128)}) %tuple.569), condition=%wide.while_cond.clone.7, body=%wide.while_body.clone.7.sunk | while | flops 2 | bytes 411249 | solution.py:95
  227.8 6.8 %while.57 = (s32[]{:T(128)}, f32[2,2,9,4096]{3,2,1,0:T(8,128)S(1)}, s32[2,4]{1,0:T(2,128)}, f32[2,2,9,2048]{3,2,0,1:T(8,128)}, s32[]{:T(128)}) while((s32[]{:T(128)}, f32[2,2,9,4096]{3,2,1,0:T(8,128)S(1)}, s32[2,4]{1,0:T(2,128)}, f32[2,2,9,2048]{3,2,0,1:T(8,128)}, s32[]{:T(128)}) %tuple.606), condition=%wide.while_cond.clone.8, body=%wide.while_body.clone.8.sunk | while | flops 2 | bytes 411249 | solution.py:96
  238.4 6.8 %while.62 = (s32[]{:T(128)}, f32[2,2,9,4096]{3,2,1,0:T(8,128)S(1)}, s32[2,4]{1,0:T(2,128)}, f32[2,2,9,2048]{3,2,0,1:T(8,128)}, s32[]{:T(128)}) while((s32[]{:T(128)}, f32[2,2,9,4096]{3,2,1,0:T(8,128)S(1)}, s32[2,4]{1,0:T(2,128)}, f32[2,2,9,2048]{3,2,0,1:T(8,128)}, s32[]{:T(128)}) %tuple.551), condition=%wide.while_cond.clone.13, body=%wide.while_body.clone.13.sunk | while | flops 2 | bytes 411249 | solution.py:95
  246.0 6.9 %while.63 = (s32[]{:T(128)}, f32[2,2,9,4096]{3,2,1,0:T(8,128)S(1)}, s32[2,4]{1,0:T(2,128)}, f32[2,2,9,2048]{3,2,0,1:T(8,128)}, s32[]{:T(128)}) while((s32[]{:T(128)}, f32[2,2,9,4096]{3,2,1,0:T(8,128)S(1)}, s32[2,4]{1,0:T(2,128)}, f32[2,2,9,2048]{3,2,0,1:T(8,128)}, s32[]{:T(128)}) %tuple.607), condition=%wide.while_cond.clone.14, body=%wide.while_body.clone.14.sunk | while | flops 2 | bytes 411249 | solution.py:96
  263.3 11.4 %all-reduce.5 = (f32[]{:T(128)}, f32[]{:T(128)}) all-reduce(f32[]{:T(128)} %get-tuple-element.797, f32[]{:T(128)} %get-tuple-element.798), channel_id=1, replica_groups=mesh['sec_0'=2,'sec_1'=4,'sec_2'=2,'tile_0'=2,'tile_1'=8] {'sec_1'}, use_global_device_ids=true, to_apply=%region_15.17 | all-reduce | flops 2 | bytes 16 | tf_op jit(solution)/shard_map/psum | solution.py:65
  277.8 9.0 %all-reduce.8 = (f32[]{:T(128)}, f32[]{:T(128)}) all-reduce(f32[]{:T(128)} %get-tuple-element.791, f32[]{:T(128)} %get-tuple-element.792), channel_id=1, replica_groups=mesh['sec_0'=2,'sec_1'=4,'sec_2'=2,'tile_0'=2,'tile_1'=8] {'tile_0'}, use_global_device_ids=true, to_apply=%region_17.19 | all-reduce | flops 2 | bytes 16 | tf_op jit(solution)/shard_map/psum | solution.py:65
  286.8 16.7 %all-reduce.2 = (f32[]{:T(128)}, f32[]{:T(128)}) all-reduce(f32[]{:T(128)} %get-tuple-element.785, f32[]{:T(128)} %get-tuple-element.786), channel_id=1, replica_groups=mesh['sec_0'=2,'sec_1'=4,'sec_2'=2,'tile_0'=2,'tile_1'=8] {'tile_1'}, use_global_device_ids=true, to_apply=%region_18.20 | all-reduce | flops 2 | bytes 16 | tf_op jit(solution)/shard_map/psum | solution.py:65
  312.8 8.3 %collective-permute-start.10 = (f32[2,2,14,2048]{3,2,1,0:T(8,128)S(1)}, f32[2,2,14,2048]{3,2,1,0:T(8,128)S(1)}, u32[]{:S(2)}, u32[]{:S(2)}) collective-permute-start(f32[2,2,14,2048]{3,2,1,0:T(8,128)S(1)} %pad_maximum_fusion.25), channel_id=1, source_target_pairs={{0,16},{16,32},{32,48},{48,64},{64,80},{80,96},{96,112},{112,128},... | collective-permute-start | bytes 1376264 | tf_op jit(solution)/shard_map/ppermute | solution.py:54
  335.7 6.9 %while.66 = (s32[]{:T(128)}, f32[2,2,9,4096]{3,2,1,0:T(8,128)S(1)}, s32[2,4]{1,0:T(2,128)}, f32[2,2,9,2048]{3,2,0,1:T(8,128)}, s32[]{:T(128)}) while((s32[]{:T(128)}, f32[2,2,9,4096]{3,2,1,0:T(8,128)S(1)}, s32[2,4]{1,0:T(2,128)}, f32[2,2,9,2048]{3,2,0,1:T(8,128)}, s32[]{:T(128)}) %tuple.623), condition=%wide.while_cond.clone.17, body=%wide.while_body.clone.17.sunk | while | flops 2 | bytes 411405 | solution.py:95
  343.3 6.5 %while.67 = (s32[]{:T(128)}, f32[2,2,9,4096]{3,2,1,0:T(8,128)S(1)}, s32[2,4]{1,0:T(2,128)}, f32[2,2,9,2048]{3,2,0,1:T(8,128)}, s32[]{:T(128)}) while((s32[]{:T(128)}, f32[2,2,9,4096]{3,2,1,0:T(8,128)S(1)}, s32[2,4]{1,0:T(2,128)}, f32[2,2,9,2048]{3,2,0,1:T(8,128)}, s32[]{:T(128)}) %tuple.621), condition=%wide.while_cond.clone.18, body=%wide.while_body.clone.18.sunk | while | flops 2 | bytes 411405 | solution.py:96
  353.6 6.8 %while.68 = (s32[]{:T(128)}, f32[2,2,9,4096]{3,2,1,0:T(8,128)S(1)}, s32[2,4]{1,0:T(2,128)}, f32[2,2,9,2048]{3,2,0,1:T(8,128)}, s32[]{:T(128)}) while((s32[]{:T(128)}, f32[2,2,9,4096]{3,2,1,0:T(8,128)S(1)}, s32[2,4]{1,0:T(2,128)}, f32[2,2,9,2048]{3,2,0,1:T(8,128)}, s32[]{:T(128)}) %tuple.619), condition=%wide.while_cond.clone.19, body=%wide.while_body.clone.19.sunk | while | flops 2 | bytes 411405 | solution.py:95
  361.3 6.7 %while.69 = (s32[]{:T(128)}, f32[2,2,9,4096]{3,2,1,0:T(8,128)S(1)}, s32[2,4]{1,0:T(2,128)}, f32[2,2,9,2048]{3,2,0,1:T(8,128)}, s32[]{:T(128)}) while((s32[]{:T(128)}, f32[2,2,9,4096]{3,2,1,0:T(8,128)S(1)}, s32[2,4]{1,0:T(2,128)}, f32[2,2,9,2048]{3,2,0,1:T(8,128)}, s32[]{:T(128)}) %tuple.617), condition=%wide.while_cond.clone.20, body=%wide.while_body.clone.20.sunk | while | flops 2 | bytes 411405 | solution.py:96
  371.8 6.6 %while.64 = (s32[]{:T(128)}, f32[2,2,9,4096]{3,2,1,0:T(8,128)S(1)}, s32[2,4]{1,0:T(2,128)}, f32[2,2,9,2048]{3,2,0,1:T(8,128)}, s32[]{:T(128)}) while((s32[]{:T(128)}, f32[2,2,9,4096]{3,2,1,0:T(8,128)S(1)}, s32[2,4]{1,0:T(2,128)}, f32[2,2,9,2048]{3,2,0,1:T(8,128)}, s32[]{:T(128)}) %tuple.615), condition=%wide.while_cond.clone.15, body=%wide.while_body.clone.15.sunk | while | flops 2 | bytes 411405 | solution.py:95
  379.2 6.7 %while.65 = (s32[]{:T(128)}, f32[2,2,9,4096]{3,2,1,0:T(8,128)S(1)}, s32[2,4]{1,0:T(2,128)}, f32[2,2,9,2048]{3,2,0,1:T(8,128)}, s32[]{:T(128)}) while((s32[]{:T(128)}, f32[2,2,9,4096]{3,2,1,0:T(8,128)S(1)}, s32[2,4]{1,0:T(2,128)}, f32[2,2,9,2048]{3,2,0,1:T(8,128)}, s32[]{:T(128)}) %tuple.613), condition=%wide.while_cond.clone.16, body=%wide.while_body.clone.16.sunk | while | flops 2 | bytes 411405 | solution.py:96
  389.8 6.7 %while.70 = (s32[]{:T(128)}, f32[2,2,9,4096]{3,2,1,0:T(8,128)S(1)}, s32[2,4]{1,0:T(2,128)}, f32[2,2,9,2048]{3,2,0,1:T(8,128)}, s32[]{:T(128)}) while((s32[]{:T(128)}, f32[2,2,9,4096]{3,2,1,0:T(8,128)S(1)}, s32[2,4]{1,0:T(2,128)}, f32[2,2,9,2048]{3,2,0,1:T(8,128)}, s32[]{:T(128)}) %tuple.609), condition=%wide.while_cond.clone.21, body=%wide.while_body.clone.21.sunk | while | flops 2 | bytes 411405 | solution.py:95
  397.3 6.7 %while.71 = (s32[]{:T(128)}, f32[2,2,9,4096]{3,2,1,0:T(8,128)S(1)}, s32[2,4]{1,0:T(2,128)}, f32[2,2,9,2048]{3,2,0,1:T(8,128)}, s32[]{:T(128)}) while((s32[]{:T(128)}, f32[2,2,9,4096]{3,2,1,0:T(8,128)S(1)}, s32[2,4]{1,0:T(2,128)}, f32[2,2,9,2048]{3,2,0,1:T(8,128)}, s32[]{:T(128)}) %tuple.611), condition=%wide.while_cond.clone.22, body=%wide.while_body.clone.22.sunk | while | flops 2 | bytes 411405 | solution.py:96
  414.6 10.8 %all-reduce.4 = (f32[]{:T(128)}, f32[]{:T(128)}) all-reduce(f32[]{:T(128)} %get-tuple-element.795, f32[]{:T(128)} %get-tuple-element.796), channel_id=1, replica_groups=mesh['sec_0'=2,'sec_1'=4,'sec_2'=2,'tile_0'=2,'tile_1'=8] {'sec_1'}, use_global_device_ids=true, to_apply=%region_27.29 | all-reduce | flops 2 | bytes 16 | tf_op jit(solution)/shard_map/psum | solution.py:65
  428.6 7.0 %all-reduce.7 = (f32[]{:T(128)}, f32[]{:T(128)}) all-reduce(f32[]{:T(128)} %get-tuple-element.789, f32[]{:T(128)} %get-tuple-element.790), channel_id=1, replica_groups=mesh['sec_0'=2,'sec_1'=4,'sec_2'=2,'tile_0'=2,'tile_1'=8] {'tile_0'}, use_global_device_ids=true, to_apply=%region_29.31 | all-reduce | flops 2 | bytes 16 | tf_op jit(solution)/shard_map/psum | solution.py:65
  435.6 16.7 %all-reduce.1 = (f32[]{:T(128)}, f32[]{:T(128)}) all-reduce(f32[]{:T(128)} %get-tuple-element.783, f32[]{:T(128)} %get-tuple-element.784), channel_id=1, replica_groups=mesh['sec_0'=2,'sec_1'=4,'sec_2'=2,'tile_0'=2,'tile_1'=8] {'tile_1'}, use_global_device_ids=true, to_apply=%region_30.32 | all-reduce | flops 2 | bytes 16 | tf_op jit(solution)/shard_map/psum | solution.py:65
  (508 shorter events, 337.8 us)
Async XLA Ops:
  0.6 17.8 %copy-start.1 = (bf16[2,4,2,8,2048]{4,3,2,1,0:T(8,128)(2,1)S(1)}, bf16[2,4,2,8,2048]{4,3,2,1,0:T(8,128)(2,1)}, u32[]{:S(2)}) copy-start(bf16[2,4,2,8,2048]{4,3,2,1,0:T(8,128)(2,1)} %param.10) | copy-start | bytes 1572868
  1.8 29.3 %collective-permute-start = (f32[2,2,3,2048]{3,2,1,0:T(4,128)S(1)}, f32[2,2,3,2048]{3,2,1,0:T(4,128)S(1)}, u32[]{:S(2)}, u32[]{:S(2)}) collective-permute-start(f32[2,2,3,2048]{3,2,1,0:T(4,128)S(1)} %get-tuple-element.908), channel_id=1, source_target_pairs={{0,1},{1,2},{2,3},{3,4},{4,5},{5,6},{6,7},{7,8},{8,9},{9,10},{10,1... | collective-permute-start | bytes 294920 | tf_op jit(solution)/shard_map/ppermute | solution.py:54
  6.2 25.6 %collective-permute-start.1 = (f32[2,2,3,2048]{3,2,1,0:T(4,128)S(1)}, f32[2,2,3,2048]{3,2,1,0:T(4,128)S(1)}, u32[]{:S(2)}, u32[]{:S(2)}) collective-permute-start(f32[2,2,3,2048]{3,2,1,0:T(4,128)S(1)} %get-tuple-element.907), channel_id=1, source_target_pairs={{1,0},{2,1},{3,2},{4,3},{5,4},{6,5},{7,6},{8,7},{9,8},{10,9},{11,1... | collective-permute-start | bytes 294920 | tf_op jit(solution)/shard_map/ppermute | solution.py:56
  8.1 22.9 %all-to-all-start = ((f32[16,1,2]{2,1,0:T(1,128)}), f32[16,1,2]{2,1,0:T(1,128)S(1)}, u32[]{:S(2)}, u32[]{:S(2)}) async-start(f32[16,1,2]{2,1,0:T(1,128)} %broadcast_in_dim.131), calls=%async_computation | async-start | bytes 16384 | tf_op jit(solution)/shard_map/all_to_all | solution.py:21
  19.2 86.1 %copy-start.2 = (f32[2,8,2048]{2,1,0:T(8,128)}, f32[2,8,2048]{2,1,0:T(8,128)S(1)}, u32[]{:S(2)}) copy-start(f32[2,8,2048]{2,1,0:T(8,128)S(1)} %get-tuple-element.868) | copy-start | bytes 393220
  19.2 86.1 %copy-start.4 = (f32[2,8,2048]{2,1,0:T(8,128)}, f32[2,8,2048]{2,1,0:T(8,128)S(1)}, u32[]{:S(2)}) copy-start(f32[2,8,2048]{2,1,0:T(8,128)S(1)} %get-tuple-element.869) | copy-start | bytes 393220
  20.8 6.2 %copy-start.33 = (s32[2,8,2048]{2,1,0:T(8,128)S(1)}, s32[2,8,2048]{2,1,0:T(8,128)}, u32[]{:S(2)}) copy-start(s32[2,8,2048]{2,1,0:T(8,128)} %param.12) | copy-start | bytes 393220
  31.8 15.1 %copy-start.32 = (f32[2,2,3,2048]{3,2,1,0:T(4,128)}, f32[2,2,3,2048]{3,2,1,0:T(4,128)S(1)}, u32[]{:S(2)}) copy-start(f32[2,2,3,2048]{3,2,1,0:T(4,128)S(1)} %collective-permute-done.1) | copy-start | bytes 294916
  31.9 9.0 %copy-start.28 = (f32[2,2,14,2048]{3,0,1,2:T(2,128)}, f32[2,2,14,2048]{3,0,1,2:T(2,128)S(1)}, u32[]{:S(2)}) copy-start(f32[2,2,14,2048]{3,0,1,2:T(2,128)S(1)} %copy_dynamic-update-slice_fusion.1) | copy-start | bytes 1376260
  31.9 8.9 %collective-permute-start.2 = (f32[2,2,14,2048]{3,0,1,2:T(2,128)S(1)}, f32[2,2,14,2048]{3,0,1,2:T(2,128)S(1)}, u32[]{:S(2)}, u32[]{:S(2)}) collective-permute-start(f32[2,2,14,2048]{3,0,1,2:T(2,128)S(1)} %copy_dynamic-update-slice_fusion.1), channel_id=1, source_target_pairs={{0,16},{16,32},{32,48},{48,64},{64,80},{80,96},{96,112},{112,128},... | collective-permute-start | bytes 1376264 | tf_op jit(solution)/shard_map/ppermute | solution.py:54
  35.4 9.8 %collective-permute-start.3 = (f32[2,2,14,2048]{3,0,1,2:T(2,128)S(1)}, f32[2,2,14,2048]{3,0,1,2:T(2,128)S(1)}, u32[]{:S(2)}, u32[]{:S(2)}) collective-permute-start(f32[2,2,14,2048]{3,0,1,2:T(2,128)S(1)} %copy_dynamic-update-slice_fusion.1), channel_id=1, source_target_pairs={{16,0},{32,16},{48,32},{64,48},{80,64},{96,80},{112,96},{128,112},... | collective-permute-start | bytes 1376264 | tf_op jit(solution)/shard_map/ppermute | solution.py:56
  95.3 10.1 %copy-start.14 = (f32[2,8,2048]{2,1,0:T(8,128)S(1)}, f32[2,8,2048]{2,1,0:T(8,128)}, u32[]{:S(2)}) copy-start(f32[2,8,2048]{2,1,0:T(8,128)} %get-tuple-element.878) | copy-start | bytes 393220
  95.3 10.1 %copy-start.15 = (f32[2,8,2048]{2,1,0:T(8,128)S(1)}, f32[2,8,2048]{2,1,0:T(8,128)}, u32[]{:S(2)}) copy-start(f32[2,8,2048]{2,1,0:T(8,128)} %get-tuple-element.879) | copy-start | bytes 393220
  99.1 6.3 %copy-start.10 = (f32[2,8,2048]{2,1,0:T(8,128)S(1)}, f32[2,8,2048]{2,1,0:T(8,128)}, u32[]{:S(2)}) copy-start(f32[2,8,2048]{2,1,0:T(8,128)} %get-tuple-element.874) | copy-start | bytes 393220
  99.1 6.3 %copy-start.11 = (f32[2,8,2048]{2,1,0:T(8,128)S(1)}, f32[2,8,2048]{2,1,0:T(8,128)}, u32[]{:S(2)}) copy-start(f32[2,8,2048]{2,1,0:T(8,128)} %get-tuple-element.875) | copy-start | bytes 393220
  99.1 6.3 %copy-start.12 = (f32[2,8,2048]{2,1,0:T(8,128)S(1)}, f32[2,8,2048]{2,1,0:T(8,128)}, u32[]{:S(2)}) copy-start(f32[2,8,2048]{2,1,0:T(8,128)} %get-tuple-element.876) | copy-start | bytes 393220
  99.1 6.3 %copy-start.13 = (f32[2,8,2048]{2,1,0:T(8,128)S(1)}, f32[2,8,2048]{2,1,0:T(8,128)}, u32[]{:S(2)}) copy-start(f32[2,8,2048]{2,1,0:T(8,128)} %get-tuple-element.877) | copy-start | bytes 393220
  106.1 48.8 %copy-start.27 = (f32[2,2,8,2048]{3,2,1,0:T(8,128)S(1)}, f32[2,2,8,2048]{3,2,1,0:T(8,128)}, u32[]{:S(2)}) copy-start(f32[2,2,8,2048]{3,2,1,0:T(8,128)} %param.9) | copy-start | bytes 786436
  155.8 3.6 collective-permute-start.4
  157.5 5.7 %collective-permute-start.5 = (f32[2,2,3,2048]{3,2,1,0:T(4,128)S(1)}, f32[2,2,3,2048]{3,2,1,0:T(4,128)S(1)}, u32[]{:S(2)}, u32[]{:S(2)}) collective-permute-start(f32[2,2,3,2048]{3,2,1,0:T(4,128)S(1)} %get-tuple-element.902), channel_id=1, source_target_pairs={{1,0},{2,1},{3,2},{4,3},{5,4},{6,5},{7,6},{8,7},{9,8},{10,9},{11,1... | collective-permute-start | bytes 294920 | tf_op jit(solution)/shard_map/ppermute | solution.py:56
  159.4 22.7 %copy-start.24 = (f32[2,2,3,2048]{3,2,1,0:T(4,128)}, f32[2,2,3,2048]{3,2,1,0:T(4,128)S(1)}, u32[]{:S(2)}) copy-start(f32[2,2,3,2048]{3,2,1,0:T(4,128)S(1)} %collective-permute-done.4) | copy-start | bytes 294916
  163.2 18.9 %copy-start.25 = (f32[2,2,3,2048]{3,2,1,0:T(4,128)}, f32[2,2,3,2048]{3,2,1,0:T(4,128)S(1)}, u32[]{:S(2)}) copy-start(f32[2,2,3,2048]{3,2,1,0:T(4,128)S(1)} %collective-permute-done.5) | copy-start | bytes 294916
  163.3 14.4 %collective-permute-start.6 = (f32[2,2,14,2048]{3,2,1,0:T(8,128)S(1)}, f32[2,2,14,2048]{3,2,1,0:T(8,128)S(1)}, u32[]{:S(2)}, u32[]{:S(2)}) collective-permute-start(f32[2,2,14,2048]{3,2,1,0:T(8,128)S(1)} %pad_maximum_fusion.24), channel_id=1, source_target_pairs={{0,16},{16,32},{32,48},{48,64},{64,80},{80,96},{96,112},{112,128},... | collective-permute-start | bytes 1376264 | tf_op jit(solution)/shard_map/ppermute | solution.py:54
  171.6 10.5 %collective-permute-start.7 = (f32[2,2,14,2048]{3,2,1,0:T(8,128)S(1)}, f32[2,2,14,2048]{3,2,1,0:T(8,128)S(1)}, u32[]{:S(2)}, u32[]{:S(2)}) collective-permute-start(f32[2,2,14,2048]{3,2,1,0:T(8,128)S(1)} %pad_maximum_fusion.24), channel_id=1, source_target_pairs={{16,0},{32,16},{48,32},{64,48},{80,64},{96,80},{112,96},{128,112},... | collective-permute-start | bytes 1376264 | tf_op jit(solution)/shard_map/ppermute | solution.py:56
  246.0 6.9 %copy-start.3 = (f32[2,8,2048]{2,1,0:T(8,128)S(1)}, f32[2,8,2048]{2,1,0:T(8,128)}, u32[]{:S(2)}) copy-start(f32[2,8,2048]{2,1,0:T(8,128)} %copy-done.2) | copy-start | bytes 393220
  246.0 7.0 %copy-start.5 = (f32[2,8,2048]{2,1,0:T(8,128)S(1)}, f32[2,8,2048]{2,1,0:T(8,128)}, u32[]{:S(2)}) copy-start(f32[2,8,2048]{2,1,0:T(8,128)} %copy-done.4) | copy-start | bytes 393220
  305.7 3.2 collective-permute-start.8
  307.0 5.7 %collective-permute-start.9 = (f32[2,2,3,2048]{3,2,1,0:T(4,128)S(1)}, f32[2,2,3,2048]{3,2,1,0:T(4,128)S(1)}, u32[]{:S(2)}, u32[]{:S(2)}) collective-permute-start(f32[2,2,3,2048]{3,2,1,0:T(4,128)S(1)} %get-tuple-element.896), channel_id=1, source_target_pairs={{1,0},{2,1},{3,2},{4,3},{5,4},{6,5},{7,6},{8,7},{9,8},{10,9},{11,1... | collective-permute-start | bytes 294920 | tf_op jit(solution)/shard_map/ppermute | solution.py:56
  308.9 22.7 %copy-start.22 = (f32[2,2,3,2048]{3,2,1,0:T(4,128)}, f32[2,2,3,2048]{3,2,1,0:T(4,128)S(1)}, u32[]{:S(2)}) copy-start(f32[2,2,3,2048]{3,2,1,0:T(4,128)S(1)} %collective-permute-done.8) | copy-start | bytes 294916
  312.7 18.9 %copy-start.23 = (f32[2,2,3,2048]{3,2,1,0:T(4,128)}, f32[2,2,3,2048]{3,2,1,0:T(4,128)S(1)}, u32[]{:S(2)}) copy-start(f32[2,2,3,2048]{3,2,1,0:T(4,128)S(1)} %collective-permute-done.9) | copy-start | bytes 294916
  312.8 14.4 %collective-permute-start.10 = (f32[2,2,14,2048]{3,2,1,0:T(8,128)S(1)}, f32[2,2,14,2048]{3,2,1,0:T(8,128)S(1)}, u32[]{:S(2)}, u32[]{:S(2)}) collective-permute-start(f32[2,2,14,2048]{3,2,1,0:T(8,128)S(1)} %pad_maximum_fusion.25), channel_id=1, source_target_pairs={{0,16},{16,32},{32,48},{48,64},{64,80},{80,96},{96,112},{112,128},... | collective-permute-start | bytes 1376264 | tf_op jit(solution)/shard_map/ppermute | solution.py:54
  321.1 10.5 %collective-permute-start.11 = (f32[2,2,14,2048]{3,2,1,0:T(8,128)S(1)}, f32[2,2,14,2048]{3,2,1,0:T(8,128)S(1)}, u32[]{:S(2)}, u32[]{:S(2)}) collective-permute-start(f32[2,2,14,2048]{3,2,1,0:T(8,128)S(1)} %pad_maximum_fusion.25), channel_id=1, source_target_pairs={{16,0},{32,16},{48,32},{64,48},{80,64},{96,80},{112,96},{128,112},... | collective-permute-start | bytes 1376264 | tf_op jit(solution)/shard_map/ppermute | solution.py:56
  (71 other events, 97.4 us)
where the time goes:
time: 460 us; the launch traced here: 455 us
  local copies, waits for them, and re-layouts  212 us (46%)
  blocking collectives  129 us (28%)
  starting transfers between devices  43.8 us (10%)
  other arithmetic  34.5 us (8%)
  waiting for transfers between devices  28.5 us (6%)
  between operations  5.72 us (1%)
    psum x15, blocking collectives, by_axis(): shard = lax.psum(shard, axis)  129 us
    another operation x113, local copies, waits for them, and re-layouts, pull(): first = jnp.roll(part_rows, -shift[1], axis=2)  92.1 us
    another operation x76, local copies, waits for them, and re-layouts, pull(): second = jnp.roll(part_rows, -shift[1] - 1, axis=2)  71.5 us
    ppermute x6, starting transfers between devices, padded(): lax.ppermute(tail, axis, [(i, (i + 1) % count) for i in range(ends)])  27.5 us
    ppermute x6, waiting for transfers between devices, padded(): lax.ppermute(head, axis, [((i + 1) % count, i) for i in range(ends)])  20.8 us
    reduce_sum x3, other arithmetic, shards(): jnp.sum(force * force)  15.6 us
    gather x40, local copies, waits for them, and re-layouts  13 us
    gather x12, local copies, waits for them, and re-layouts, pull(): part_rows = lax.dynamic_slice_in_dim(block, 3 + shift[0], height + 1, 1)  10.4 us
  transfers between devices with their start and end apart: 13, of which 8 were waited for; matrix products, arithmetic and copies ran while one was open for 5% of the time, Pallas kernels for 0%

commit v1 on v0

v1 whole, which is shorter than its diff:
```python
import jax
import jax.numpy as jnp
from jax import lax
from jax.experimental import pallas as pl
from jax.experimental.pallas import tpu as pltpu
from jax.sharding import Mesh
from jax.sharding import PartitionSpec as P

ITERS = 3
SEC = ("sec_0", "sec_1", "sec_2")
TILE = ("tile_0", "tile_1")
SEC_TILE = SEC + TILE

in_stiff = 1.0
anchor_stiff = 0.25
cross_stiff = (0.25, 0.5, 0.5, 0.25)
reaches = (-2, -1, 1, 2)
ALPHAS = tuple(0.1 * 0.99**k for k in range(ITERS))
DELTAS = tuple(0.25 * 1.1**k for k in range(ITERS))
UP, DOWN = 2, 3
TINY = 1e-06
NB = 6
PAIRS = [(i, j) for i in range(NB) for j in range(i, NB)]
CANCEL = 1000.0

VMEM = pl.BlockSpec(memory_space=pltpu.VMEM)
SMEM = pl.BlockSpec(memory_space=pltpu.SMEM)


def params():
    return pltpu.CompilerParams(vmem_limit_bytes=48 << 20)


def call(body, out_shape, in_specs, name, flops=4_000_000, bytes_accessed=4_000_000, scratch=()):
    multi = isinstance(out_shape, (list, tuple))
    return pl.pallas_call(
        body,
        out_shape=out_shape,
        in_specs=in_specs,
        out_specs=[VMEM] * len(out_shape) if multi else VMEM,
        scratch_shapes=list(scratch),
        compiler_params=params(),
        cost_estimate=pl.CostEstimate(flops=flops, bytes_accessed=bytes_accessed, transcendentals=0),
        name=name,
    )


def f32(*shape):
    return jax.ShapeDtypeStruct(shape, jnp.float32)


def relayout(u_ref, vel_ref, fixed_ref, out_ref):
    comps, count, height, width = u_ref.shape
    q = width // 128
    for s in range(count):
        for j in range(q):
            cols = pl.ds(128 * j, 128)
            keep = (1 - fixed_ref[s, :, cols]).astype(jnp.float32)
            for c in range(comps):
                rows = pl.ds(j, height, stride=q)
                out_ref.at[0, c, s][rows, :] = u_ref[c, s, :, cols]
                out_ref.at[1, c, s][rows, :] = vel_ref[c, s, :, cols] * keep


def weights(
    place_ref, offsets_ref, anchor_ref, frac_ref, fixed_ref,
    w_ref, diag_ref, keep_ref, base_ref,
):
    count, height, width = fixed_ref.shape
    q = width // 128
    sec_first, row_first, sections, rows = (place_ref[k] for k in range(4))
    grow = row_first + lax.broadcasted_iota(jnp.int32, (height, 128), 0)
    lane = lax.broadcasted_iota(jnp.int32, (height, 128), 1)
    row_links = (grow > 0).astype(jnp.float32) + (grow < rows - 1).astype(jnp.float32)
    for s in range(count):
        shift, row_stiff = [], []
        for i in range(4):
            dr, dc = offsets_ref[i * count * 2 + s * 2], offsets_ref[i * count * 2 + s * 2 + 1]
            other = sec_first + s + reaches[i]
            there = ((other >= 0) & (other < sections)).astype(jnp.float32) * cross_stiff[i]
            row_ok = (grow + dr >= 0) & (grow + dr + 1 <= rows - 1)
            shift.append((dr, dc))
            row_stiff.append(jnp.where(row_ok, there, 0.0))
        for j in range(q):
            cols = pl.ds(128 * j, 128)
            gcol = lane + 128 * j
            keep = (1 - fixed_ref[s, :, cols]).astype(jnp.float32)
            total = jnp.zeros((height, 128), jnp.float32)
            base = [keep * (anchor_stiff * anchor_ref[s * 2 + c]) for c in range(2)]
            at = pl.ds(j, height, stride=q)
            for i in range(4):
                dr, dc = shift[i]
                col_ok = (gcol + dc >= 0) & (gcol + dc + 1 <= width - 1)
                stiff = jnp.where(col_ok, row_stiff[i], 0.0) * keep
                frow = frac_ref[0, i, s, :, cols].astype(jnp.float32)
                fcol = frac_ref[1, i, s, :, cols].astype(jnp.float32)
                low = stiff * frow
                high = stiff - low
                w11 = low * fcol
                w01 = high * fcol
                w_ref.at[s, i, 0][at, :] = high - w01
                w_ref.at[s, i, 1][at, :] = w01
                w_ref.at[s, i, 2][at, :] = low - w11
                w_ref.at[s, i, 3][at, :] = w11
                total = total + stiff
                base[0] = base[0] + stiff * (dr.astype(jnp.float32) + frow)
                base[1] = base[1] + stiff * (dc.astype(jnp.float32) + fcol)
            links = row_links + (gcol > 0).astype(jnp.float32) + (gcol < width - 1).astype(jnp.float32)
            diag_ref.at[s][at, :] = total + keep * (in_stiff * links + anchor_stiff)
            keep_ref.at[s][at, :] = keep * in_stiff
            for c in range(2):
                base_ref.at[c, s][at, :] = base[c]


def apply_springs(offsets_ref, ext, left, right, w, diag, keep, base, out, affine):
    vecs, comps, count, tall, q, lanes = ext.shape
    height = tall - UP - DOWN
    lane = lax.broadcasted_iota(jnp.int32, (q, lanes), 1)
    sub = lax.broadcasted_iota(jnp.int32, (q, lanes), 0)
    first = (sub == 0) & (lane == 0)
    last = (sub == q - 1) & (lane == lanes - 1)
    for s in range(count):
        for r in range(height):
            at = pl.ds(r * q, q)
            kept, own = keep[s, at, :], diag[s, at, :]
            for v in range(vecs):
                for c in range(comps):
                    x = ext[v, c, s, r + UP]
                    before = jnp.where(lane < lanes - 1, x, pltpu.roll(x, 1, 0))
                    after = jnp.where(lane >= 1, x, pltpu.roll(x, q - 1, 0))
                    before = jnp.where(first, 0.0, pltpu.roll(before, 1, 1))
                    after = jnp.where(last, 0.0, pltpu.roll(after, lanes - 1, 1))
                    near = ext[v, c, s, r + UP - 1] + ext[v, c, s, r + UP + 1] + before + after
                    y = kept * near - own * x
                    if affine[v]:
                        y = y + base[c, s, at, :]
                    out[v, c, s, r] = y
        for i in range(4):
            slot = s + 2 + reaches[i]
            source = (left, ext, right)[slot // count]
            index = slot % count
            dr, dc = offsets_ref[i * count * 2 + s * 2], offsets_ref[i * count * 2 + s * 2 + 1]
            ahead = dc >= 0
            turn = jnp.where(ahead, q - 1, 1)
            shift0 = lax.rem(lanes - dc, lanes)
            shift1 = lax.rem(lanes - dc - 1, lanes)
            low0 = jnp.where(ahead, dc, 0)
            high0 = jnp.where(ahead, lanes, lanes + dc)
            low1 = jnp.where(ahead, dc + 1, 0)
            high1 = jnp.where(ahead, lanes, lanes + dc + 1)
            own0 = (lane >= low0) & (lane < high0)
            own1 = (lane >= low1) & (lane < high1)
            held = {}
            for k in range(height + 1):
                if k > 0:
                    at = pl.ds((k - 1) * q, q)
                    w00, w01, w10, w11 = (w[s, i, n, at, :] for n in range(4))
                for v in range(vecs):
                    for c in range(comps):
                        x = source[v, c, index, k + UP + dr]
                        y = pltpu.roll(x, turn, 0)
                        a0 = pltpu.roll(jnp.where(own0, x, y), shift0, 1)
                        a1 = pltpu.roll(jnp.where(own1, x, y), shift1, 1)
                        if k > 0:
                            p0, p1 = held[v, c]
                            term = (w00 * p0 + w01 * p1) + (w10 * a0 + w11 * a1)
                            out[v, c, s, k - 1] += term
                        held[v, c] = (a0, a1)


def springs_body(affine, *refs):
    apply_springs(*refs, affine)


def last_body(devices, offsets, ext, left, right, w, diag, keep, base, start, force, second, out, part):
    apply_springs(offsets, ext, left, right, w, diag, keep, base, out, (False,))
    _, comps, count, height, q, lanes = out.shape
    sums = [jnp.zeros((8, lanes), jnp.float32) for _ in PAIRS]
    for c in range(comps):
        for s in range(count):
            for r in range(height):
                for h in range(q // 8):
                    at = pl.ds(8 * h, 8)
                    vec = (
                        start[1, c, s, r, at, :], force[0, c, s, r, at, :], force[1, c, s, r, at, :],
                        second[0, c, s, r, at, :], second[1, c, s, r, at, :], out[0, c, s, r, at, :],
                    )
                    sums = [g + vec[i] * vec[j] for g, (i, j) in zip(sums, PAIRS)]
    lane = lax.broadcasted_iota(jnp.int32, (1, lanes), 1)
    packed = jnp.zeros((1, lanes), jnp.float32)
    for n, g in enumerate(sums):
        packed = jnp.where(lane == n, jnp.sum(g), packed)
    part[...] = jnp.broadcast_to(packed[None], part.shape)


def coefficients(gram, norms=None):
    zero = jnp.zeros_like(gram[0, 0])
    one = zero + 1.0
    vel = [one] + [zero] * (NB - 1)
    move = [zero] * NB
    force = [zero, one] + [zero] * (NB - 2)
    bad = zero

    def form(x):
        total, size = zero, zero
        for i, j in PAIRS:
            term = x[i] * x[j] * gram[i, j] * (1.0 if i == j else 2.0)
            total, size = total + term, size + jnp.abs(term)
        return jnp.maximum(total, 0.0), size

    for step in range(ITERS):
        alpha, delta = ALPHAS[step], DELTAS[step]
        if norms is None:
            (ff, fs), (vv, vs) = form(force), form(vel)
            lost = (fs > CANCEL * (ff + TINY)) | (vs > CANCEL * (vv + TINY))
            bad = jnp.where(lost, 1.0, bad)
        else:
            ff, vv = norms(force), norms(vel)
        ratio = jnp.sqrt(vv / (ff + TINY))
        gain = alpha * ratio + delta
        vel = [(1.0 - alpha) * a + gain * f for a, f in zip(vel, force)]
        move = [m + delta * a for m, a in zip(move, vel)]
        force = [zero, one] + move[: NB - 2]
    return vel, move, bad


def solve_body(parts, out):
    lanes = parts.shape[-1]
    total = jnp.sum(parts[...], axis=0)
    lane = lax.broadcasted_iota(jnp.int32, (1, lanes), 1)
    gram = {
        pair: jnp.sum(jnp.where(lane == n, total, 0.0), axis=1, keepdims=True)
        for n, pair in enumerate(PAIRS)
    }
    vel, move, bad = coefficients(gram)
    packed = jnp.zeros((1, lanes), jnp.float32)
    for n, value in enumerate(vel + move + [bad]):
        packed = jnp.where(lane == n, value, packed)
    out[...] = packed


def final_body(coef, start, force, second, third, u_ref, v_ref):
    comps, count, height, width = u_ref.shape
    q = width // 128
    vel = [coef[n] for n in range(NB)]
    move = [coef[NB + n] for n in range(NB)]
    for c in range(comps):
        for s in range(count):
            for j in range(q):
                at = pl.ds(j, height, stride=q)
                cols = pl.ds(128 * j, 128)
                vec = (
                    start.at[1, c, s][at, :], force.at[0, c, s][at, :], force.at[1, c, s][at, :],
                    second.at[0, c, s][at, :], second.at[1, c, s][at, :], third.at[0, c, s][at, :],
                )
                u = start.at[0, c, s][at, :]
                v = vel[0] * vec[0]
                u = u + move[0] * vec[0]
                for n in range(1, NB):
                    v = v + vel[n] * vec[n]
                    u = u + move[n] * vec[n]
                u_ref[c, s, :, cols] = u
                v_ref[c, s, :, cols] = v


def neighbours(low_edge, high_edge, axis):
    count = lax.axis_size(axis)
    pairs = [(i, i + 1) for i in range(count - 1)]
    before = lax.ppermute(high_edge, axis, pairs)
    after = lax.ppermute(low_edge, axis, [(b, a) for a, b in pairs])
    return before, after


def exchange(x):
    height = x.shape[3]
    above, below = neighbours(x[:, :, :, :DOWN], x[:, :, :, height - UP :], TILE)
    ext = jnp.concatenate([above, x, below], axis=3)
    left, right = neighbours(ext, ext, SEC)
    return ext, left, right


def sent_to_all(shard, axis):
    count = lax.axis_size(axis)
    return lax.all_to_all(
        jnp.broadcast_to(shard[None], (count, *shard.shape)), axis, 0, 0, tiled=True
    )


def shards(displacement, velocity, frac, offsets, fixed, trans):
    comps, count, height, width = displacement.shape
    q = width // 128
    devices = lax.axis_size(SEC_TILE)
    place = jnp.stack(
        [
            lax.axis_index(SEC) * count,
            lax.axis_index(TILE) * height,
            jnp.int32(count * lax.axis_size(SEC)),
            jnp.int32(height * lax.axis_size(TILE)),
        ]
    ).astype(jnp.int32)
    shifts = offsets.reshape(-1)

    start = call(
        relayout, f32(2, comps, count, height * q, 128), [VMEM] * 3, "relayout"
    )(displacement, velocity, fixed)
    by_row = start.reshape(2, comps, count, height, q, 128)

    local = jnp.cumsum(trans, 0)
    pieces = sent_to_all(local[-1], SEC).reshape(-1, 2)
    passed = jnp.arange(pieces.shape[0]) < lax.axis_index(SEC)
    anchor = local + jnp.sum(jnp.where(passed[:, None], pieces, 0.0), 0)[None]

    w, diag, keep, base = call(
        weights,
        [
            f32(count, 4, 4, height * q, 128),
            f32(count, height * q, 128),
            f32(count, height * q, 128),
            f32(comps, count, height * q, 128),
        ],
        [SMEM] * 3 + [VMEM] * 2,
        "weights",
    )(place, shifts, anchor.reshape(-1), frac, fixed)

    def springs(x, affine, name):
        return call(
            lambda *refs: springs_body(affine, *refs),
            f32(*x.shape),
            [SMEM] + [VMEM] * 7,
            name,
        )(shifts, *exchange(x), w, diag, keep, base)

    force = springs(by_row, (True, False), "force")
    second = springs(force, (False, False), "second")
    third, part = call(
        lambda *refs: last_body(devices, *refs),
        [f32(1, *by_row.shape[1:]), f32(devices, 1, 128)],
        [SMEM] + [VMEM] * 10,
        "third",
    )(shifts, *exchange(second[:1]), w, diag, keep, base, by_row, force, second)

    parts = lax.all_to_all(part, SEC_TILE, 0, 0, tiled=True)
    coef = call(solve_body, f32(1, 128), [VMEM], "solve")(parts)[0]

    def measured(coef):
        basis = (by_row[1], force[0], force[1], second[0], second[1], third[0])

        def norms(x):
            vec = sum(a * b for a, b in zip(x, basis))
            return lax.psum(jnp.sum(vec * vec), SEC_TILE)

        vel, move, _ = coefficients({(0, 0): coef[0] * 0.0}, norms)
        return jnp.concatenate([jnp.stack(vel + move), coef[2 * NB :]])

    coef = lax.cond(coef[2 * NB] > 0.5, measured, lambda coef: coef, coef)

    flat = lambda x: x.reshape(*x.shape[:3], height * q, 128)
    return call(
        final_body,
        [f32(*displacement.shape)] * 2,
        [SMEM] + [VMEM] * 4,
        "final",
    )(coef, start, flat(force), flat(second), flat(third))


def solution(mesh):
    torus = Mesh(
        mesh.devices.reshape(2, 4, 2, 2, 8), ("sec_0", "sec_1", "sec_2", "tile_0", "tile_1")
    )
    in_specs = (
        P(None, SEC, TILE, None),
        P(None, SEC, TILE, None),
        P(None, None, SEC, TILE, None),
        P(None, SEC, TILE, None),
        P(SEC, TILE, None),
        P(SEC, None),
    )
    out_specs = (P(None, SEC, TILE, None), P(None, SEC, TILE, None))
    return jax.shard_map(
        shards, mesh=torus, in_specs=in_specs, out_specs=out_specs, check_vma=False
    )
```

time: 460 us -> 132 us (0.29); the launches traced: 455 us -> 132 us
  local copies, waits for them, and re-layouts: 212 us -> 4.45 us
  blocking collectives: 129 us -> 43.7 us
  other arithmetic: 34.5 us -> 0.41 us
  Pallas kernels: 0 us -> 10.6 us
    another operation x189 -> x0, local copies, waits for them, and re-layouts: 164 us -> none  [the longest x113 92.1 us: pull(): first = jnp.roll(part_rows, -shift[1], axis=2)]
    psum x15 -> x0, blocking collectives: 129 us -> none  [by_axis(): shard = lax.psum(shard, axis)]
    all_to_all x0 -> x1, blocking collectives: none -> 43.7 us  [shards(): parts = lax.all_to_all(part, SEC_TILE, 0, 0, tiled=True)]
    gather x52 -> x0, local copies, waits for them, and re-layouts: 23.4 us -> none
    reduce_sum x6 -> x1, other arithmetic: 17.8 us -> 0.12 us  [shards(): anchor = local + jnp.sum(jnp.where(passed[:, None], pieces, 0.0), 0)[None]]
    pallas_call x0 -> x7, Pallas kernels: none -> 10.6 us  [the longest x2 4.29 us: springs(): call(lambda *refs: springs_body(affine, *refs), f32(*x.shape), [SMEM] + [...]
    transpose x8 -> x0, local copies, waits for them, and re-layouts: 9.1 us -> none  [pull(): part_rows = lax.dynamic_slice_in_dim(block, 3 + shift[0], height + 1, 1)]
    ppermute x12, waiting for transfers between devices: 28.5 us -> 20.5 us  [the longest x6 12.8 us: neighbours(): after = lax.ppermute(low_edge, axis, [(b, a) for a, b in pairs])]
  transfers between devices with their start and end apart: 13 -> 13, of which waited for: 8 -> 9; matrix products, arithmetic and copies ran while one was open for 5% -> 1% of each run, Pallas kernels for 0% -> 1%
where the time goes in v1:
time: 132 us
  blocking collectives  43.7 us (33%)
  starting transfers between devices  42.8 us (32%)
  waiting for transfers between devices  28 us (21%)
  Pallas kernels  10.6 us (8%)
  local copies, waits for them, and re-layouts  4.45 us (3%)
  between operations  1.58 us (1%)
    all_to_all x1, blocking collectives, shards(): parts = lax.all_to_all(part, SEC_TILE, 0, 0, tiled=True)  43.7 us
    ppermute x6, starting transfers between devices, neighbours(): before = lax.ppermute(high_edge, axis, pairs)  23 us
    ppermute x6, starting transfers between devices, neighbours(): after = lax.ppermute(low_edge, axis, [(b, a) for a, b in pairs])  14.5 us
    ppermute x6, waiting for transfers between devices, neighbours(): after = lax.ppermute(low_edge, axis, [(b, a) for a, b in pairs])  12.8 us
    ppermute x6, waiting for transfers between devices, neighbours(): before = lax.ppermute(high_edge, axis, pairs)  7.68 us
    all_to_all x1, waiting for transfers between devices, sent_to_all(): lax.all_to_all(jnp.broadcast_to(shard[None], (count, *shard.shape)), axis...  7.51 us
    all_to_all x1, starting transfers between devices, sent_to_all(): lax.all_to_all(jnp.broadcast_to(shard[None], (count, *shard.shape)), axis...  5.29 us
    pallas_call x2, Pallas kernels, springs(): call(lambda *refs: springs_body(affine, *refs), f32(*x.shape), [SMEM] + [...  4.29 us
  transfers between devices with their start and end apart: 13, of which 9 were waited for; matrix products, arithmetic and copies ran while one was open for 1% of the time, Pallas kernels for 1%

profile of v1, /device:TPU:1, one launch (start us, length us, event | category | flops | bytes accessed | tf_op | source)
XLA Modules:
  0.0 131.6 jit_solution(11390607947713833678)
XLA Ops:
  0.6 0.9 copy-done.1
  1.5 0.9 copy-done.3
  2.5 0.9 copy-done.4
  3.6 1.4 %collective-permute-start.1 = (f32[2,2,2,3,16,128]{5,4,3,2,1,0:T(8,128)S(1)}, f32[2,2,2,3,16,128]{5,4,3,2,1,0:T(8,128)S(1)}, u32[]{:S(2)}, u32[]{:S(2)}) collective-permute-start(f32[2,2,2,3,16,128]{5,4,3,2,1,0:T(8,128)S(1)} %slice.61), channel_id=1, source_target_pairs={{1,0},{2,1},{3,2},{4,3},{5,4},{6,5},{7,6},{8,7},{9,8},{10,9},{11,1... | collective-permute-start | bytes 589832 | tf_op jit(solution)/shard_map/ppermute | solution.py:270
  5.1 5.0 %collective-permute-start = (f32[2,2,2,2,16,128]{5,4,3,2,1,0:T(8,128)S(1)}, f32[2,2,2,2,16,128]{5,4,3,2,1,0:T(8,128)S(1)}, u32[]{:S(2)}, u32[]{:S(2)}) collective-permute-start(f32[2,2,2,2,16,128]{5,4,3,2,1,0:T(8,128)S(1)} %slice.60), channel_id=1, source_target_pairs={{0,1},{1,2},{2,3},{3,4},{4,5},{5,6},{6,7},{7,8},{8,9},{9,10},{10,1... | collective-permute-start | bytes 393224 | tf_op jit(solution)/shard_map/ppermute | solution.py:269
  10.1 1.9 %collective-permute-done = f32[2,2,2,2,16,128]{5,4,3,2,1,0:T(8,128)S(1)} collective-permute-done((f32[2,2,2,2,16,128]{5,4,3,2,1,0:T(8,128)S(1)}, f32[2,2,2,2,16,128]{5,4,3,2,1,0:T(8,128)S(1)}, u32[]{:S(2)}, u32[]{:S(2)}) %collective-permute-start) | collective-permute-done | bytes 131104 | tf_op jit(solution)/shard_map/ppermute | solution.py:269
  12.1 5.2 %collective-permute-start.3 = (f32[2,2,2,13,16,128]{5,4,3,2,1,0:T(8,128)S(1)}, f32[2,2,2,13,16,128]{5,4,3,2,1,0:T(8,128)S(1)}, u32[]{:S(2)}, u32[]{:S(2)}) collective-permute-start(f32[2,2,2,13,16,128]{5,4,3,2,1,0:T(8,128)S(1)} %pad_maximum_fusion.refs_1_), channel_id=1, source_target_pairs={{16,0},{32,16},{48,32},{64,48},{80,64},{96,80},{112,96},{128,112},... | collective-permute-start | bytes 2555912 | tf_op jit(solution)/shard_map/ppermute | solution.py:270
  17.4 1.9 %collective-permute-start.2 = (f32[2,2,2,13,16,128]{5,4,3,2,1,0:T(8,128)S(1)}, f32[2,2,2,13,16,128]{5,4,3,2,1,0:T(8,128)S(1)}, u32[]{:S(2)}, u32[]{:S(2)}) collective-permute-start(f32[2,2,2,13,16,128]{5,4,3,2,1,0:T(8,128)S(1)} %pad_maximum_fusion.refs_1_), channel_id=1, source_target_pairs={{0,16},{16,32},{32,48},{48,64},{64,80},{80,96},{96,112},{112,128},... | collective-permute-start | bytes 2555912 | tf_op jit(solution)/shard_map/ppermute | solution.py:269
  19.3 0.6 broadcast_in_dim.20
  20.0 5.3 %all-to-all-start = ((f32[16,1,2]{2,1,0:T(1,128)}), f32[16,1,2]{2,1,0:T(1,128)S(1)}, u32[]{:S(2)}, u32[]{:S(2)}) async-start(f32[16,1,2]{2,1,0:T(1,128)} %broadcast_in_dim.20), calls=%async_computation | async-start | bytes 16384 | tf_op jit(solution)/shard_map/all_to_all | solution.py:284
  25.5 7.5 %all-to-all-done = f32[16,1,2]{2,1,0:T(1,128)S(1)} async-done(((f32[16,1,2]{2,1,0:T(1,128)}), f32[16,1,2]{2,1,0:T(1,128)S(1)}, u32[]{:S(2)}, u32[]{:S(2)}) %all-to-all-start) | async-done | bytes 160 | tf_op jit(solution)/shard_map/all_to_all | solution.py:284
  33.3 1.9 %weights.1 = (f32[2,4,4,128,128]{4,3,2,1,0:T(8,128)S(1)}, f32[2,128,128]{2,1,0:T(8,128)S(1)}, f32[2,128,128]{2,1,0:T(8,128)S(1)}, f32[2,2,128,128]{3,2,1,0:T(8,128)S(1)}) custom-call(s32[4]{0:T(128)S(1)} %pad_add_fusion.place_ref, s32[16]{0:T(128)S(1)} %reshape.76.offsets_ref.refs_0_, f32[4]{0:T(128)S(1)} %add.212.anchor_ref, ...), custom_call_target="tpu_custom_call" | custom-call | flops 4000000 | bytes 4000000 | tf_op jit(solution)/shard_map/weights/pallas_call | solution.py:313
  35.3 2.1 %force.1.refs_9_ = f32[2,2,2,8,16,128]{5,4,3,2,1,0:T(8,128)S(1)} custom-call(s32[16]{0:T(128)S(1)} %reshape.76.offsets_ref.refs_0_, f32[2,2,2,13,16,128]{5,4,3,2,1,0:T(8,128)S(1)} %pad_maximum_fusion.refs_1_, f32[2,2,2,13,16,128]{5,4,3,2,1,0:T(8,128)S(1)} %collective-permute-done.2.refs_2_, f32[2,2,2,13,16,128]{5,4,3,2,1,0:T(8,128)S(1)} %collective-permute-done.3.refs_3_, ...), custom_call_target="tpu_custom_call" | custom-call | flops 4000000 | bytes 4000000 | tf_op jit(solution)/shard_map/force/pallas_call | solution.py:326
  37.4 1.3 collective-permute-start.5
  38.8 4.3 %collective-permute-start.4 = (f32[2,2,2,2,16,128]{5,4,3,2,1,0:T(8,128)S(1)}, f32[2,2,2,2,16,128]{5,4,3,2,1,0:T(8,128)S(1)}, u32[]{:S(2)}, u32[]{:S(2)}) collective-permute-start(f32[2,2,2,2,16,128]{5,4,3,2,1,0:T(8,128)S(1)} %slice.62), channel_id=1, source_target_pairs={{0,1},{1,2},{2,3},{3,4},{4,5},{5,6},{6,7},{7,8},{8,9},{9,10},{10,1... | collective-permute-start | bytes 393224 | tf_op jit(solution)/shard_map/ppermute | solution.py:269
  43.0 2.1 %collective-permute-done.4 = f32[2,2,2,2,16,128]{5,4,3,2,1,0:T(8,128)S(1)} collective-permute-done((f32[2,2,2,2,16,128]{5,4,3,2,1,0:T(8,128)S(1)}, f32[2,2,2,2,16,128]{5,4,3,2,1,0:T(8,128)S(1)}, u32[]{:S(2)}, u32[]{:S(2)}) %collective-permute-start.4) | collective-permute-done | bytes 131104 | tf_op jit(solution)/shard_map/ppermute | solution.py:269
  45.7 3.3 %collective-permute-start.7 = (f32[2,2,2,13,16,128]{5,4,3,2,1,0:T(8,128)S(1)}, f32[2,2,2,13,16,128]{5,4,3,2,1,0:T(8,128)S(1)}, u32[]{:S(2)}, u32[]{:S(2)}) collective-permute-start(f32[2,2,2,13,16,128]{5,4,3,2,1,0:T(8,128)S(1)} %pad_maximum_fusion.1.refs_1_), channel_id=1, source_target_pairs={{16,0},{32,16},{48,32},{64,48},{80,64},{96,80},{112,96},{128,112},... | collective-permute-start | bytes 2555912 | tf_op jit(solution)/shard_map/ppermute | solution.py:270
  49.0 2.4 %collective-permute-start.6 = (f32[2,2,2,13,16,128]{5,4,3,2,1,0:T(8,128)S(1)}, f32[2,2,2,13,16,128]{5,4,3,2,1,0:T(8,128)S(1)}, u32[]{:S(2)}, u32[]{:S(2)}) collective-permute-start(f32[2,2,2,13,16,128]{5,4,3,2,1,0:T(8,128)S(1)} %pad_maximum_fusion.1.refs_1_), channel_id=1, source_target_pairs={{0,16},{16,32},{32,48},{48,64},{64,80},{80,96},{96,112},{112,128},... | collective-permute-start | bytes 2555912 | tf_op jit(solution)/shard_map/ppermute | solution.py:269
  51.4 8.4 %collective-permute-done.7.refs_3_ = f32[2,2,2,13,16,128]{5,4,3,2,1,0:T(8,128)S(1)} collective-permute-done((f32[2,2,2,13,16,128]{5,4,3,2,1,0:T(8,128)S(1)}, f32[2,2,2,13,16,128]{5,4,3,2,1,0:T(8,128)S(1)}, u32[]{:S(2)}, u32[]{:S(2)}) %collective-permute-start.7) | collective-permute-done | bytes 852000 | tf_op jit(solution)/shard_map/ppermute | solution.py:270
  59.8 1.2 collective-permute-done.6.refs_2_
  61.0 2.1 %second.1.refs_10_ = f32[2,2,2,8,16,128]{5,4,3,2,1,0:T(8,128)S(1)} custom-call(s32[16]{0:T(128)S(1)} %reshape.76.offsets_ref.refs_0_, f32[2,2,2,13,16,128]{5,4,3,2,1,0:T(8,128)S(1)} %pad_maximum_fusion.1.refs_1_, f32[2,2,2,13,16,128]{5,4,3,2,1,0:T(8,128)S(1)} %collective-permute-done.6.refs_2_, ...), custom_call_target="tpu_custom_call" | custom-call | flops 4000000 | bytes 4000000 | tf_op jit(solution)/shard_map/second/pallas_call | solution.py:326
  63.2 1.3 collective-permute-start.9
  64.5 4.2 %collective-permute-start.8 = (f32[1,2,2,2,16,128]{5,4,3,2,1,0:T(8,128)S(1)}, f32[1,2,2,2,16,128]{5,4,3,2,1,0:T(8,128)S(1)}, u32[]{:S(2)}, u32[]{:S(2)}) collective-permute-start(f32[1,2,2,2,16,128]{5,4,3,2,1,0:T(8,128)S(1)} %slice.64), channel_id=1, source_target_pairs={{0,1},{1,2},{2,3},{3,4},{4,5},{5,6},{6,7},{7,8},{8,9},{9,10},{10,1... | collective-permute-start | bytes 196616 | tf_op jit(solution)/shard_map/ppermute | solution.py:269
  68.8 1.3 collective-permute-done.8
  70.1 1.9 %collective-permute-start.11 = (f32[1,2,2,13,16,128]{5,4,3,2,1,0:T(8,128)S(1)}, f32[1,2,2,13,16,128]{5,4,3,2,1,0:T(8,128)S(1)}, u32[]{:S(2)}, u32[]{:S(2)}) collective-permute-start(f32[1,2,2,13,16,128]{5,4,3,2,1,0:T(8,128)S(1)} %pad_maximum_fusion.2.refs_1_), channel_id=1, source_target_pairs={{16,0},{32,16},{48,32},{64,48},{80,64},{96,80},{112,96},{128,112},... | collective-permute-start | bytes 1277960 | tf_op jit(solution)/shard_map/ppermute | solution.py:270
  72.0 5.3 %collective-permute-start.10 = (f32[1,2,2,13,16,128]{5,4,3,2,1,0:T(8,128)S(1)}, f32[1,2,2,13,16,128]{5,4,3,2,1,0:T(8,128)S(1)}, u32[]{:S(2)}, u32[]{:S(2)}) collective-permute-start(f32[1,2,2,13,16,128]{5,4,3,2,1,0:T(8,128)S(1)} %pad_maximum_fusion.2.refs_1_), channel_id=1, source_target_pairs={{0,16},{16,32},{32,48},{48,64},{64,80},{80,96},{96,112},{112,128},... | collective-permute-start | bytes 1277960 | tf_op jit(solution)/shard_map/ppermute | solution.py:269
  77.3 3.9 %collective-permute-done.11.refs_3_ = f32[1,2,2,13,16,128]{5,4,3,2,1,0:T(8,128)S(1)} collective-permute-done((f32[1,2,2,13,16,128]{5,4,3,2,1,0:T(8,128)S(1)}, f32[1,2,2,13,16,128]{5,4,3,2,1,0:T(8,128)S(1)}, u32[]{:S(2)}, u32[]{:S(2)}) %collective-permute-start.11) | collective-permute-done | bytes 426016 | tf_op jit(solution)/shard_map/ppermute | solution.py:270
  81.2 1.2 collective-permute-done.10.refs_2_
  82.4 1.9 %third.1 = (f32[1,2,2,8,16,128]{5,4,3,2,1,0:T(8,128)S(1)}, f32[256,1,128]{2,1,0:T(1,128)S(1)}) custom-call(s32[16]{0:T(128)S(1)} %reshape.76.offsets_ref.refs_0_, f32[1,2,2,13,16,128]{5,4,3,2,1,0:T(8,128)S(1)} %pad_maximum_fusion.2.refs_1_, f32[1,2,2,13,16,128]{5,4,3,2,1,0:T(8,128)S(1)} %collective-permute-done.10.refs_2_, ...), custom_call_target="tpu_custom_call" | custom-call | flops 4000000 | bytes 4000000 | tf_op jit(solution)/shard_map/third/pallas_call | solution.py:335
  84.3 43.7 %all_to_all.14.parts = f32[256,1,128]{2,1,0:T(1,128)S(1)} all-to-all(f32[256,1,128]{2,1,0:T(1,128)S(1)} %get-tuple-element.31), channel_id=1, replica_groups=mesh['sec_0'=2,'sec_1'=4,'sec_2'=2,'tile_0'=2,'tile_1'=8] {'sec_0','sec_..., dimensions={0} | all-to-all | bytes 262144 | tf_op jit(solution)/shard_map/all_to_all | solution.py:342
  128.5 0.6 slice.59
  129.7 1.8 %final.1 = (f32[2,2,8,2048]{3,2,1,0:T(8,128)}, f32[2,2,8,2048]{3,2,1,0:T(8,128)}) custom-call(f32[128]{0:T(128)S(1)} %get-tuple-element.43.coef, f32[2,2,2,128,128]{4,3,2,1,0:T(8,128)S(1)} %copy-done.6, f32[2,2,2,128,128]{4,3,2,1,0:T(8,128)S(1)} %bitcast.170, f32[2,2,2,128,128]{4,3,2,1,0:T(8,128)S(1)} %bitcast.171, f32[1,2,2,128,128]{4,3,2,1,0:T(8,128)S(1)} %bitcast.177), custom_call_target="tpu_custom_call" | custom-call | flops 4000000 | bytes 4000000 | tf_op jit(solution)/shard_map/final/pallas_call | solution.py:358
  (43 shorter events, 2.0 us)
Async XLA Ops:
  0.6 0.9 copy-start.1
  1.5 0.9 copy-start.3
  2.5 0.9 copy-start.4
  3.4 15.9 %copy-start.8 = (f32[2,2]{1,0:T(2,128)S(1)}, f32[2,2]{1,0:T(2,128)}, u32[]{:S(2)}) copy-start(f32[2,2]{1,0:T(2,128)} %param.13) | copy-start | bytes 52
  3.4 21.9 %copy-start.7 = (s32[4,2,1,2]{0,3,2,1:T(2,128)S(1)}, s32[4,2,1,2]{0,3,2,1:T(2,128)}, u32[]{:S(2)}) copy-start(s32[4,2,1,2]{0,3,2,1:T(2,128)} %param.11) | copy-start | bytes 196
  3.4 29.9 %copy-start = (bf16[2,4,2,8,2048]{4,3,2,1,0:T(8,128)(2,1)S(1)}, bf16[2,4,2,8,2048]{4,3,2,1,0:T(8,128)(2,1)}, u32[]{:S(2)}) copy-start(bf16[2,4,2,8,2048]{4,3,2,1,0:T(8,128)(2,1)} %frac_ref.1) | copy-start | bytes 1572868
  3.4 29.9 %copy-start.2 = (s32[2,8,2048]{2,1,0:T(8,128)S(1)}, s32[2,8,2048]{2,1,0:T(8,128)}, u32[]{:S(2)}) copy-start(s32[2,8,2048]{2,1,0:T(8,128)} %fixed_ref.3) | copy-start | bytes 393220
  3.6 8.4 %copy-start.5 = (f32[2,2,2,128,128]{4,3,2,1,0:T(8,128)}, f32[2,2,2,128,128]{4,3,2,1,0:T(8,128)S(1)}, u32[]{:S(2)}) copy-start(f32[2,2,2,128,128]{4,3,2,1,0:T(8,128)S(1)} %relayout.1.start) | copy-start | bytes 1572868
  3.6 8.4 %collective-permute-start.1 = (f32[2,2,2,3,16,128]{5,4,3,2,1,0:T(8,128)S(1)}, f32[2,2,2,3,16,128]{5,4,3,2,1,0:T(8,128)S(1)}, u32[]{:S(2)}, u32[]{:S(2)}) collective-permute-start(f32[2,2,2,3,16,128]{5,4,3,2,1,0:T(8,128)S(1)} %slice.61), channel_id=1, source_target_pairs={{1,0},{2,1},{3,2},{4,3},{5,4},{6,5},{7,6},{8,7},{9,8},{10,9},{11,1... | collective-permute-start | bytes 589832 | tf_op jit(solution)/shard_map/ppermute | solution.py:270
  5.1 6.9 %collective-permute-start = (f32[2,2,2,2,16,128]{5,4,3,2,1,0:T(8,128)S(1)}, f32[2,2,2,2,16,128]{5,4,3,2,1,0:T(8,128)S(1)}, u32[]{:S(2)}, u32[]{:S(2)}) collective-permute-start(f32[2,2,2,2,16,128]{5,4,3,2,1,0:T(8,128)S(1)} %slice.60), channel_id=1, source_target_pairs={{0,1},{1,2},{2,3},{3,4},{4,5},{5,6},{6,7},{7,8},{8,9},{9,10},{10,1... | collective-permute-start | bytes 393224 | tf_op jit(solution)/shard_map/ppermute | solution.py:269
  12.1 23.1 %collective-permute-start.3 = (f32[2,2,2,13,16,128]{5,4,3,2,1,0:T(8,128)S(1)}, f32[2,2,2,13,16,128]{5,4,3,2,1,0:T(8,128)S(1)}, u32[]{:S(2)}, u32[]{:S(2)}) collective-permute-start(f32[2,2,2,13,16,128]{5,4,3,2,1,0:T(8,128)S(1)} %pad_maximum_fusion.refs_1_), channel_id=1, source_target_pairs={{16,0},{32,16},{48,32},{64,48},{80,64},{96,80},{112,96},{128,112},... | collective-permute-start | bytes 2555912 | tf_op jit(solution)/shard_map/ppermute | solution.py:270
  17.4 17.9 %collective-permute-start.2 = (f32[2,2,2,13,16,128]{5,4,3,2,1,0:T(8,128)S(1)}, f32[2,2,2,13,16,128]{5,4,3,2,1,0:T(8,128)S(1)}, u32[]{:S(2)}, u32[]{:S(2)}) collective-permute-start(f32[2,2,2,13,16,128]{5,4,3,2,1,0:T(8,128)S(1)} %pad_maximum_fusion.refs_1_), channel_id=1, source_target_pairs={{0,16},{16,32},{32,48},{48,64},{64,80},{80,96},{96,112},{112,128},... | collective-permute-start | bytes 2555912 | tf_op jit(solution)/shard_map/ppermute | solution.py:269
  20.0 13.1 %all-to-all-start = ((f32[16,1,2]{2,1,0:T(1,128)}), f32[16,1,2]{2,1,0:T(1,128)S(1)}, u32[]{:S(2)}, u32[]{:S(2)}) async-start(f32[16,1,2]{2,1,0:T(1,128)} %broadcast_in_dim.20), calls=%async_computation | async-start | bytes 16384 | tf_op jit(solution)/shard_map/all_to_all | solution.py:284
  37.4 8.2 %collective-permute-start.5 = (f32[2,2,2,3,16,128]{5,4,3,2,1,0:T(8,128)S(1)}, f32[2,2,2,3,16,128]{5,4,3,2,1,0:T(8,128)S(1)}, u32[]{:S(2)}, u32[]{:S(2)}) collective-permute-start(f32[2,2,2,3,16,128]{5,4,3,2,1,0:T(8,128)S(1)} %slice.63), channel_id=1, source_target_pairs={{1,0},{2,1},{3,2},{4,3},{5,4},{6,5},{7,6},{8,7},{9,8},{10,9},{11,1... | collective-permute-start | bytes 589832 | tf_op jit(solution)/shard_map/ppermute | solution.py:270
  38.8 6.4 %collective-permute-start.4 = (f32[2,2,2,2,16,128]{5,4,3,2,1,0:T(8,128)S(1)}, f32[2,2,2,2,16,128]{5,4,3,2,1,0:T(8,128)S(1)}, u32[]{:S(2)}, u32[]{:S(2)}) collective-permute-start(f32[2,2,2,2,16,128]{5,4,3,2,1,0:T(8,128)S(1)} %slice.62), channel_id=1, source_target_pairs={{0,1},{1,2},{2,3},{3,4},{4,5},{5,6},{6,7},{7,8},{8,9},{9,10},{10,1... | collective-permute-start | bytes 393224 | tf_op jit(solution)/shard_map/ppermute | solution.py:269
  45.7 36.7 %copy-start.6 = (f32[2,2,2,128,128]{4,3,2,1,0:T(8,128)S(1)}, f32[2,2,2,128,128]{4,3,2,1,0:T(8,128)}, u32[]{:S(2)}) copy-start(f32[2,2,2,128,128]{4,3,2,1,0:T(8,128)} %copy-done.5) | copy-start | bytes 1572868
  45.7 14.1 %collective-permute-start.7 = (f32[2,2,2,13,16,128]{5,4,3,2,1,0:T(8,128)S(1)}, f32[2,2,2,13,16,128]{5,4,3,2,1,0:T(8,128)S(1)}, u32[]{:S(2)}, u32[]{:S(2)}) collective-permute-start(f32[2,2,2,13,16,128]{5,4,3,2,1,0:T(8,128)S(1)} %pad_maximum_fusion.1.refs_1_), channel_id=1, source_target_pairs={{16,0},{32,16},{48,32},{64,48},{80,64},{96,80},{112,96},{128,112},... | collective-permute-start | bytes 2555912 | tf_op jit(solution)/shard_map/ppermute | solution.py:270
  49.0 12.0 %collective-permute-start.6 = (f32[2,2,2,13,16,128]{5,4,3,2,1,0:T(8,128)S(1)}, f32[2,2,2,13,16,128]{5,4,3,2,1,0:T(8,128)S(1)}, u32[]{:S(2)}, u32[]{:S(2)}) collective-permute-start(f32[2,2,2,13,16,128]{5,4,3,2,1,0:T(8,128)S(1)} %pad_maximum_fusion.1.refs_1_), channel_id=1, source_target_pairs={{0,16},{16,32},{32,48},{48,64},{64,80},{80,96},{96,112},{112,128},... | collective-permute-start | bytes 2555912 | tf_op jit(solution)/shard_map/ppermute | solution.py:269
  63.2 6.9 %collective-permute-start.9 = (f32[1,2,2,3,16,128]{5,4,3,2,1,0:T(8,128)S(1)}, f32[1,2,2,3,16,128]{5,4,3,2,1,0:T(8,128)S(1)}, u32[]{:S(2)}, u32[]{:S(2)}) collective-permute-start(f32[1,2,2,3,16,128]{5,4,3,2,1,0:T(8,128)S(1)} %slice.66), channel_id=1, source_target_pairs={{1,0},{2,1},{3,2},{4,3},{5,4},{6,5},{7,6},{8,7},{9,8},{10,9},{11,1... | collective-permute-start | bytes 294920 | tf_op jit(solution)/shard_map/ppermute | solution.py:270
  64.5 5.6 %collective-permute-start.8 = (f32[1,2,2,2,16,128]{5,4,3,2,1,0:T(8,128)S(1)}, f32[1,2,2,2,16,128]{5,4,3,2,1,0:T(8,128)S(1)}, u32[]{:S(2)}, u32[]{:S(2)}) collective-permute-start(f32[1,2,2,2,16,128]{5,4,3,2,1,0:T(8,128)S(1)} %slice.64), channel_id=1, source_target_pairs={{0,1},{1,2},{2,3},{3,4},{4,5},{5,6},{6,7},{7,8},{8,9},{9,10},{10,1... | collective-permute-start | bytes 196616 | tf_op jit(solution)/shard_map/ppermute | solution.py:269
  70.1 11.1 %collective-permute-start.11 = (f32[1,2,2,13,16,128]{5,4,3,2,1,0:T(8,128)S(1)}, f32[1,2,2,13,16,128]{5,4,3,2,1,0:T(8,128)S(1)}, u32[]{:S(2)}, u32[]{:S(2)}) collective-permute-start(f32[1,2,2,13,16,128]{5,4,3,2,1,0:T(8,128)S(1)} %pad_maximum_fusion.2.refs_1_), channel_id=1, source_target_pairs={{16,0},{32,16},{48,32},{64,48},{80,64},{96,80},{112,96},{128,112},... | collective-permute-start | bytes 1277960 | tf_op jit(solution)/shard_map/ppermute | solution.py:270
  72.0 10.3 %collective-permute-start.10 = (f32[1,2,2,13,16,128]{5,4,3,2,1,0:T(8,128)S(1)}, f32[1,2,2,13,16,128]{5,4,3,2,1,0:T(8,128)S(1)}, u32[]{:S(2)}, u32[]{:S(2)}) collective-permute-start(f32[1,2,2,13,16,128]{5,4,3,2,1,0:T(8,128)S(1)} %pad_maximum_fusion.2.refs_1_), channel_id=1, source_target_pairs={{0,16},{16,32},{32,48},{48,64},{64,80},{80,96},{96,112},{112,128},... | collective-permute-start | bytes 1277960 | tf_op jit(solution)/shard_map/ppermute | solution.py:269

commit v2 on v1

--- a/solution.py
+++ b/solution.py
@@ -5,6 +5,7 @@
 from jax.experimental.pallas import tpu as pltpu
 from jax.sharding import Mesh
 from jax.sharding import PartitionSpec as P
+
 
 ITERS = 3
 SEC = ("sec_0", "sec_1", "sec_2")
@@ -25,13 +26,14 @@
 
 VMEM = pl.BlockSpec(memory_space=pltpu.VMEM)
 SMEM = pl.BlockSpec(memory_space=pltpu.SMEM)
+HBM = pl.BlockSpec(memory_space=pltpu.HBM)
 
 
 def params():
     return pltpu.CompilerParams(vmem_limit_bytes=48 << 20)
 
 
-def call(body, out_shape, in_specs, name, flops=4_000_000, bytes_accessed=4_000_000, scratch=()):
+def call(body, out_shape, in_specs, flops=4_000_000, bytes_accessed=4_000_000, scratch=()):
     multi = isinstance(out_shape, (list, tuple))
     return pl.pallas_call(
         body,
@@ -41,7 +43,6 @@
         scratch_shapes=list(scratch),
         compiler_params=params(),
         cost_estimate=pl.CostEstimate(flops=flops, bytes_accessed=bytes_accessed, transcendentals=0),
-        name=name,
     )
 
 
@@ -49,7 +50,17 @@
     return jax.ShapeDtypeStruct(shape, jnp.float32)
 
 
-def relayout(u_ref, vel_ref, fixed_ref, out_ref):
+def relayout(u_hbm, vel_hbm, fixed_hbm, out_ref, u_ref, vel_ref, fixed_ref, sems):
+    copies = [
+        pltpu.make_async_copy(a, b, sems.at[n])
+        for n, (a, b) in enumerate(
+            ((u_hbm, u_ref), (vel_hbm, vel_ref), (fixed_hbm, fixed_ref))
+        )
+    ]
+    for copy in copies:
+        copy.start()
+    for copy in copies:
+        copy.wait()
     comps, count, height, width = u_ref.shape
     q = width // 128
     for s in range(count):
@@ -112,7 +123,7 @@
                 base_ref.at[c, s][at, :] = base[c]
 
 
-def apply_springs(offsets_ref, ext, left, right, w, diag, keep, base, out, affine):
+def stay(ext, diag, keep, base, out, affine):
     vecs, comps, count, tall, q, lanes = ext.shape
     height = tall - UP - DOWN
     lane = lax.broadcasted_iota(jnp.int32, (q, lanes), 1)
@@ -135,62 +146,94 @@
                     if affine[v]:
                         y = y + base[c, s, at, :]
                     out[v, c, s, r] = y
-        for i in range(4):
-            slot = s + 2 + reaches[i]
-            source = (left, ext, right)[slot // count]
-            index = slot % count
-            dr, dc = offsets_ref[i * count * 2 + s * 2], offsets_ref[i * count * 2 + s * 2 + 1]
-            ahead = dc >= 0
-            turn = jnp.where(ahead, q - 1, 1)
-            shift0 = lax.rem(lanes - dc, lanes)
-            shift1 = lax.rem(lanes - dc - 1, lanes)
-            low0 = jnp.where(ahead, dc, 0)
-            high0 = jnp.where(ahead, lanes, lanes + dc)
-            low1 = jnp.where(ahead, dc + 1, 0)
-            high1 = jnp.where(ahead, lanes, lanes + dc + 1)
-            own0 = (lane >= low0) & (lane < high0)
-            own1 = (lane >= low1) & (lane < high1)
-            held = {}
-            for k in range(height + 1):
+
+
+def pull(offsets_ref, source, index, s, i, w, out):
+    vecs, comps, count, tall, q, lanes = source.shape
+    height = tall - UP - DOWN
+    lane = lax.broadcasted_iota(jnp.int32, (q, lanes), 1)
+    spot = i * (count * 2) + s * 2
+    dr, dc = offsets_ref[spot], offsets_ref[spot + 1]
+    ahead = dc >= 0
+    turn = jnp.where(ahead, q - 1, 1)
+    shift0 = lax.rem(lanes - dc, lanes)
+    shift1 = lax.rem(lanes - dc - 1, lanes)
+    low0 = jnp.where(ahead, dc, 0)
+    high0 = jnp.where(ahead, lanes, lanes + dc)
+    low1 = jnp.where(ahead, dc + 1, 0)
+    high1 = jnp.where(ahead, lanes, lanes + dc + 1)
+    own0 = (lane >= low0) & (lane < high0)
+    own1 = (lane >= low1) & (lane < high1)
+    held = {}
+    for k in range(height + 1):
+        if k > 0:
+            at = pl.ds((k - 1) * q, q)
+            w00, w01, w10, w11 = (w[s, i, n, at, :] for n in range(4))
+        for v in range(vecs):
+            for c in range(comps):
+                x = source[v, c, index, k + UP + dr]
+                y = pltpu.roll(x, turn, 0)
+                a0 = pltpu.roll(jnp.where(own0, x, y), shift0, 1)
+                a1 = pltpu.roll(jnp.where(own1, x, y), shift1, 1)
                 if k > 0:
-                    at = pl.ds((k - 1) * q, q)
-                    w00, w01, w10, w11 = (w[s, i, n, at, :] for n in range(4))
-                for v in range(vecs):
-                    for c in range(comps):
-                        x = source[v, c, index, k + UP + dr]
-                        y = pltpu.roll(x, turn, 0)
-                        a0 = pltpu.roll(jnp.where(own0, x, y), shift0, 1)
-                        a1 = pltpu.roll(jnp.where(own1, x, y), shift1, 1)
-                        if k > 0:
-                            p0, p1 = held[v, c]
-                            term = (w00 * p0 + w01 * p1) + (w10 * a0 + w11 * a1)
-                            out[v, c, s, k - 1] += term
-                        held[v, c] = (a0, a1)
-
-
-def springs_body(affine, *refs):
-    apply_springs(*refs, affine)
-
-
-def last_body(devices, offsets, ext, left, right, w, diag, keep, base, start, force, second, out, part):
-    apply_springs(offsets, ext, left, right, w, diag, keep, base, out, (False,))
-    _, comps, count, height, q, lanes = out.shape
-    sums = [jnp.zeros((8, lanes), jnp.float32) for _ in PAIRS]
+                    p0, p1 = held[v, c]
+                    term = (w00 * p0 + w01 * p1) + (w10 * a0 + w11 * a1)
+                    out[v, c, s, k - 1] += term
+                held[v, c] = (a0, a1)
+
+
+def pull_pair(odd, offsets, source, w, out):
+    for behind, ahead in (((0, 0, 0), (0, 3, 0)), ((0, 1, 1), (1, 2, 0)), ((1, 0, 1), (1, 3, 1))):
+        s, i, index = (jnp.where(odd, b, a) for a, b in zip(behind, ahead))
+        pull(offsets, source, index, s, i, w, out)
+
+
+def near_body(affine, place, offsets, ext, chip, w, diag, keep, base, out):
+    stay(ext, diag, keep, base, out, affine)
+    pull(offsets, ext, 1, 0, 2, w, out)
+    pull(offsets, ext, 0, 1, 1, w, out)
+    pull_pair(place[4] == 0, offsets, chip, w, out)
+
+
+def far_body(place, offsets, part, link, w, out):
+    out[...] = part[...]
+    pull_pair(place[4] == 1, offsets, link, w, out)
+
+
+def products(pairs, blocks):
+    comps, count, height, q, lanes = next(iter(blocks.values()))[0].shape[1:]
+    sums = [jnp.zeros((8, lanes), jnp.float32) for _ in pairs]
     for c in range(comps):
         for s in range(count):
             for r in range(height):
                 for h in range(q // 8):
                     at = pl.ds(8 * h, 8)
-                    vec = (
-                        start[1, c, s, r, at, :], force[0, c, s, r, at, :], force[1, c, s, r, at, :],
-                        second[0, c, s, r, at, :], second[1, c, s, r, at, :], out[0, c, s, r, at, :],
-                    )
-                    sums = [g + vec[i] * vec[j] for g, (i, j) in zip(sums, PAIRS)]
+                    vec = {n: ref[v, c, s, r, at, :] for n, (ref, v) in blocks.items()}
+                    sums = [g + vec[i] * vec[j] for g, (i, j) in zip(sums, pairs)]
     lane = lax.broadcasted_iota(jnp.int32, (1, lanes), 1)
     packed = jnp.zeros((1, lanes), jnp.float32)
-    for n, g in enumerate(sums):
-        packed = jnp.where(lane == n, jnp.sum(g), packed)
-    part[...] = jnp.broadcast_to(packed[None], part.shape)
+    for pair, g in zip(pairs, sums):
+        packed = jnp.where(lane == PAIRS.index(pair), jnp.sum(g), packed)
+    return packed
+
+
+EARLY = [pair for pair in PAIRS if pair[1] < NB - 1]
+LATE = [pair for pair in PAIRS if pair[1] == NB - 1]
+
+
+def basis(start, force, second):
+    return {0: (start, 1), 1: (force, 0), 2: (force, 1), 3: (second, 0), 4: (second, 1)}
+
+
+def near_last_body(place, offsets, ext, chip, w, diag, keep, base, start, force, second, out, early):
+    near_body((False,), place, offsets, ext, chip, w, diag, keep, base, out)
+    early[...] = products(EARLY, basis(start, force, second))
+
+
+def far_last_body(place, offsets, part, link, w, early, start, force, second, out, sums):
+    far_body(place, offsets, part, link, w, out)
+    late = products(LATE, {**basis(start, force, second), NB - 1: (out, 0)})
+    sums[...] = jnp.broadcast_to((early[...] + late)[None], sums.shape)
 
 
 def coefficients(gram, norms=None):
@@ -263,20 +306,28 @@
                 v_ref[c, s, :, cols] = v
 
 
-def neighbours(low_edge, high_edge, axis):
-    count = lax.axis_size(axis)
-    pairs = [(i, i + 1) for i in range(count - 1)]
-    before = lax.ppermute(high_edge, axis, pairs)
-    after = lax.ppermute(low_edge, axis, [(b, a) for a, b in pairs])
-    return before, after
-
-
-def exchange(x):
+def swapped(x, axis, first):
+    pairs = []
+    for i in range(first, lax.axis_size(axis) - 1, 2):
+        pairs += [(i, i + 1), (i + 1, i)]
+    return lax.ppermute(x, axis, pairs)
+
+
+def taller(x):
     height = x.shape[3]
-    above, below = neighbours(x[:, :, :, :DOWN], x[:, :, :, height - UP :], TILE)
-    ext = jnp.concatenate([above, x, below], axis=3)
-    left, right = neighbours(ext, ext, SEC)
-    return ext, left, right
+    odd = lax.axis_index(TILE) % 2 == 1
+    top = lambda a: lax.dynamic_slice_in_dim(x, jnp.where(a, 0, height - DOWN), DOWN, 3)
+    outer = swapped(top(~odd), TILE, 1)
+    inner = swapped(top(odd), TILE, 0)
+    above = jnp.where(odd, inner, outer)[:, :, :, DOWN - UP :]
+    below = jnp.where(odd, outer, inner)
+    return jnp.concatenate([above, x, below], axis=3)
+
+
+def across(ext):
+    link = swapped(ext, SEC, 1)
+    chip = swapped(ext, SEC, 0)
+    return chip, link
 
 
 def sent_to_all(shard, axis):
@@ -296,12 +347,21 @@
             lax.axis_index(TILE) * height,
             jnp.int32(count * lax.axis_size(SEC)),
             jnp.int32(height * lax.axis_size(TILE)),
+            lax.axis_index(SEC) % 2,
         ]
     ).astype(jnp.int32)
     shifts = offsets.reshape(-1)
 
     start = call(
-        relayout, f32(2, comps, count, height * q, 128), [VMEM] * 3, "relayout"
+        relayout,
+        f32(2, comps, count, height * q, 128),
+        [HBM] * 3,
+        scratch=[
+            pltpu.VMEM(displacement.shape, jnp.float32),
+            pltpu.VMEM(displacement.shape, jnp.float32),
+            pltpu.VMEM(fixed.shape, jnp.int32),
+            pltpu.SemaphoreType.DMA((3,)),
+        ],
     )(displacement, velocity, fixed)
     by_row = start.reshape(2, comps, count, height, q, 128)
 
@@ -319,28 +379,29 @@
             f32(comps, count, height * q, 128),
         ],
         [SMEM] * 3 + [VMEM] * 2,
-        "weights",
     )(place, shifts, anchor.reshape(-1), frac, fixed)
 
-    def springs(x, affine, name):
-        return call(
-            lambda *refs: springs_body(affine, *refs),
-            f32(*x.shape),
-            [SMEM] + [VMEM] * 7,
-            name,
-        )(shifts, *exchange(x), w, diag, keep, base)
-
-    force = springs(by_row, (True, False), "force")
-    second = springs(force, (False, False), "second")
+    def springs(x, affine):
+        ext = taller(x)
+        chip, link = across(ext)
+        part = call(
+            lambda *refs: near_body(affine, *refs), f32(*x.shape), [SMEM] * 2 + [VMEM] * 6
+        )(place, shifts, ext, chip, w, diag, keep, base)
+        return call(far_body, f32(*x.shape), [SMEM] * 2 + [VMEM] * 3)(place, shifts, part, link, w)
+
+    force = springs(by_row, (True, False))
+    second = springs(force, (False, False))
+    ext = taller(second[:1])
+    chip, link = across(ext)
+    third, early = call(
+        near_last_body, [f32(*second[:1].shape), f32(1, 128)], [SMEM] * 2 + [VMEM] * 9
+    )(place, shifts, ext, chip, w, diag, keep, base, by_row, force, second)
     third, part = call(
-        lambda *refs: last_body(devices, *refs),
-        [f32(1, *by_row.shape[1:]), f32(devices, 1, 128)],
-        [SMEM] + [VMEM] * 10,
-        "third",
-    )(shifts, *exchange(second[:1]), w, diag, keep, base, by_row, force, second)
+        far_last_body, [f32(*third.shape), f32(devices, 1, 128)], [SMEM] * 2 + [VMEM] * 7
+    )(place, shifts, third, link, w, early, by_row, force, second)
 
     parts = lax.all_to_all(part, SEC_TILE, 0, 0, tiled=True)
-    coef = call(solve_body, f32(1, 128), [VMEM], "solve")(parts)[0]
+    coef = call(solve_body, f32(1, 128), [VMEM])(parts)[0]
 
     def measured(coef):
         basis = (by_row[1], force[0], force[1], second[0], second[1], third[0])
@@ -356,10 +417,7 @@
 
     flat = lambda x: x.reshape(*x.shape[:3], height * q, 128)
     return call(
-        final_body,
-        [f32(*displacement.shape)] * 2,
-        [SMEM] + [VMEM] * 4,
-        "final",
+        final_body, [f32(*displacement.shape)] * 2, [SMEM] + [VMEM] * 4
     )(coef, start, flat(force), flat(second), flat(third))
 
 

time: 132 us -> 119 us (0.902)
  starting transfers between devices: 42.8 us -> 33.9 us
  blocking collectives: 43.7 us -> 35.3 us
  Pallas kernels: 10.6 us -> 12.9 us
  waiting for transfers between devices: 28 us -> 29.8 us
    ppermute x12, starting transfers between devices: 37.5 us -> 28.8 us  [swapped(): return lax.ppermute(x, axis, pairs)]
    all_to_all x1, blocking collectives: 43.7 us -> 35.3 us  [shards(): parts = lax.all_to_all(part, SEC_TILE, 0, 0, tiled=True)]
    pallas_call x6 -> x9, Pallas kernels: 8.71 us -> 11 us  [the longest x2 3.33 us: springs(): call(lambda *refs: near_body(affine, *refs), f32(*x.shape), [SMEM] * 2 +...]
    ppermute x12, waiting for transfers between devices: 20.5 us -> 22.3 us  [swapped(): return lax.ppermute(x, axis, pairs)]
  transfers between devices with their start and end apart: 13 -> 13, of which waited for: 9 -> 6; matrix products, arithmetic and copies ran while one was open for 1% -> 1% of each run, Pallas kernels for 1% -> 6%
where the time goes in v2:
time: 119 us
  blocking collectives  35.3 us (30%)
  starting transfers between devices  33.9 us (28%)
  waiting for transfers between devices  29.8 us (25%)
  Pallas kernels  12.9 us (11%)
  local copies, waits for them, and re-layouts  4.59 us (4%)
  between operations  1.6 us (1%)
    all_to_all x1, blocking collectives, shards(): parts = lax.all_to_all(part, SEC_TILE, 0, 0, tiled=True)  35.3 us
    ppermute x12, starting transfers between devices, swapped(): return lax.ppermute(x, axis, pairs)  28.8 us
    ppermute x12, waiting for transfers between devices, swapped(): return lax.ppermute(x, axis, pairs)  22.3 us
    all_to_all x1, waiting for transfers between devices, sent_to_all(): lax.all_to_all(jnp.broadcast_to(shard[None], (count, *shard.shape)), axis...  7.47 us
    all_to_all x1, starting transfers between devices, sent_to_all(): lax.all_to_all(jnp.broadcast_to(shard[None], (count, *shard.shape)), axis...  5.15 us
    pallas_call x2, Pallas kernels, springs(): call(lambda *refs: near_body(affine, *refs), f32(*x.shape), [SMEM] * 2 +...  3.33 us
    unnamed x19, local copies, waits for them, and re-layouts  2.92 us
  transfers between devices with their start and end apart: 13, of which 6 were waited for; matrix products, arithmetic and copies ran while one was open for 1% of the time, Pallas kernels for 6%

profile of v2, /device:TPU:1, one launch (start us, length us, event | category | flops | bytes accessed | tf_op | source)
XLA Modules:
  0.0 118.5 jit_solution(13525378708326912909)
XLA Ops:
  0.7 0.9 copy-done.1
  1.6 0.9 copy-done.3
  2.5 0.9 copy-done.4
  3.9 2.5 %collective-permute-start = (f32[2,2,2,3,16,128]{5,4,3,2,1,0:T(8,128)S(1)}, f32[2,2,2,3,16,128]{5,4,3,2,1,0:T(8,128)S(1)}, u32[]{:S(2)}, u32[]{:S(2)}) collective-permute-start(f32[2,2,2,3,16,128]{5,4,3,2,1,0:T(8,128)S(1)} %get-tuple-element.49), channel_id=1, source_target_pairs={{0,1},{1,0},{2,3},{3,2},{4,5},{5,4},{6,7},{7,6},{8,9},{9,8},{10,11... | collective-permute-start | bytes 589832 | tf_op jit(solution)/shard_map/ppermute | solution.py:313
  6.5 0.7 collective-permute-start.1
  7.1 2.9 %collective-permute-done = f32[2,2,2,3,16,128]{5,4,3,2,1,0:T(8,128)S(1)} collective-permute-done((f32[2,2,2,3,16,128]{5,4,3,2,1,0:T(8,128)S(1)}, f32[2,2,2,3,16,128]{5,4,3,2,1,0:T(8,128)S(1)}, u32[]{:S(2)}, u32[]{:S(2)}) %collective-permute-start) | collective-permute-done | bytes 196640 | tf_op jit(solution)/shard_map/ppermute | solution.py:313
  10.2 2.9 %collective-permute-start.2 = (f32[2,2,2,13,16,128]{5,4,3,2,1,0:T(8,128)S(1)}, f32[2,2,2,13,16,128]{5,4,3,2,1,0:T(8,128)S(1)}, u32[]{:S(2)}, u32[]{:S(2)}) collective-permute-start(f32[2,2,2,13,16,128]{5,4,3,2,1,0:T(8,128)S(1)} %pad_maximum_fusion.refs_2_), channel_id=1, source_target_pairs={{0,16},{16,0},{32,48},{48,32},{64,80},{80,64},{96,112},{112,96},{1... | collective-permute-start | bytes 2555912 | tf_op jit(solution)/shard_map/ppermute | solution.py:313
  13.1 2.5 %collective-permute-start.3 = (f32[2,2,2,13,16,128]{5,4,3,2,1,0:T(8,128)S(1)}, f32[2,2,2,13,16,128]{5,4,3,2,1,0:T(8,128)S(1)}, u32[]{:S(2)}, u32[]{:S(2)}) collective-permute-start(f32[2,2,2,13,16,128]{5,4,3,2,1,0:T(8,128)S(1)} %pad_maximum_fusion.refs_2_), channel_id=1, source_target_pairs={{16,32},{32,16},{48,64},{64,48},{80,96},{96,80},{112,128},{128,112... | collective-permute-start | bytes 2555912 | tf_op jit(solution)/shard_map/ppermute | solution.py:313
  15.7 0.6 broadcast_in_dim.20
  16.3 5.1 %all-to-all-start = ((f32[16,1,2]{2,1,0:T(1,128)}), f32[16,1,2]{2,1,0:T(1,128)S(1)}, u32[]{:S(2)}, u32[]{:S(2)}) async-start(f32[16,1,2]{2,1,0:T(1,128)} %broadcast_in_dim.20), calls=%async_computation | async-start | bytes 16384 | tf_op jit(solution)/shard_map/all_to_all | solution.py:335
  21.7 7.5 %all-to-all-done = f32[16,1,2]{2,1,0:T(1,128)S(1)} async-done(((f32[16,1,2]{2,1,0:T(1,128)}), f32[16,1,2]{2,1,0:T(1,128)S(1)}, u32[]{:S(2)}, u32[]{:S(2)}) %all-to-all-start) | async-done | bytes 160 | tf_op jit(solution)/shard_map/all_to_all | solution.py:335
  29.5 1.9 %shard_map.78 = (f32[2,4,4,128,128]{4,3,2,1,0:T(8,128)S(1)}, f32[2,128,128]{2,1,0:T(8,128)S(1)}, f32[2,128,128]{2,1,0:T(8,128)S(1)}, f32[2,2,128,128]{3,2,1,0:T(8,128)S(1)}) custom-call(s32[5]{0:T(128)S(1)} %stack.51.place_ref.refs_0_.place, s32[16]{0:T(128)S(1)} %reshape.76.offsets_ref.refs_1_.offsets, f32[4]{0:T(128)S(1)} %add.234.anchor_ref, ...), custom_call_target="tpu_custom_call" | custom-call | flops 4000000 | bytes 4000000 | tf_op jit(solution)/shard_map/pallas_call | solution.py:373
  31.4 1.7 %shard_map.79.part = f32[2,2,2,8,16,128]{5,4,3,2,1,0:T(8,128)S(1)} custom-call(s32[5]{0:T(128)S(1)} %stack.51.place_ref.refs_0_.place, s32[16]{0:T(128)S(1)} %reshape.76.offsets_ref.refs_1_.offsets, f32[2,2,2,13,16,128]{5,4,3,2,1,0:T(8,128)S(1)} %pad_maximum_fusion.refs_2_, f32[2,2,2,13,16,128]{5,4,3,2,1,0:T(8,128)S(1)} %collective-permute-done.2.refs_3_, ...), custom_call_target="tpu_custom_call" | custom-call | flops 4000000 | bytes 4000000 | tf_op jit(solution)/shard_map/pallas_call | solution.py:387
  33.1 1.1 shard_map.80.force
  34.2 5.2 %collective-permute-start.4 = (f32[2,2,2,3,16,128]{5,4,3,2,1,0:T(8,128)S(1)}, f32[2,2,2,3,16,128]{5,4,3,2,1,0:T(8,128)S(1)}, u32[]{:S(2)}, u32[]{:S(2)}) collective-permute-start(f32[2,2,2,3,16,128]{5,4,3,2,1,0:T(8,128)S(1)} %get-tuple-element.47), channel_id=1, source_target_pairs={{0,1},{1,0},{2,3},{3,2},{4,5},{5,4},{6,7},{7,6},{8,9},{9,8},{10,11... | collective-permute-start | bytes 589832 | tf_op jit(solution)/shard_map/ppermute | solution.py:313
  39.5 0.7 collective-permute-start.5
  40.2 3.9 %collective-permute-done.4 = f32[2,2,2,3,16,128]{5,4,3,2,1,0:T(8,128)S(1)} collective-permute-done((f32[2,2,2,3,16,128]{5,4,3,2,1,0:T(8,128)S(1)}, f32[2,2,2,3,16,128]{5,4,3,2,1,0:T(8,128)S(1)}, u32[]{:S(2)}, u32[]{:S(2)}) %collective-permute-start.4) | collective-permute-done | bytes 196640 | tf_op jit(solution)/shard_map/ppermute | solution.py:313
  44.2 1.4 %collective-permute-start.6 = (f32[2,2,2,13,16,128]{5,4,3,2,1,0:T(8,128)S(1)}, f32[2,2,2,13,16,128]{5,4,3,2,1,0:T(8,128)S(1)}, u32[]{:S(2)}, u32[]{:S(2)}) collective-permute-start(f32[2,2,2,13,16,128]{5,4,3,2,1,0:T(8,128)S(1)} %pad_maximum_fusion.1.refs_2_), channel_id=1, source_target_pairs={{0,16},{16,0},{32,48},{48,32},{64,80},{80,64},{96,112},{112,96},{1... | collective-permute-start | bytes 2555912 | tf_op jit(solution)/shard_map/ppermute | solution.py:313
  45.6 2.4 %collective-permute-start.7 = (f32[2,2,2,13,16,128]{5,4,3,2,1,0:T(8,128)S(1)}, f32[2,2,2,13,16,128]{5,4,3,2,1,0:T(8,128)S(1)}, u32[]{:S(2)}, u32[]{:S(2)}) collective-permute-start(f32[2,2,2,13,16,128]{5,4,3,2,1,0:T(8,128)S(1)} %pad_maximum_fusion.1.refs_2_), channel_id=1, source_target_pairs={{16,32},{32,16},{48,64},{64,48},{80,96},{96,80},{112,128},{128,112... | collective-permute-start | bytes 2555912 | tf_op jit(solution)/shard_map/ppermute | solution.py:313
  48.0 1.6 %shard_map.81.part = f32[2,2,2,8,16,128]{5,4,3,2,1,0:T(8,128)S(1)} custom-call(s32[5]{0:T(128)S(1)} %stack.51.place_ref.refs_0_.place, s32[16]{0:T(128)S(1)} %reshape.76.offsets_ref.refs_1_.offsets, f32[2,2,2,13,16,128]{5,4,3,2,1,0:T(8,128)S(1)} %pad_maximum_fusion.1.refs_2_, f32[2,2,2,13,16,128]{5,4,3,2,1,0:T(8,128)S(1)} %collective-permute-done.6.refs_3_, ...), custom_call_target="tpu_custom_call" | custom-call | flops 4000000 | bytes 4000000 | tf_op jit(solution)/shard_map/pallas_call | solution.py:387
  49.7 9.9 %collective-permute-done.7.link = f32[2,2,2,13,16,128]{5,4,3,2,1,0:T(8,128)S(1)} collective-permute-done((f32[2,2,2,13,16,128]{5,4,3,2,1,0:T(8,128)S(1)}, f32[2,2,2,13,16,128]{5,4,3,2,1,0:T(8,128)S(1)}, u32[]{:S(2)}, u32[]{:S(2)}) %collective-permute-start.7) | collective-permute-done | bytes 852000 | tf_op jit(solution)/shard_map/ppermute | solution.py:313
  59.6 1.1 shard_map.82.second
  60.7 5.6 %collective-permute-start.8 = (f32[1,2,2,3,16,128]{5,4,3,2,1,0:T(8,128)S(1)}, f32[1,2,2,3,16,128]{5,4,3,2,1,0:T(8,128)S(1)}, u32[]{:S(2)}, u32[]{:S(2)}) collective-permute-start(f32[1,2,2,3,16,128]{5,4,3,2,1,0:T(8,128)S(1)} %get-tuple-element.51), channel_id=1, source_target_pairs={{0,1},{1,0},{2,3},{3,2},{4,5},{5,4},{6,7},{7,6},{8,9},{9,8},{10,11... | collective-permute-start | bytes 294920 | tf_op jit(solution)/shard_map/ppermute | solution.py:313
  66.3 0.7 collective-permute-start.9
  67.0 1.3 %collective-permute-done.8 = f32[1,2,2,3,16,128]{5,4,3,2,1,0:T(8,128)S(1)} collective-permute-done((f32[1,2,2,3,16,128]{5,4,3,2,1,0:T(8,128)S(1)}, f32[1,2,2,3,16,128]{5,4,3,2,1,0:T(8,128)S(1)}, u32[]{:S(2)}, u32[]{:S(2)}) %collective-permute-start.8) | collective-permute-done | bytes 98336 | tf_op jit(solution)/shard_map/ppermute | solution.py:313
  68.5 4.2 %collective-permute-start.11 = (f32[1,2,2,13,16,128]{5,4,3,2,1,0:T(8,128)S(1)}, f32[1,2,2,13,16,128]{5,4,3,2,1,0:T(8,128)S(1)}, u32[]{:S(2)}, u32[]{:S(2)}) collective-permute-start(f32[1,2,2,13,16,128]{5,4,3,2,1,0:T(8,128)S(1)} %pad_maximum_fusion.2.ext), channel_id=1, source_target_pairs={{16,32},{32,16},{48,64},{64,48},{80,96},{96,80},{112,128},{128,112... | collective-permute-start | bytes 1277960 | tf_op jit(solution)/shard_map/ppermute | solution.py:313
  72.7 1.5 %shard_map.83 = (f32[1,2,2,8,16,128]{5,4,3,2,1,0:T(8,128)S(1)}, f32[1,128]{1,0:T(1,128)S(1)}) custom-call(s32[5]{0:T(128)S(1)} %stack.51.place_ref.refs_0_.place, s32[16]{0:T(128)S(1)} %reshape.76.offsets_ref.refs_1_.offsets, f32[1,2,2,13,16,128]{5,4,3,2,1,0:T(8,128)S(1)} %pad_maximum_fusion.2.ext, ...), custom_call_target="tpu_custom_call" | custom-call | flops 4000000 | bytes 4000000 | tf_op jit(solution)/shard_map/pallas_call | solution.py:396
  74.2 4.3 %collective-permute-done.11.link = f32[1,2,2,13,16,128]{5,4,3,2,1,0:T(8,128)S(1)} collective-permute-done((f32[1,2,2,13,16,128]{5,4,3,2,1,0:T(8,128)S(1)}, f32[1,2,2,13,16,128]{5,4,3,2,1,0:T(8,128)S(1)}, u32[]{:S(2)}, u32[]{:S(2)}) %collective-permute-start.11) | collective-permute-done | bytes 426016 | tf_op jit(solution)/shard_map/ppermute | solution.py:313
  78.5 1.2 %shard_map.84 = (f32[1,2,2,8,16,128]{5,4,3,2,1,0:T(8,128)S(1)}, f32[256,1,128]{2,1,0:T(1,128)S(1)}) custom-call(s32[5]{0:T(128)S(1)} %stack.51.place_ref.refs_0_.place, s32[16]{0:T(128)S(1)} %reshape.76.offsets_ref.refs_1_.offsets, f32[1,2,2,8,16,128]{5,4,3,2,1,0:T(8,128)S(1)} %get-tuple-element.33.part, ...), custom_call_target="tpu_custom_call" | custom-call | flops 4000000 | bytes 4000000 | tf_op jit(solution)/shard_map/pallas_call | solution.py:399
  79.7 35.3 %all_to_all.14.parts = f32[256,1,128]{2,1,0:T(1,128)S(1)} all-to-all(f32[256,1,128]{2,1,0:T(1,128)S(1)} %get-tuple-element.35), channel_id=1, replica_groups=mesh['sec_0'=2,'sec_1'=4,'sec_2'=2,'tile_0'=2,'tile_1'=8] {'sec_0','sec_..., dimensions={0} | all-to-all | bytes 262144 | tf_op jit(solution)/shard_map/all_to_all | solution.py:403
  115.4 0.6 slice.45
  116.7 1.8 %shard_map.86 = (f32[2,2,8,2048]{3,2,1,0:T(8,128)}, f32[2,2,8,2048]{3,2,1,0:T(8,128)}) custom-call(f32[128]{0:T(128)S(1)} %get-tuple-element.53.coef, f32[2,2,2,128,128]{4,3,2,1,0:T(8,128)S(1)} %copy-done.6, f32[2,2,2,128,128]{4,3,2,1,0:T(8,128)S(1)} %bitcast.171, f32[2,2,2,128,128]{4,3,2,1,0:T(8,128)S(1)} %bitcast.172, f32[1,2,2,128,128]{4,3,2,1,0:T(8,128)S(1)} %bitcast.178), custom_call_target="tpu_custom_call" | custom-call | flops 4000000 | bytes 4000000 | tf_op jit(solution)/shard_map/pallas_call | solution.py:419
  (49 shorter events, 2.1 us)
Async XLA Ops:
  0.7 0.9 copy-start.1
  1.6 0.9 copy-start.3
  2.5 0.9 copy-start.4
  3.5 12.1 %copy-start.8 = (f32[2,2]{1,0:T(2,128)S(1)}, f32[2,2]{1,0:T(2,128)}, u32[]{:S(2)}) copy-start(f32[2,2]{1,0:T(2,128)} %param.13) | copy-start | bytes 52
  3.5 17.9 %copy-start.7 = (s32[4,2,1,2]{0,3,2,1:T(2,128)S(1)}, s32[4,2,1,2]{0,3,2,1:T(2,128)}, u32[]{:S(2)}) copy-start(s32[4,2,1,2]{0,3,2,1:T(2,128)} %param.11) | copy-start | bytes 196
  3.5 26.0 %copy-start = (bf16[2,4,2,8,2048]{4,3,2,1,0:T(8,128)(2,1)S(1)}, bf16[2,4,2,8,2048]{4,3,2,1,0:T(8,128)(2,1)}, u32[]{:S(2)}) copy-start(bf16[2,4,2,8,2048]{4,3,2,1,0:T(8,128)(2,1)} %frac_ref.1) | copy-start | bytes 1572868
  3.5 26.0 %copy-start.2 = (s32[2,8,2048]{2,1,0:T(8,128)S(1)}, s32[2,8,2048]{2,1,0:T(8,128)}, u32[]{:S(2)}) copy-start(s32[2,8,2048]{2,1,0:T(8,128)} %fixed_ref.1) | copy-start | bytes 393220
  3.9 6.3 %copy-start.5 = (f32[2,2,2,128,128]{4,3,2,1,0:T(8,128)}, f32[2,2,2,128,128]{4,3,2,1,0:T(8,128)S(1)}, u32[]{:S(2)}) copy-start(f32[2,2,2,128,128]{4,3,2,1,0:T(8,128)S(1)} %shard_map.77.start) | copy-start | bytes 1572868
  3.9 6.1 %collective-permute-start = (f32[2,2,2,3,16,128]{5,4,3,2,1,0:T(8,128)S(1)}, f32[2,2,2,3,16,128]{5,4,3,2,1,0:T(8,128)S(1)}, u32[]{:S(2)}, u32[]{:S(2)}) collective-permute-start(f32[2,2,2,3,16,128]{5,4,3,2,1,0:T(8,128)S(1)} %get-tuple-element.49), channel_id=1, source_target_pairs={{0,1},{1,0},{2,3},{3,2},{4,5},{5,4},{6,7},{7,6},{8,9},{9,8},{10,11... | collective-permute-start | bytes 589832 | tf_op jit(solution)/shard_map/ppermute | solution.py:313
  6.5 3.6 %collective-permute-start.1 = (f32[2,2,2,3,16,128]{5,4,3,2,1,0:T(8,128)S(1)}, f32[2,2,2,3,16,128]{5,4,3,2,1,0:T(8,128)S(1)}, u32[]{:S(2)}, u32[]{:S(2)}) collective-permute-start(f32[2,2,2,3,16,128]{5,4,3,2,1,0:T(8,128)S(1)} %get-tuple-element.50), channel_id=1, source_target_pairs={{1,2},{2,1},{3,4},{4,3},{5,6},{6,5},{7,8},{8,7},{9,10},{10,9},{11,... | collective-permute-start | bytes 589832 | tf_op jit(solution)/shard_map/ppermute | solution.py:313
  10.2 21.2 %collective-permute-start.2 = (f32[2,2,2,13,16,128]{5,4,3,2,1,0:T(8,128)S(1)}, f32[2,2,2,13,16,128]{5,4,3,2,1,0:T(8,128)S(1)}, u32[]{:S(2)}, u32[]{:S(2)}) collective-permute-start(f32[2,2,2,13,16,128]{5,4,3,2,1,0:T(8,128)S(1)} %pad_maximum_fusion.refs_2_), channel_id=1, source_target_pairs={{0,16},{16,0},{32,48},{48,32},{64,80},{80,64},{96,112},{112,96},{1... | collective-permute-start | bytes 2555912 | tf_op jit(solution)/shard_map/ppermute | solution.py:313
  13.1 20.0 %collective-permute-start.3 = (f32[2,2,2,13,16,128]{5,4,3,2,1,0:T(8,128)S(1)}, f32[2,2,2,13,16,128]{5,4,3,2,1,0:T(8,128)S(1)}, u32[]{:S(2)}, u32[]{:S(2)}) collective-permute-start(f32[2,2,2,13,16,128]{5,4,3,2,1,0:T(8,128)S(1)} %pad_maximum_fusion.refs_2_), channel_id=1, source_target_pairs={{16,32},{32,16},{48,64},{64,48},{80,96},{96,80},{112,128},{128,112... | collective-permute-start | bytes 2555912 | tf_op jit(solution)/shard_map/ppermute | solution.py:313
  16.3 12.9 %all-to-all-start = ((f32[16,1,2]{2,1,0:T(1,128)}), f32[16,1,2]{2,1,0:T(1,128)S(1)}, u32[]{:S(2)}, u32[]{:S(2)}) async-start(f32[16,1,2]{2,1,0:T(1,128)} %broadcast_in_dim.20), calls=%async_computation | async-start | bytes 16384 | tf_op jit(solution)/shard_map/all_to_all | solution.py:335
  34.2 9.8 %collective-permute-start.4 = (f32[2,2,2,3,16,128]{5,4,3,2,1,0:T(8,128)S(1)}, f32[2,2,2,3,16,128]{5,4,3,2,1,0:T(8,128)S(1)}, u32[]{:S(2)}, u32[]{:S(2)}) collective-permute-start(f32[2,2,2,3,16,128]{5,4,3,2,1,0:T(8,128)S(1)} %get-tuple-element.47), channel_id=1, source_target_pairs={{0,1},{1,0},{2,3},{3,2},{4,5},{5,4},{6,7},{7,6},{8,9},{9,8},{10,11... | collective-permute-start | bytes 589832 | tf_op jit(solution)/shard_map/ppermute | solution.py:313
  39.5 4.6 %collective-permute-start.5 = (f32[2,2,2,3,16,128]{5,4,3,2,1,0:T(8,128)S(1)}, f32[2,2,2,3,16,128]{5,4,3,2,1,0:T(8,128)S(1)}, u32[]{:S(2)}, u32[]{:S(2)}) collective-permute-start(f32[2,2,2,3,16,128]{5,4,3,2,1,0:T(8,128)S(1)} %get-tuple-element.48), channel_id=1, source_target_pairs={{1,2},{2,1},{3,4},{4,3},{5,6},{6,5},{7,8},{8,7},{9,10},{10,9},{11,... | collective-permute-start | bytes 589832 | tf_op jit(solution)/shard_map/ppermute | solution.py:313
  44.2 3.8 %collective-permute-start.6 = (f32[2,2,2,13,16,128]{5,4,3,2,1,0:T(8,128)S(1)}, f32[2,2,2,13,16,128]{5,4,3,2,1,0:T(8,128)S(1)}, u32[]{:S(2)}, u32[]{:S(2)}) collective-permute-start(f32[2,2,2,13,16,128]{5,4,3,2,1,0:T(8,128)S(1)} %pad_maximum_fusion.1.refs_2_), channel_id=1, source_target_pairs={{0,16},{16,0},{32,48},{48,32},{64,80},{80,64},{96,112},{112,96},{1... | collective-permute-start | bytes 2555912 | tf_op jit(solution)/shard_map/ppermute | solution.py:313
  45.6 14.0 %collective-permute-start.7 = (f32[2,2,2,13,16,128]{5,4,3,2,1,0:T(8,128)S(1)}, f32[2,2,2,13,16,128]{5,4,3,2,1,0:T(8,128)S(1)}, u32[]{:S(2)}, u32[]{:S(2)}) collective-permute-start(f32[2,2,2,13,16,128]{5,4,3,2,1,0:T(8,128)S(1)} %pad_maximum_fusion.1.refs_2_), channel_id=1, source_target_pairs={{16,32},{32,16},{48,64},{64,48},{80,96},{96,80},{112,128},{128,112... | collective-permute-start | bytes 2555912 | tf_op jit(solution)/shard_map/ppermute | solution.py:313
  60.7 12.0 %copy-start.6 = (f32[2,2,2,128,128]{4,3,2,1,0:T(8,128)S(1)}, f32[2,2,2,128,128]{4,3,2,1,0:T(8,128)}, u32[]{:S(2)}) copy-start(f32[2,2,2,128,128]{4,3,2,1,0:T(8,128)} %copy-done.5) | copy-start | bytes 1572868
  60.7 7.6 %collective-permute-start.8 = (f32[1,2,2,3,16,128]{5,4,3,2,1,0:T(8,128)S(1)}, f32[1,2,2,3,16,128]{5,4,3,2,1,0:T(8,128)S(1)}, u32[]{:S(2)}, u32[]{:S(2)}) collective-permute-start(f32[1,2,2,3,16,128]{5,4,3,2,1,0:T(8,128)S(1)} %get-tuple-element.51), channel_id=1, source_target_pairs={{0,1},{1,0},{2,3},{3,2},{4,5},{5,4},{6,7},{7,6},{8,9},{9,8},{10,11... | collective-permute-start | bytes 294920 | tf_op jit(solution)/shard_map/ppermute | solution.py:313
  66.3 2.0 %collective-permute-start.9 = (f32[1,2,2,3,16,128]{5,4,3,2,1,0:T(8,128)S(1)}, f32[1,2,2,3,16,128]{5,4,3,2,1,0:T(8,128)S(1)}, u32[]{:S(2)}, u32[]{:S(2)}) collective-permute-start(f32[1,2,2,3,16,128]{5,4,3,2,1,0:T(8,128)S(1)} %get-tuple-element.52), channel_id=1, source_target_pairs={{1,2},{2,1},{3,4},{4,3},{5,6},{6,5},{7,8},{8,7},{9,10},{10,9},{11,... | collective-permute-start | bytes 294920 | tf_op jit(solution)/shard_map/ppermute | solution.py:313
  68.4 4.3 %collective-permute-start.10 = (f32[1,2,2,13,16,128]{5,4,3,2,1,0:T(8,128)S(1)}, f32[1,2,2,13,16,128]{5,4,3,2,1,0:T(8,128)S(1)}, u32[]{:S(2)}, u32[]{:S(2)}) collective-permute-start(f32[1,2,2,13,16,128]{5,4,3,2,1,0:T(8,128)S(1)} %pad_maximum_fusion.2.ext), channel_id=1, source_target_pairs={{0,16},{16,0},{32,48},{48,32},{64,80},{80,64},{96,112},{112,96},{1... | collective-permute-start | bytes 1277960 | tf_op jit(solution)/shard_map/ppermute | solution.py:313
  68.5 10.0 %collective-permute-start.11 = (f32[1,2,2,13,16,128]{5,4,3,2,1,0:T(8,128)S(1)}, f32[1,2,2,13,16,128]{5,4,3,2,1,0:T(8,128)S(1)}, u32[]{:S(2)}, u32[]{:S(2)}) collective-permute-start(f32[1,2,2,13,16,128]{5,4,3,2,1,0:T(8,128)S(1)} %pad_maximum_fusion.2.ext), channel_id=1, source_target_pairs={{16,32},{32,16},{48,64},{64,48},{80,96},{96,80},{112,128},{128,112... | collective-permute-start | bytes 1277960 | tf_op jit(solution)/shard_map/ppermute | solution.py:313

commit v3 on v2

--- a/solution.py
+++ b/solution.py
@@ -27,13 +27,10 @@
 VMEM = pl.BlockSpec(memory_space=pltpu.VMEM)
 SMEM = pl.BlockSpec(memory_space=pltpu.SMEM)
 HBM = pl.BlockSpec(memory_space=pltpu.HBM)
-
-
-def params():
-    return pltpu.CompilerParams(vmem_limit_bytes=48 << 20)
-
-
-def call(body, out_shape, in_specs, flops=4_000_000, bytes_accessed=4_000_000, scratch=()):
+FULL = (64 << 20) - (1280 << 10)
+
+
+def call(body, out_shape, in_specs, flops=4_000_000, bytes_accessed=4_000_000, scratch=(), vmem=16 << 20):
     multi = isinstance(out_shape, (list, tuple))
     return pl.pallas_call(
         body,
@@ -41,7 +38,7 @@
         in_specs=in_specs,
         out_specs=[VMEM] * len(out_shape) if multi else VMEM,
         scratch_shapes=list(scratch),
-        compiler_params=params(),
+        compiler_params=pltpu.CompilerParams(vmem_limit_bytes=vmem),
         cost_estimate=pl.CostEstimate(flops=flops, bytes_accessed=bytes_accessed, transcendentals=0),
     )
 
@@ -74,53 +71,56 @@
 
 
 def weights(
-    place_ref, offsets_ref, anchor_ref, frac_ref, fixed_ref,
-    w_ref, diag_ref, keep_ref, base_ref,
+    place_ref, offsets_ref, frac_ref, fixed_ref,
+    w_ref, diag_ref, keep_ref, base_ref, frac,
 ):
     count, height, width = fixed_ref.shape
     q = width // 128
     sec_first, row_first, sections, rows = (place_ref[k] for k in range(4))
-    grow = row_first + lax.broadcasted_iota(jnp.int32, (height, 128), 0)
-    lane = lax.broadcasted_iota(jnp.int32, (height, 128), 1)
-    row_links = (grow > 0).astype(jnp.float32) + (grow < rows - 1).astype(jnp.float32)
     for s in range(count):
-        shift, row_stiff = [], []
+        for j in range(q):
+            cols = pl.ds(128 * j, 128)
+            at = pl.ds(j, height, stride=q)
+            keep_ref.at[s][at, :] = (1 - fixed_ref[s, :, cols]).astype(jnp.float32)
+            for i in range(4):
+                for c in range(2):
+                    frac.at[c, i][at, :] = frac_ref[c, i, s, :, cols].astype(jnp.float32)
+        sub = lax.broadcasted_iota(jnp.int32, (q, 128), 0)
+        gcol = lax.broadcasted_iota(jnp.int32, (q, 128), 1) + 128 * sub
+        col_links = (gcol > 0).astype(jnp.float32) + (gcol < width - 1).astype(jnp.float32)
+        springs = []
         for i in range(4):
             dr, dc = offsets_ref[i * count * 2 + s * 2], offsets_ref[i * count * 2 + s * 2 + 1]
             other = sec_first + s + reaches[i]
-            there = ((other >= 0) & (other < sections)).astype(jnp.float32) * cross_stiff[i]
-            row_ok = (grow + dr >= 0) & (grow + dr + 1 <= rows - 1)
-            shift.append((dr, dc))
-            row_stiff.append(jnp.where(row_ok, there, 0.0))
-        for j in range(q):
-            cols = pl.ds(128 * j, 128)
-            gcol = lane + 128 * j
-            keep = (1 - fixed_ref[s, :, cols]).astype(jnp.float32)
-            total = jnp.zeros((height, 128), jnp.float32)
-            base = [keep * (anchor_stiff * anchor_ref[s * 2 + c]) for c in range(2)]
-            at = pl.ds(j, height, stride=q)
+            there = (other >= 0) & (other < sections)
+            col_ok = (gcol + dc >= 0) & (gcol + dc + 1 <= width - 1) & there
+            springs.append((dr, dc, jnp.where(col_ok, cross_stiff[i], 0.0)))
+        for r in range(height):
+            at = pl.ds(r * q, q)
+            grow = row_first + r
+            row_links = jnp.where(grow > 0, 1.0, 0.0) + jnp.where(grow < rows - 1, 1.0, 0.0)
+            keep = keep_ref[s, at, :]
+            total = keep * (in_stiff * (row_links + col_links) + anchor_stiff)
+            base = [jnp.zeros((q, 128), jnp.float32) for _ in range(2)]
             for i in range(4):
-                dr, dc = shift[i]
-                col_ok = (gcol + dc >= 0) & (gcol + dc + 1 <= width - 1)
-                stiff = jnp.where(col_ok, row_stiff[i], 0.0) * keep
-                frow = frac_ref[0, i, s, :, cols].astype(jnp.float32)
-                fcol = frac_ref[1, i, s, :, cols].astype(jnp.float32)
+                dr, dc, col_stiff = springs[i]
+                row_ok = (grow + dr >= 0) & (grow + dr + 1 <= rows - 1)
+                stiff = col_stiff * keep * jnp.where(row_ok, 1.0, 0.0)
+                frow, fcol = frac[0, i, at, :], frac[1, i, at, :]
                 low = stiff * frow
                 high = stiff - low
                 w11 = low * fcol
                 w01 = high * fcol
-                w_ref.at[s, i, 0][at, :] = high - w01
-                w_ref.at[s, i, 1][at, :] = w01
-                w_ref.at[s, i, 2][at, :] = low - w11
-                w_ref.at[s, i, 3][at, :] = w11
+                w_ref[s, i, 0, at, :] = high - w01
+                w_ref[s, i, 1, at, :] = w01
+                w_ref[s, i, 2, at, :] = low - w11
+                w_ref[s, i, 3, at, :] = w11
                 total = total + stiff
                 base[0] = base[0] + stiff * (dr.astype(jnp.float32) + frow)
                 base[1] = base[1] + stiff * (dc.astype(jnp.float32) + fcol)
-            links = row_links + (gcol > 0).astype(jnp.float32) + (gcol < width - 1).astype(jnp.float32)
-            diag_ref.at[s][at, :] = total + keep * (in_stiff * links + anchor_stiff)
-            keep_ref.at[s][at, :] = keep * in_stiff
+            diag_ref[s, at, :] = total
             for c in range(2):
-                base_ref.at[c, s][at, :] = base[c]
+                base_ref[c, s, at, :] = base[c]
 
 
 def stay(ext, diag, keep, base, out, affine):
@@ -141,7 +141,7 @@
                     after = jnp.where(lane >= 1, x, pltpu.roll(x, q - 1, 0))
                     before = jnp.where(first, 0.0, pltpu.roll(before, 1, 1))
                     after = jnp.where(last, 0.0, pltpu.roll(after, lanes - 1, 1))
-                    near = ext[v, c, s, r + UP - 1] + ext[v, c, s, r + UP + 1] + before + after
+                    near = in_stiff * (ext[v, c, s, r + UP - 1] + ext[v, c, s, r + UP + 1] + before + after)
                     y = kept * near - own * x
                     if affine[v]:
                         y = y + base[c, s, at, :]
@@ -200,6 +200,17 @@
     pull_pair(place[4] == 1, offsets, link, w, out)
 
 
+def far_first_body(place, offsets, anchor, part, link, w, keep, out):
+    _, comps, count, height, q, _ = out.shape
+    out[1:] = part[1:]
+    for s in range(count):
+        for c in range(comps):
+            pulled = anchor_stiff * anchor[s, c]
+            for r in range(height):
+                out[0, c, s, r] = part[0, c, s, r] + keep[s, pl.ds(r * q, q), :] * pulled
+    pull_pair(place[4] == 1, offsets, link, w, out)
+
+
 def products(pairs, blocks):
     comps, count, height, q, lanes = next(iter(blocks.values()))[0].shape[1:]
     sums = [jnp.zeros((8, lanes), jnp.float32) for _ in pairs]
@@ -282,28 +293,29 @@
     out[...] = packed
 
 
-def final_body(coef, start, force, second, third, u_ref, v_ref):
+def final_body(coef, start, force, second, third, u_ref, v_ref, flat):
     comps, count, height, width = u_ref.shape
     q = width // 128
     vel = [coef[n] for n in range(NB)]
     move = [coef[NB + n] for n in range(NB)]
+    blocks = ((start, 1), (force, 0), (force, 1), (second, 0), (second, 1), (third, 0))
     for c in range(comps):
         for s in range(count):
-            for j in range(q):
-                at = pl.ds(j, height, stride=q)
-                cols = pl.ds(128 * j, 128)
-                vec = (
-                    start.at[1, c, s][at, :], force.at[0, c, s][at, :], force.at[1, c, s][at, :],
-                    second.at[0, c, s][at, :], second.at[1, c, s][at, :], third.at[0, c, s][at, :],
-                )
-                u = start.at[0, c, s][at, :]
+            for r in range(height):
+                at = pl.ds(r * q, q)
+                vec = [ref[n, c, s, at, :] for ref, n in blocks]
+                u = start[0, c, s, at, :]
                 v = vel[0] * vec[0]
                 u = u + move[0] * vec[0]
                 for n in range(1, NB):
                     v = v + vel[n] * vec[n]
                     u = u + move[n] * vec[n]
-                u_ref[c, s, :, cols] = u
-                v_ref[c, s, :, cols] = v
+                flat[0, at, :] = u
+                flat[1, at, :] = v
+            for j in range(q):
+                at = pl.ds(j, height, stride=q)
+                u_ref[c, s, :, pl.ds(128 * j, 128)] = flat.at[0][at, :]
+                v_ref[c, s, :, pl.ds(128 * j, 128)] = flat.at[1][at, :]
 
 
 def swapped(x, axis, first):
@@ -313,28 +325,21 @@
     return lax.ppermute(x, axis, pairs)
 
 
-def taller(x):
+def exchange(x, first=()):
     height = x.shape[3]
     odd = lax.axis_index(TILE) % 2 == 1
-    top = lambda a: lax.dynamic_slice_in_dim(x, jnp.where(a, 0, height - DOWN), DOWN, 3)
-    outer = swapped(top(~odd), TILE, 1)
-    inner = swapped(top(odd), TILE, 0)
+    edge = lambda top: lax.dynamic_slice_in_dim(x, jnp.where(top, 0, height - DOWN), DOWN, 3)
+    outer = swapped(edge(~odd), TILE, 1)
+    inner = swapped(edge(odd), TILE, 0)
+    link = swapped(lax.optimization_barrier((x, *first))[0] if first else x, SEC, 1)
     above = jnp.where(odd, inner, outer)[:, :, :, DOWN - UP :]
     below = jnp.where(odd, outer, inner)
-    return jnp.concatenate([above, x, below], axis=3)
-
-
-def across(ext):
-    link = swapped(ext, SEC, 1)
+    edges = jnp.concatenate([above, below], axis=3)
+    link_edges = swapped(edges, SEC, 1)
+    ext = jnp.concatenate([above, x, below], axis=3)
     chip = swapped(ext, SEC, 0)
-    return chip, link
-
-
-def sent_to_all(shard, axis):
-    count = lax.axis_size(axis)
-    return lax.all_to_all(
-        jnp.broadcast_to(shard[None], (count, *shard.shape)), axis, 0, 0, tiled=True
-    )
+    link = jnp.concatenate([link_edges[:, :, :, :UP], link, link_edges[:, :, :, UP:]], axis=3)
+    return ext, chip, link
 
 
 def shards(displacement, velocity, frac, offsets, fixed, trans):
@@ -362,13 +367,17 @@
             pltpu.VMEM(fixed.shape, jnp.int32),
             pltpu.SemaphoreType.DMA((3,)),
         ],
+        vmem=FULL,
     )(displacement, velocity, fixed)
     by_row = start.reshape(2, comps, count, height, q, 128)
 
     local = jnp.cumsum(trans, 0)
-    pieces = sent_to_all(local[-1], SEC).reshape(-1, 2)
-    passed = jnp.arange(pieces.shape[0]) < lax.axis_index(SEC)
-    anchor = local + jnp.sum(jnp.where(passed[:, None], pieces, 0.0), 0)[None]
+    group = lax.axis_size(SEC)
+    pieces = lax.all_to_all(
+        jnp.broadcast_to(local[-1][None, None], (group, 1, 2)), SEC, 0, 0, tiled=True
+    )
+    passed = jnp.arange(group) < lax.axis_index(SEC)
+    anchor = local + jnp.sum(jnp.where(passed[:, None], pieces[:, 0], 0.0), 0)[None]
 
     w, diag, keep, base = call(
         weights,
@@ -378,21 +387,24 @@
             f32(count, height * q, 128),
             f32(comps, count, height * q, 128),
         ],
-        [SMEM] * 3 + [VMEM] * 2,
-    )(place, shifts, anchor.reshape(-1), frac, fixed)
-
-    def springs(x, affine):
-        ext = taller(x)
-        chip, link = across(ext)
-        part = call(
+        [SMEM] * 2 + [VMEM] * 2,
+        scratch=[pltpu.VMEM((2, 4, height * q, 128), jnp.float32)],
+    )(place, shifts, frac, fixed)
+
+    def near(x, ext, chip, affine):
+        return call(
             lambda *refs: near_body(affine, *refs), f32(*x.shape), [SMEM] * 2 + [VMEM] * 6
         )(place, shifts, ext, chip, w, diag, keep, base)
-        return call(far_body, f32(*x.shape), [SMEM] * 2 + [VMEM] * 3)(place, shifts, part, link, w)
-
-    force = springs(by_row, (True, False))
-    second = springs(force, (False, False))
-    ext = taller(second[:1])
-    chip, link = across(ext)
+
+    ext, chip, link = exchange(by_row, (place, shifts, anchor))
+    part = near(by_row, ext, chip, (True, False))
+    force = call(far_first_body, f32(*part.shape), [SMEM] * 3 + [VMEM] * 4)(
+        place, shifts, anchor, part, link, w, keep
+    )
+    ext, chip, link = exchange(force)
+    part = near(force, ext, chip, (False, False))
+    second = call(far_body, f32(*part.shape), [SMEM] * 2 + [VMEM] * 3)(place, shifts, part, link, w)
+    ext, chip, link = exchange(second[:1])
     third, early = call(
         near_last_body, [f32(*second[:1].shape), f32(1, 128)], [SMEM] * 2 + [VMEM] * 9
     )(place, shifts, ext, chip, w, diag, keep, base, by_row, force, second)
@@ -417,7 +429,10 @@
 
     flat = lambda x: x.reshape(*x.shape[:3], height * q, 128)
     return call(
-        final_body, [f32(*displacement.shape)] * 2, [SMEM] + [VMEM] * 4
+        final_body,
+        [f32(*displacement.shape)] * 2,
+        [SMEM] + [VMEM] * 4,
+        scratch=[pltpu.VMEM((2, height * q, 128), jnp.float32)],
     )(coef, start, flat(force), flat(second), flat(third))
 
 

time: 119 us -> 124 us (1.042)
  starting transfers between devices: 33.9 us -> 44.9 us
  blocking collectives: 35.3 us -> 31.3 us
  local copies, waits for them, and re-layouts: 4.59 us -> 2.43 us
    ppermute x12 -> x15, starting transfers between devices: 28.8 us -> 38.1 us  [swapped(): return lax.ppermute(x, axis, pairs)]
    all_to_all x1, waiting for transfers between devices: 7.47 us -> 0.01 us  [shards(): lax.all_to_all(jnp.broadcast_to(local[-1][None, None], (group, 1, 2)), SE...]
    ppermute x12 -> x15, waiting for transfers between devices: 22.3 us -> 29.2 us  [swapped(): return lax.ppermute(x, axis, pairs)]
    all_to_all x1, blocking collectives: 35.3 us -> 31.3 us  [shards(): parts = lax.all_to_all(part, SEC_TILE, 0, 0, tiled=True)]
    unnamed x19 -> x5, local copies, waits for them, and re-layouts: 2.92 us -> 0.79 us
    all_to_all x1, starting transfers between devices: 5.15 us -> 6.82 us  [shards(): lax.all_to_all(jnp.broadcast_to(local[-1][None, None], (group, 1, 2)), SE...]
  transfers between devices with their start and end apart: 13 -> 16, of which waited for: 6 -> 6; matrix products, arithmetic and copies ran while one was open for 1% -> 1% of each run, Pallas kernels for 6% -> 2%
where the time goes in v3:
time: 124 us
  starting transfers between devices  44.9 us (36%)
  blocking collectives  31.3 us (25%)
  waiting for transfers between devices  29.2 us (24%)
  Pallas kernels  13.1 us (11%)
  local copies, waits for them, and re-layouts  2.43 us (2%)
  between operations  1.68 us (1%)
  other arithmetic  1.38 us (1%)
    ppermute x15, starting transfers between devices, swapped(): return lax.ppermute(x, axis, pairs)  38.1 us
    all_to_all x1, blocking collectives, shards(): parts = lax.all_to_all(part, SEC_TILE, 0, 0, tiled=True)  31.3 us
    ppermute x15, waiting for transfers between devices, swapped(): return lax.ppermute(x, axis, pairs)  29.2 us
    all_to_all x1, starting transfers between devices, shards(): lax.all_to_all(jnp.broadcast_to(local[-1][None, None], (group, 1, 2)), SE...  6.82 us
    pallas_call x2, Pallas kernels, near(): call(lambda *refs: near_body(affine, *refs), f32(*x.shape), [SMEM] * 2 +...  3.3 us
  transfers between devices with their start and end apart: 16, of which 6 were waited for; matrix products, arithmetic and copies ran while one was open for 1% of the time, Pallas kernels for 2%

profile of v3, /device:TPU:1, one launch (start us, length us, event | category | flops | bytes accessed | tf_op | source)
XLA Modules:
  0.0 123.9 jit_solution(4501132528102706521)
XLA Ops:
  0.6 0.7 reduce_window_sum.11
  2.0 6.8 %all-to-all-start = ((f32[16,1,2]{2,1,0:T(1,128)}), f32[16,1,2]{2,1,0:T(1,128)S(1)}, u32[]{:S(2)}, u32[]{:S(2)}) async-start(f32[16,1,2]{2,1,0:T(1,128)} %broadcast_in_dim.23), calls=%async_computation | async-start | bytes 16384 | tf_op jit(solution)/shard_map/all_to_all | solution.py:376
  8.8 1.3 %shard_map.77.start = f32[2,2,2,128,128]{4,3,2,1,0:T(8,128)S(1)} custom-call(f32[2,2,8,2048]{3,2,1,0:T(8,128)} %u_hbm.1, f32[2,2,8,2048]{3,2,1,0:T(8,128)} %vel_hbm.1, s32[2,8,2048]{2,1,0:T(8,128)} %fixed_ref.1), custom_call_target="tpu_custom_call" | custom-call | flops 4000000 | bytes 4000000 | tf_op jit(solution)/shard_map/pallas_call | solution.py:360
  10.1 0.8 collective-permute-start.1
  10.9 4.6 %collective-permute-start = (f32[2,2,2,3,16,128]{5,4,3,2,1,0:T(8,128)S(1)}, f32[2,2,2,3,16,128]{5,4,3,2,1,0:T(8,128)S(1)}, u32[]{:S(2)}, u32[]{:S(2)}) collective-permute-start(f32[2,2,2,3,16,128]{5,4,3,2,1,0:T(8,128)S(1)} %get-tuple-element.51), channel_id=1, source_target_pairs={{0,1},{1,0},{2,3},{3,2},{4,5},{5,4},{6,7},{7,6},{8,9},{9,8},{10,11... | collective-permute-start | bytes 589832 | tf_op jit(solution)/shard_map/ppermute | solution.py:325
  15.5 0.8 copy.10
  16.7 3.7 %collective-permute-done = f32[2,2,2,3,16,128]{5,4,3,2,1,0:T(8,128)S(1)} collective-permute-done((f32[2,2,2,3,16,128]{5,4,3,2,1,0:T(8,128)S(1)}, f32[2,2,2,3,16,128]{5,4,3,2,1,0:T(8,128)S(1)}, u32[]{:S(2)}, u32[]{:S(2)}) %collective-permute-start) | collective-permute-done | bytes 196640 | tf_op jit(solution)/shard_map/ppermute | solution.py:325
  20.5 1.1 collective-permute-start.2
  21.6 3.2 %collective-permute-start.4 = (f32[2,2,2,8,16,128]{5,4,3,2,1,0:T(8,128)S(1)}, f32[2,2,2,8,16,128]{5,4,3,2,1,0:T(8,128)S(1)}, u32[]{:S(2)}, u32[]{:S(2)}) collective-permute-start(f32[2,2,2,8,16,128]{5,4,3,2,1,0:T(8,128)S(1)} %bitcast.175), channel_id=1, source_target_pairs={{16,32},{32,16},{48,64},{64,48},{80,96},{96,80},{112,128},{128,112... | collective-permute-start | bytes 1572872 | tf_op jit(solution)/shard_map/ppermute | solution.py:325
  24.8 2.4 %collective-permute-start.3 = (f32[2,2,2,5,16,128]{5,4,3,2,1,0:T(8,128)S(1)}, f32[2,2,2,5,16,128]{5,4,3,2,1,0:T(8,128)S(1)}, u32[]{:S(2)}, u32[]{:S(2)}) collective-permute-start(f32[2,2,2,5,16,128]{5,4,3,2,1,0:T(8,128)S(1)} %pad_maximum_fusion.6), channel_id=1, source_target_pairs={{16,32},{32,16},{48,64},{64,48},{80,96},{96,80},{112,128},{128,112... | collective-permute-start | bytes 983048 | tf_op jit(solution)/shard_map/ppermute | solution.py:325
  27.2 1.4 %shard_map.78 = (f32[2,4,4,128,128]{4,3,2,1,0:T(8,128)S(1)}, f32[2,128,128]{2,1,0:T(8,128)S(1)}, f32[2,128,128]{2,1,0:T(8,128)S(1)}, f32[2,2,128,128]{3,2,1,0:T(8,128)S(1)}) custom-call(s32[5]{0:T(128)S(1)} %stack.51.place_ref.refs_0_.place, s32[16]{0:T(128)S(1)} %reshape.69.offsets_ref.refs_1_.offsets, bf16[2,4,2,8,2048]{4,3,2,1,0:T(8,128)(2,1)S(1)} %copy-done.1, ...), custom_call_target="tpu_custom_call" | custom-call | flops 4000000 | bytes 4000000 | tf_op jit(solution)/shard_map/pallas_call | solution.py:382
  28.6 7.3 %collective-permute-done.3 = f32[2,2,2,5,16,128]{5,4,3,2,1,0:T(8,128)S(1)} collective-permute-done((f32[2,2,2,5,16,128]{5,4,3,2,1,0:T(8,128)S(1)}, f32[2,2,2,5,16,128]{5,4,3,2,1,0:T(8,128)S(1)}, u32[]{:S(2)}, u32[]{:S(2)}) %collective-permute-start.3) | collective-permute-done | bytes 327712 | tf_op jit(solution)/shard_map/ppermute | solution.py:325
  36.0 1.7 %shard_map.79.part = f32[2,2,2,8,16,128]{5,4,3,2,1,0:T(8,128)S(1)} custom-call(s32[5]{0:T(128)S(1)} %stack.51.place_ref.refs_0_.place, s32[16]{0:T(128)S(1)} %reshape.69.offsets_ref.refs_1_.offsets, f32[2,2,2,13,16,128]{5,4,3,2,1,0:T(8,128)S(1)} %pad_maximum_fusion.refs_2_, f32[2,2,2,13,16,128]{5,4,3,2,1,0:T(8,128)S(1)} %collective-permute-done.2.refs_3_, ...), custom_call_target="tpu_custom_call" | custom-call | flops 4000000 | bytes 4000000 | tf_op jit(solution)/shard_map/pallas_call | solution.py:395
  37.7 1.1 shard_map.80.force
  38.8 0.7 collective-permute-start.6
  39.5 5.8 %collective-permute-start.5 = (f32[2,2,2,3,16,128]{5,4,3,2,1,0:T(8,128)S(1)}, f32[2,2,2,3,16,128]{5,4,3,2,1,0:T(8,128)S(1)}, u32[]{:S(2)}, u32[]{:S(2)}) collective-permute-start(f32[2,2,2,3,16,128]{5,4,3,2,1,0:T(8,128)S(1)} %get-tuple-element.49), channel_id=1, source_target_pairs={{0,1},{1,0},{2,3},{3,2},{4,5},{5,4},{6,7},{7,6},{8,9},{9,8},{10,11... | collective-permute-start | bytes 589832 | tf_op jit(solution)/shard_map/ppermute | solution.py:325
  45.3 3.1 %collective-permute-done.5 = f32[2,2,2,3,16,128]{5,4,3,2,1,0:T(8,128)S(1)} collective-permute-done((f32[2,2,2,3,16,128]{5,4,3,2,1,0:T(8,128)S(1)}, f32[2,2,2,3,16,128]{5,4,3,2,1,0:T(8,128)S(1)}, u32[]{:S(2)}, u32[]{:S(2)}) %collective-permute-start.5) | collective-permute-done | bytes 196640 | tf_op jit(solution)/shard_map/ppermute | solution.py:325
  48.6 5.7 %collective-permute-start.9 = (f32[2,2,2,8,16,128]{5,4,3,2,1,0:T(8,128)S(1)}, f32[2,2,2,8,16,128]{5,4,3,2,1,0:T(8,128)S(1)}, u32[]{:S(2)}, u32[]{:S(2)}) collective-permute-start(f32[2,2,2,8,16,128]{5,4,3,2,1,0:T(8,128)S(1)} %shard_map.80.force), channel_id=1, source_target_pairs={{16,32},{32,16},{48,64},{64,48},{80,96},{96,80},{112,128},{128,112... | collective-permute-start | bytes 1572872 | tf_op jit(solution)/shard_map/ppermute | solution.py:325
  54.3 1.9 %collective-permute-start.8 = (f32[2,2,2,5,16,128]{5,4,3,2,1,0:T(8,128)S(1)}, f32[2,2,2,5,16,128]{5,4,3,2,1,0:T(8,128)S(1)}, u32[]{:S(2)}, u32[]{:S(2)}) collective-permute-start(f32[2,2,2,5,16,128]{5,4,3,2,1,0:T(8,128)S(1)} %pad_maximum_fusion.7), channel_id=1, source_target_pairs={{16,32},{32,16},{48,64},{64,48},{80,96},{96,80},{112,128},{128,112... | collective-permute-start | bytes 983048 | tf_op jit(solution)/shard_map/ppermute | solution.py:325
  56.3 8.4 %collective-permute-done.8 = f32[2,2,2,5,16,128]{5,4,3,2,1,0:T(8,128)S(1)} collective-permute-done((f32[2,2,2,5,16,128]{5,4,3,2,1,0:T(8,128)S(1)}, f32[2,2,2,5,16,128]{5,4,3,2,1,0:T(8,128)S(1)}, u32[]{:S(2)}, u32[]{:S(2)}) %collective-permute-start.8) | collective-permute-done | bytes 327712 | tf_op jit(solution)/shard_map/ppermute | solution.py:325
  64.8 1.6 %shard_map.81.part = f32[2,2,2,8,16,128]{5,4,3,2,1,0:T(8,128)S(1)} custom-call(s32[5]{0:T(128)S(1)} %stack.51.place_ref.refs_0_.place, s32[16]{0:T(128)S(1)} %reshape.69.offsets_ref.refs_1_.offsets, f32[2,2,2,13,16,128]{5,4,3,2,1,0:T(8,128)S(1)} %pad_maximum_fusion.2.refs_2_, f32[2,2,2,13,16,128]{5,4,3,2,1,0:T(8,128)S(1)} %collective-permute-done.7.refs_3_, ...), custom_call_target="tpu_custom_call" | custom-call | flops 4000000 | bytes 4000000 | tf_op jit(solution)/shard_map/pallas_call | solution.py:395
  66.5 1.1 shard_map.82.second
  67.6 0.7 collective-permute-start.11
  68.3 3.9 %collective-permute-start.10 = (f32[1,2,2,3,16,128]{5,4,3,2,1,0:T(8,128)S(1)}, f32[1,2,2,3,16,128]{5,4,3,2,1,0:T(8,128)S(1)}, u32[]{:S(2)}, u32[]{:S(2)}) collective-permute-start(f32[1,2,2,3,16,128]{5,4,3,2,1,0:T(8,128)S(1)} %get-tuple-element.53), channel_id=1, source_target_pairs={{0,1},{1,0},{2,3},{3,2},{4,5},{5,4},{6,7},{7,6},{8,9},{9,8},{10,11... | collective-permute-start | bytes 294920 | tf_op jit(solution)/shard_map/ppermute | solution.py:325
  72.2 2.0 %collective-permute-done.10 = f32[1,2,2,3,16,128]{5,4,3,2,1,0:T(8,128)S(1)} collective-permute-done((f32[1,2,2,3,16,128]{5,4,3,2,1,0:T(8,128)S(1)}, f32[1,2,2,3,16,128]{5,4,3,2,1,0:T(8,128)S(1)}, u32[]{:S(2)}, u32[]{:S(2)}) %collective-permute-start.10) | collective-permute-done | bytes 98336 | tf_op jit(solution)/shard_map/ppermute | solution.py:325
  74.4 5.4 %collective-permute-start.14 = (f32[1,2,2,8,16,128]{5,4,3,2,1,0:T(8,128)S(1)}, f32[1,2,2,8,16,128]{5,4,3,2,1,0:T(8,128)S(1)}, u32[]{:S(2)}, u32[]{:S(2)}) collective-permute-start(f32[1,2,2,8,16,128]{5,4,3,2,1,0:T(8,128)S(1)} %slice.75), channel_id=1, source_target_pairs={{16,32},{32,16},{48,64},{64,48},{80,96},{96,80},{112,128},{128,112... | collective-permute-start | bytes 786440 | tf_op jit(solution)/shard_map/ppermute | solution.py:325
  79.8 1.9 %collective-permute-start.13 = (f32[1,2,2,5,16,128]{5,4,3,2,1,0:T(8,128)S(1)}, f32[1,2,2,5,16,128]{5,4,3,2,1,0:T(8,128)S(1)}, u32[]{:S(2)}, u32[]{:S(2)}) collective-permute-start(f32[1,2,2,5,16,128]{5,4,3,2,1,0:T(8,128)S(1)} %pad_maximum_fusion.8), channel_id=1, source_target_pairs={{16,32},{32,16},{48,64},{64,48},{80,96},{96,80},{112,128},{128,112... | collective-permute-start | bytes 491528 | tf_op jit(solution)/shard_map/ppermute | solution.py:325
  81.7 4.7 %collective-permute-done.13 = f32[1,2,2,5,16,128]{5,4,3,2,1,0:T(8,128)S(1)} collective-permute-done((f32[1,2,2,5,16,128]{5,4,3,2,1,0:T(8,128)S(1)}, f32[1,2,2,5,16,128]{5,4,3,2,1,0:T(8,128)S(1)}, u32[]{:S(2)}, u32[]{:S(2)}) %collective-permute-start.13) | collective-permute-done | bytes 163872 | tf_op jit(solution)/shard_map/ppermute | solution.py:325
  86.5 1.6 %shard_map.83 = (f32[1,2,2,8,16,128]{5,4,3,2,1,0:T(8,128)S(1)}, f32[1,128]{1,0:T(1,128)S(1)}) custom-call(s32[5]{0:T(128)S(1)} %stack.51.place_ref.refs_0_.place, s32[16]{0:T(128)S(1)} %reshape.69.offsets_ref.refs_1_.offsets, f32[1,2,2,13,16,128]{5,4,3,2,1,0:T(8,128)S(1)} %pad_maximum_fusion.4.ext, ...), custom_call_target="tpu_custom_call" | custom-call | flops 4000000 | bytes 4000000 | tf_op jit(solution)/shard_map/pallas_call | solution.py:408
  88.1 1.2 shard_map.84
  89.3 31.3 %all_to_all.10.parts = f32[256,1,128]{2,1,0:T(1,128)S(1)} all-to-all(f32[256,1,128]{2,1,0:T(1,128)S(1)} %get-tuple-element.37), channel_id=1, replica_groups=mesh['sec_0'=2,'sec_1'=4,'sec_2'=2,'tile_0'=2,'tile_1'=8] {'sec_0','sec_..., dimensions={0} | all-to-all | bytes 262144 | tf_op jit(solution)/shard_map/all_to_all | solution.py:415
  122.3 1.7 %shard_map.86 = (f32[2,2,8,2048]{3,2,1,0:T(8,128)}, f32[2,2,8,2048]{3,2,1,0:T(8,128)}) custom-call(f32[128]{0:T(128)S(1)} %get-tuple-element.55.coef, f32[2,2,2,128,128]{4,3,2,1,0:T(8,128)S(1)} %shard_map.77.start, f32[2,2,2,128,128]{4,3,2,1,0:T(8,128)S(1)} %bitcast.171, f32[2,2,2,128,128]{4,3,2,1,0:T(8,128)S(1)} %bitcast.172, ...), custom_call_target="tpu_custom_call" | custom-call | flops 4000000 | bytes 4000000 | tf_op jit(solution)/shard_map/pallas_call | solution.py:431
  (52 shorter events, 3.0 us)
Async XLA Ops:
  2.0 14.5 %all-to-all-start = ((f32[16,1,2]{2,1,0:T(1,128)}), f32[16,1,2]{2,1,0:T(1,128)S(1)}, u32[]{:S(2)}, u32[]{:S(2)}) async-start(f32[16,1,2]{2,1,0:T(1,128)} %broadcast_in_dim.23), calls=%async_computation | async-start | bytes 16384 | tf_op jit(solution)/shard_map/all_to_all | solution.py:376
  10.0 17.2 %copy-start = (s32[2,8,2048]{2,1,0:T(8,128)S(1)}, s32[2,8,2048]{2,1,0:T(8,128)}, u32[]{:S(2)}) copy-start(s32[2,8,2048]{2,1,0:T(8,128)} %fixed_ref.1) | copy-start | bytes 393220
  10.0 17.2 %copy-start.1 = (bf16[2,4,2,8,2048]{4,3,2,1,0:T(8,128)(2,1)S(1)}, bf16[2,4,2,8,2048]{4,3,2,1,0:T(8,128)(2,1)}, u32[]{:S(2)}) copy-start(bf16[2,4,2,8,2048]{4,3,2,1,0:T(8,128)(2,1)} %frac_ref.1) | copy-start | bytes 1572868
  10.1 6.6 %collective-permute-start.1 = (f32[2,2,2,3,16,128]{5,4,3,2,1,0:T(8,128)S(1)}, f32[2,2,2,3,16,128]{5,4,3,2,1,0:T(8,128)S(1)}, u32[]{:S(2)}, u32[]{:S(2)}) collective-permute-start(f32[2,2,2,3,16,128]{5,4,3,2,1,0:T(8,128)S(1)} %get-tuple-element.52), channel_id=1, source_target_pairs={{1,2},{2,1},{3,4},{4,3},{5,6},{6,5},{7,8},{8,7},{9,10},{10,9},{11,... | collective-permute-start | bytes 589832 | tf_op jit(solution)/shard_map/ppermute | solution.py:325
  10.9 9.5 %collective-permute-start = (f32[2,2,2,3,16,128]{5,4,3,2,1,0:T(8,128)S(1)}, f32[2,2,2,3,16,128]{5,4,3,2,1,0:T(8,128)S(1)}, u32[]{:S(2)}, u32[]{:S(2)}) collective-permute-start(f32[2,2,2,3,16,128]{5,4,3,2,1,0:T(8,128)S(1)} %get-tuple-element.51), channel_id=1, source_target_pairs={{0,1},{1,0},{2,3},{3,2},{4,5},{5,4},{6,7},{7,6},{8,9},{9,8},{10,11... | collective-permute-start | bytes 589832 | tf_op jit(solution)/shard_map/ppermute | solution.py:325
  20.5 15.5 %collective-permute-start.2 = (f32[2,2,2,13,16,128]{5,4,3,2,1,0:T(8,128)S(1)}, f32[2,2,2,13,16,128]{5,4,3,2,1,0:T(8,128)S(1)}, u32[]{:S(2)}, u32[]{:S(2)}) collective-permute-start(f32[2,2,2,13,16,128]{5,4,3,2,1,0:T(8,128)S(1)} %pad_maximum_fusion.refs_2_), channel_id=1, source_target_pairs={{0,16},{16,0},{32,48},{48,32},{64,80},{80,64},{96,112},{112,96},{1... | collective-permute-start | bytes 2555912 | tf_op jit(solution)/shard_map/ppermute | solution.py:325
  21.6 14.3 %collective-permute-start.4 = (f32[2,2,2,8,16,128]{5,4,3,2,1,0:T(8,128)S(1)}, f32[2,2,2,8,16,128]{5,4,3,2,1,0:T(8,128)S(1)}, u32[]{:S(2)}, u32[]{:S(2)}) collective-permute-start(f32[2,2,2,8,16,128]{5,4,3,2,1,0:T(8,128)S(1)} %bitcast.175), channel_id=1, source_target_pairs={{16,32},{32,16},{48,64},{64,48},{80,96},{96,80},{112,128},{128,112... | collective-permute-start | bytes 1572872 | tf_op jit(solution)/shard_map/ppermute | solution.py:325
  24.8 11.1 %collective-permute-start.3 = (f32[2,2,2,5,16,128]{5,4,3,2,1,0:T(8,128)S(1)}, f32[2,2,2,5,16,128]{5,4,3,2,1,0:T(8,128)S(1)}, u32[]{:S(2)}, u32[]{:S(2)}) collective-permute-start(f32[2,2,2,5,16,128]{5,4,3,2,1,0:T(8,128)S(1)} %pad_maximum_fusion.6), channel_id=1, source_target_pairs={{16,32},{32,16},{48,64},{64,48},{80,96},{96,80},{112,128},{128,112... | collective-permute-start | bytes 983048 | tf_op jit(solution)/shard_map/ppermute | solution.py:325
  38.8 6.4 %collective-permute-start.6 = (f32[2,2,2,3,16,128]{5,4,3,2,1,0:T(8,128)S(1)}, f32[2,2,2,3,16,128]{5,4,3,2,1,0:T(8,128)S(1)}, u32[]{:S(2)}, u32[]{:S(2)}) collective-permute-start(f32[2,2,2,3,16,128]{5,4,3,2,1,0:T(8,128)S(1)} %get-tuple-element.50), channel_id=1, source_target_pairs={{1,2},{2,1},{3,4},{4,3},{5,6},{6,5},{7,8},{8,7},{9,10},{10,9},{11,... | collective-permute-start | bytes 589832 | tf_op jit(solution)/shard_map/ppermute | solution.py:325
  39.5 8.8 %collective-permute-start.5 = (f32[2,2,2,3,16,128]{5,4,3,2,1,0:T(8,128)S(1)}, f32[2,2,2,3,16,128]{5,4,3,2,1,0:T(8,128)S(1)}, u32[]{:S(2)}, u32[]{:S(2)}) collective-permute-start(f32[2,2,2,3,16,128]{5,4,3,2,1,0:T(8,128)S(1)} %get-tuple-element.49), channel_id=1, source_target_pairs={{0,1},{1,0},{2,3},{3,2},{4,5},{5,4},{6,7},{7,6},{8,9},{9,8},{10,11... | collective-permute-start | bytes 589832 | tf_op jit(solution)/shard_map/ppermute | solution.py:325
  48.5 16.3 %collective-permute-start.7 = (f32[2,2,2,13,16,128]{5,4,3,2,1,0:T(8,128)S(1)}, f32[2,2,2,13,16,128]{5,4,3,2,1,0:T(8,128)S(1)}, u32[]{:S(2)}, u32[]{:S(2)}) collective-permute-start(f32[2,2,2,13,16,128]{5,4,3,2,1,0:T(8,128)S(1)} %pad_maximum_fusion.2.refs_2_), channel_id=1, source_target_pairs={{0,16},{16,0},{32,48},{48,32},{64,80},{80,64},{96,112},{112,96},{1... | collective-permute-start | bytes 2555912 | tf_op jit(solution)/shard_map/ppermute | solution.py:325
  48.6 16.1 %collective-permute-start.9 = (f32[2,2,2,8,16,128]{5,4,3,2,1,0:T(8,128)S(1)}, f32[2,2,2,8,16,128]{5,4,3,2,1,0:T(8,128)S(1)}, u32[]{:S(2)}, u32[]{:S(2)}) collective-permute-start(f32[2,2,2,8,16,128]{5,4,3,2,1,0:T(8,128)S(1)} %shard_map.80.force), channel_id=1, source_target_pairs={{16,32},{32,16},{48,64},{64,48},{80,96},{96,80},{112,128},{128,112... | collective-permute-start | bytes 1572872 | tf_op jit(solution)/shard_map/ppermute | solution.py:325
  54.3 10.3 %collective-permute-start.8 = (f32[2,2,2,5,16,128]{5,4,3,2,1,0:T(8,128)S(1)}, f32[2,2,2,5,16,128]{5,4,3,2,1,0:T(8,128)S(1)}, u32[]{:S(2)}, u32[]{:S(2)}) collective-permute-start(f32[2,2,2,5,16,128]{5,4,3,2,1,0:T(8,128)S(1)} %pad_maximum_fusion.7), channel_id=1, source_target_pairs={{16,32},{32,16},{48,64},{64,48},{80,96},{96,80},{112,128},{128,112... | collective-permute-start | bytes 983048 | tf_op jit(solution)/shard_map/ppermute | solution.py:325
  67.6 4.6 %collective-permute-start.11 = (f32[1,2,2,3,16,128]{5,4,3,2,1,0:T(8,128)S(1)}, f32[1,2,2,3,16,128]{5,4,3,2,1,0:T(8,128)S(1)}, u32[]{:S(2)}, u32[]{:S(2)}) collective-permute-start(f32[1,2,2,3,16,128]{5,4,3,2,1,0:T(8,128)S(1)} %get-tuple-element.54), channel_id=1, source_target_pairs={{1,2},{2,1},{3,4},{4,3},{5,6},{6,5},{7,8},{8,7},{9,10},{10,9},{11,... | collective-permute-start | bytes 294920 | tf_op jit(solution)/shard_map/ppermute | solution.py:325
  68.3 5.9 %collective-permute-start.10 = (f32[1,2,2,3,16,128]{5,4,3,2,1,0:T(8,128)S(1)}, f32[1,2,2,3,16,128]{5,4,3,2,1,0:T(8,128)S(1)}, u32[]{:S(2)}, u32[]{:S(2)}) collective-permute-start(f32[1,2,2,3,16,128]{5,4,3,2,1,0:T(8,128)S(1)} %get-tuple-element.53), channel_id=1, source_target_pairs={{0,1},{1,0},{2,3},{3,2},{4,5},{5,4},{6,7},{7,6},{8,9},{9,8},{10,11... | collective-permute-start | bytes 294920 | tf_op jit(solution)/shard_map/ppermute | solution.py:325
  74.3 12.2 %collective-permute-start.12 = (f32[1,2,2,13,16,128]{5,4,3,2,1,0:T(8,128)S(1)}, f32[1,2,2,13,16,128]{5,4,3,2,1,0:T(8,128)S(1)}, u32[]{:S(2)}, u32[]{:S(2)}) collective-permute-start(f32[1,2,2,13,16,128]{5,4,3,2,1,0:T(8,128)S(1)} %pad_maximum_fusion.4.ext), channel_id=1, source_target_pairs={{0,16},{16,0},{32,48},{48,32},{64,80},{80,64},{96,112},{112,96},{1... | collective-permute-start | bytes 1277960 | tf_op jit(solution)/shard_map/ppermute | solution.py:325
  74.4 12.1 %collective-permute-start.14 = (f32[1,2,2,8,16,128]{5,4,3,2,1,0:T(8,128)S(1)}, f32[1,2,2,8,16,128]{5,4,3,2,1,0:T(8,128)S(1)}, u32[]{:S(2)}, u32[]{:S(2)}) collective-permute-start(f32[1,2,2,8,16,128]{5,4,3,2,1,0:T(8,128)S(1)} %slice.75), channel_id=1, source_target_pairs={{16,32},{32,16},{48,64},{64,48},{80,96},{96,80},{112,128},{128,112... | collective-permute-start | bytes 786440 | tf_op jit(solution)/shard_map/ppermute | solution.py:325
  79.8 6.6 %collective-permute-start.13 = (f32[1,2,2,5,16,128]{5,4,3,2,1,0:T(8,128)S(1)}, f32[1,2,2,5,16,128]{5,4,3,2,1,0:T(8,128)S(1)}, u32[]{:S(2)}, u32[]{:S(2)}) collective-permute-start(f32[1,2,2,5,16,128]{5,4,3,2,1,0:T(8,128)S(1)} %pad_maximum_fusion.8), channel_id=1, source_target_pairs={{16,32},{32,16},{48,64},{64,48},{80,96},{96,80},{112,128},{128,112... | collective-permute-start | bytes 491528 | tf_op jit(solution)/shard_map/ppermute | solution.py:325

commit v4 on v3

--- a/solution.py
+++ b/solution.py
@@ -27,16 +27,15 @@
 VMEM = pl.BlockSpec(memory_space=pltpu.VMEM)
 SMEM = pl.BlockSpec(memory_space=pltpu.SMEM)
 HBM = pl.BlockSpec(memory_space=pltpu.HBM)
-FULL = (64 << 20) - (1280 << 10)
-
-
-def call(body, out_shape, in_specs, flops=4_000_000, bytes_accessed=4_000_000, scratch=(), vmem=16 << 20):
+
+
+def call(body, out_shape, in_specs, flops=4_000_000, bytes_accessed=4_000_000, scratch=(), vmem=16 << 20, out=VMEM):
     multi = isinstance(out_shape, (list, tuple))
     return pl.pallas_call(
         body,
         out_shape=out_shape,
         in_specs=in_specs,
-        out_specs=[VMEM] * len(out_shape) if multi else VMEM,
+        out_specs=[out] * len(out_shape) if multi else out,
         scratch_shapes=list(scratch),
         compiler_params=pltpu.CompilerParams(vmem_limit_bytes=vmem),
         cost_estimate=pl.CostEstimate(flops=flops, bytes_accessed=bytes_accessed, transcendentals=0),
@@ -47,18 +46,18 @@
     return jax.ShapeDtypeStruct(shape, jnp.float32)
 
 
-def relayout(u_hbm, vel_hbm, fixed_hbm, out_ref, u_ref, vel_ref, fixed_ref, sems):
-    copies = [
-        pltpu.make_async_copy(a, b, sems.at[n])
-        for n, (a, b) in enumerate(
-            ((u_hbm, u_ref), (vel_hbm, vel_ref), (fixed_hbm, fixed_ref))
-        )
-    ]
-    for copy in copies:
-        copy.start()
-    for copy in copies:
-        copy.wait()
+def relayout(u_ref, out_ref):
     comps, count, height, width = u_ref.shape
+    q = width // 128
+    for s in range(count):
+        for j in range(q):
+            for c in range(comps):
+                rows = pl.ds(j, height, stride=q)
+                out_ref.at[0, c, s][rows, :] = u_ref[c, s, :, pl.ds(128 * j, 128)]
+
+
+def relayout_moving(vel_ref, fixed_ref, out_ref):
+    comps, count, height, width = vel_ref.shape
     q = width // 128
     for s in range(count):
         for j in range(q):
@@ -66,8 +65,7 @@
             keep = (1 - fixed_ref[s, :, cols]).astype(jnp.float32)
             for c in range(comps):
                 rows = pl.ds(j, height, stride=q)
-                out_ref.at[0, c, s][rows, :] = u_ref[c, s, :, cols]
-                out_ref.at[1, c, s][rows, :] = vel_ref[c, s, :, cols] * keep
+                out_ref.at[0, c, s][rows, :] = vel_ref[c, s, :, cols] * keep
 
 
 def weights(
@@ -90,7 +88,7 @@
         col_links = (gcol > 0).astype(jnp.float32) + (gcol < width - 1).astype(jnp.float32)
         springs = []
         for i in range(4):
-            dr, dc = offsets_ref[i * count * 2 + s * 2], offsets_ref[i * count * 2 + s * 2 + 1]
+            dr, dc = offsets_ref[s, 0, i], offsets_ref[s, 1, i]
             other = sec_first + s + reaches[i]
             there = (other >= 0) & (other < sections)
             col_ok = (gcol + dc >= 0) & (gcol + dc + 1 <= width - 1) & there
@@ -149,11 +147,10 @@
 
 
 def pull(offsets_ref, source, index, s, i, w, out):
-    vecs, comps, count, tall, q, lanes = source.shape
+    vecs, comps, _, tall, q, lanes = source.shape
     height = tall - UP - DOWN
     lane = lax.broadcasted_iota(jnp.int32, (q, lanes), 1)
-    spot = i * (count * 2) + s * 2
-    dr, dc = offsets_ref[spot], offsets_ref[spot + 1]
+    dr, dc = offsets_ref[s, 0, i], offsets_ref[s, 1, i]
     ahead = dc >= 0
     turn = jnp.where(ahead, q - 1, 1)
     shift0 = lax.rem(lanes - dc, lanes)
@@ -200,12 +197,15 @@
     pull_pair(place[4] == 1, offsets, link, w, out)
 
 
-def far_first_body(place, offsets, anchor, part, link, w, keep, out):
+def far_first_body(place, offsets, before, trans, part, link, w, keep, moving, out):
     _, comps, count, height, q, _ = out.shape
-    out[1:] = part[1:]
+    out[1:] = moving[...]
     for s in range(count):
         for c in range(comps):
-            pulled = anchor_stiff * anchor[s, c]
+            anchor = before[c]
+            for earlier in range(s + 1):
+                anchor = anchor + trans[earlier, c]
+            pulled = anchor_stiff * anchor
             for r in range(height):
                 out[0, c, s, r] = part[0, c, s, r] + keep[s, pl.ds(r * q, q), :] * pulled
     pull_pair(place[4] == 1, offsets, link, w, out)
@@ -228,22 +228,22 @@
     return packed
 
 
-EARLY = [pair for pair in PAIRS if pair[1] < NB - 1]
-LATE = [pair for pair in PAIRS if pair[1] == NB - 1]
-
-
-def basis(start, force, second):
-    return {0: (start, 1), 1: (force, 0), 2: (force, 1), 3: (second, 0), 4: (second, 1)}
-
-
-def near_last_body(place, offsets, ext, chip, w, diag, keep, base, start, force, second, out, early):
-    near_body((False,), place, offsets, ext, chip, w, diag, keep, base, out)
-    early[...] = products(EARLY, basis(start, force, second))
-
-
-def far_last_body(place, offsets, part, link, w, early, start, force, second, out, sums):
+EARLY = [pair for pair in PAIRS if pair[1] < NB - 2]
+LATE = [pair for pair in PAIRS if pair[1] >= NB - 2]
+
+
+def basis(*stages):
+    return {2 * k + n: (stage, 1 - n) for k, stage in enumerate(stages) for n in range(2)}
+
+
+def near_last_body(affine, place, offsets, ext, chip, w, diag, keep, base, force, second, out, early):
+    near_body(affine, place, offsets, ext, chip, w, diag, keep, base, out)
+    early[...] = products(EARLY, basis(force, second))
+
+
+def far_last_body(place, offsets, part, link, w, early, force, second, out, sums):
     far_body(place, offsets, part, link, w, out)
-    late = products(LATE, {**basis(start, force, second), NB - 1: (out, 0)})
+    late = products(LATE, basis(force, second, out))
     sums[...] = jnp.broadcast_to((early[...] + late)[None], sums.shape)
 
 
@@ -278,7 +278,7 @@
     return vel, move, bad
 
 
-def solve_body(parts, out):
+def solve_body(parts, out, lost):
     lanes = parts.shape[-1]
     total = jnp.sum(parts[...], axis=0)
     lane = lax.broadcasted_iota(jnp.int32, (1, lanes), 1)
@@ -288,34 +288,44 @@
     }
     vel, move, bad = coefficients(gram)
     packed = jnp.zeros((1, lanes), jnp.float32)
-    for n, value in enumerate(vel + move + [bad]):
+    for n, value in enumerate(vel + move):
         packed = jnp.where(lane == n, value, packed)
     out[...] = packed
-
-
-def final_body(coef, start, force, second, third, u_ref, v_ref, flat):
-    comps, count, height, width = u_ref.shape
+    lost[...] = (bad > 0.5).astype(jnp.int32)
+
+
+def final_body(coef, start, force, second, third, u_hbm, v_hbm, flat, rows, sems):
+    _, blocks, height, width = rows.shape
     q = width // 128
     vel = [coef[n] for n in range(NB)]
     move = [coef[NB + n] for n in range(NB)]
-    blocks = ((start, 1), (force, 0), (force, 1), (second, 0), (second, 1), (third, 0))
-    for c in range(comps):
-        for s in range(count):
-            for r in range(height):
-                at = pl.ds(r * q, q)
-                vec = [ref[n, c, s, at, :] for ref, n in blocks]
-                u = start[0, c, s, at, :]
-                v = vel[0] * vec[0]
-                u = u + move[0] * vec[0]
-                for n in range(1, NB):
-                    v = v + vel[n] * vec[n]
-                    u = u + move[n] * vec[n]
-                flat[0, at, :] = u
-                flat[1, at, :] = v
-            for j in range(q):
-                at = pl.ds(j, height, stride=q)
-                u_ref[c, s, :, pl.ds(128 * j, 128)] = flat.at[0][at, :]
-                v_ref[c, s, :, pl.ds(128 * j, 128)] = flat.at[1][at, :]
+    order = basis(force, second, third)
+    count = start.shape[2]
+    copies = []
+    for block in range(blocks):
+        c, s = divmod(block, count)
+        for r in range(height):
+            at = pl.ds(r * q, q)
+            vec = [ref[n, c, s, at, :] for ref, n in order.values()]
+            u = start[0, c, s, at, :]
+            v = vel[0] * vec[0]
+            u = u + move[0] * vec[0]
+            for n in range(1, NB):
+                v = v + vel[n] * vec[n]
+                u = u + move[n] * vec[n]
+            flat[block, 0, at, :] = u
+            flat[block, 1, at, :] = v
+        for j in range(q):
+            at = pl.ds(j, height, stride=q)
+            for k in range(2):
+                rows[k, block, :, pl.ds(128 * j, 128)] = flat.at[block, k][at, :]
+        for k, hbm in enumerate((u_hbm, v_hbm)):
+            copies.append(
+                pltpu.make_async_copy(rows.at[k, block], hbm.at[c, s], sems.at[k, block])
+            )
+            copies[-1].start()
+    for copy in copies:
+        copy.wait()
 
 
 def swapped(x, axis, first):
@@ -355,29 +365,19 @@
             lax.axis_index(SEC) % 2,
         ]
     ).astype(jnp.int32)
-    shifts = offsets.reshape(-1)
-
-    start = call(
-        relayout,
-        f32(2, comps, count, height * q, 128),
-        [HBM] * 3,
-        scratch=[
-            pltpu.VMEM(displacement.shape, jnp.float32),
-            pltpu.VMEM(displacement.shape, jnp.float32),
-            pltpu.VMEM(fixed.shape, jnp.int32),
-            pltpu.SemaphoreType.DMA((3,)),
-        ],
-        vmem=FULL,
-    )(displacement, velocity, fixed)
-    by_row = start.reshape(2, comps, count, height, q, 128)
-
-    local = jnp.cumsum(trans, 0)
+    shifts = jnp.transpose(offsets[:, :, 0], (1, 2, 0))
+
+    start = call(relayout, f32(1, comps, count, height * q, 128), [VMEM])(displacement)
+    by_row = start.reshape(1, comps, count, height, q, 128)
+    moving = call(
+        relayout_moving, f32(*start.shape), [VMEM] * 2
+    )(velocity, fixed).reshape(by_row.shape)
+
     group = lax.axis_size(SEC)
-    pieces = lax.all_to_all(
-        jnp.broadcast_to(local[-1][None, None], (group, 1, 2)), SEC, 0, 0, tiled=True
-    )
+    moved = jnp.broadcast_to(jnp.sum(trans, 0)[None, None], (group, 1, 2))
+    pieces = lax.all_to_all(moved, SEC, 0, 0, tiled=True)
     passed = jnp.arange(group) < lax.axis_index(SEC)
-    anchor = local + jnp.sum(jnp.where(passed[:, None], pieces[:, 0], 0.0), 0)[None]
+    before = jnp.sum(jnp.where(passed[:, None], pieces[:, 0], 0.0), 0)
 
     w, diag, keep, base = call(
         weights,
@@ -396,43 +396,56 @@
             lambda *refs: near_body(affine, *refs), f32(*x.shape), [SMEM] * 2 + [VMEM] * 6
         )(place, shifts, ext, chip, w, diag, keep, base)
 
-    ext, chip, link = exchange(by_row, (place, shifts, anchor))
-    part = near(by_row, ext, chip, (True, False))
-    force = call(far_first_body, f32(*part.shape), [SMEM] * 3 + [VMEM] * 4)(
-        place, shifts, anchor, part, link, w, keep
+    ext, chip, link = exchange(by_row, (place, shifts, before))
+    part = near(by_row, ext, chip, (True,))
+    both = f32(2, *part.shape[1:])
+    force = call(far_first_body, both, [SMEM] * 4 + [VMEM] * 5)(
+        place, shifts, before, trans, part, link, w, keep, moving
     )
     ext, chip, link = exchange(force)
     part = near(force, ext, chip, (False, False))
-    second = call(far_body, f32(*part.shape), [SMEM] * 2 + [VMEM] * 3)(place, shifts, part, link, w)
-    ext, chip, link = exchange(second[:1])
+    second = call(far_body, both, [SMEM] * 2 + [VMEM] * 3)(place, shifts, part, link, w)
+    ext, chip, link = exchange(second)
     third, early = call(
-        near_last_body, [f32(*second[:1].shape), f32(1, 128)], [SMEM] * 2 + [VMEM] * 9
-    )(place, shifts, ext, chip, w, diag, keep, base, by_row, force, second)
+        lambda *refs: near_last_body((False, False), *refs),
+        [both, f32(1, 128)],
+        [SMEM] * 2 + [VMEM] * 8,
+    )(place, shifts, ext, chip, w, diag, keep, base, force, second)
     third, part = call(
-        far_last_body, [f32(*third.shape), f32(devices, 1, 128)], [SMEM] * 2 + [VMEM] * 7
-    )(place, shifts, third, link, w, early, by_row, force, second)
+        far_last_body, [both, f32(devices, 1, 128)], [SMEM] * 2 + [VMEM] * 6
+    )(place, shifts, third, link, w, early, force, second)
 
     parts = lax.all_to_all(part, SEC_TILE, 0, 0, tiled=True)
-    coef = call(solve_body, f32(1, 128), [VMEM])(parts)[0]
+    coef, lost = call(
+        solve_body, [f32(1, 128), jax.ShapeDtypeStruct((1, 1), jnp.int32)], [VMEM]
+    )(parts)
+    coef = coef[0]
 
     def measured(coef):
-        basis = (by_row[1], force[0], force[1], second[0], second[1], third[0])
+        stages = (force, second, third)
+        order = [stage[n] for stage in stages for n in (1, 0)]
 
         def norms(x):
-            vec = sum(a * b for a, b in zip(x, basis))
+            vec = sum(a * b for a, b in zip(x, order))
             return lax.psum(jnp.sum(vec * vec), SEC_TILE)
 
         vel, move, _ = coefficients({(0, 0): coef[0] * 0.0}, norms)
         return jnp.concatenate([jnp.stack(vel + move), coef[2 * NB :]])
 
-    coef = lax.cond(coef[2 * NB] > 0.5, measured, lambda coef: coef, coef)
+    coef = lax.cond(lost[0, 0] > 0, measured, lambda coef: coef, coef)
 
     flat = lambda x: x.reshape(*x.shape[:3], height * q, 128)
+    blocks = comps * count
     return call(
         final_body,
         [f32(*displacement.shape)] * 2,
         [SMEM] + [VMEM] * 4,
-        scratch=[pltpu.VMEM((2, height * q, 128), jnp.float32)],
+        scratch=[
+            pltpu.VMEM((blocks, 2, height * q, 128), jnp.float32),
+            pltpu.VMEM((2, blocks, height, width), jnp.float32),
+            pltpu.SemaphoreType.DMA((2, blocks)),
+        ],
+        out=HBM,
     )(coef, start, flat(force), flat(second), flat(third))
 
 

time: 124 us -> 124 us (level)
    pallas_call x6 -> x7, Pallas kernels: 6.73 us -> 6.69 us  [the longest x1 1.98 us: shards(): call(lambda *refs: near_last_body((False, False), *refs), [both, f32(1, 1...]
  transfers between devices with their start and end apart: 16 -> 16, of which waited for: 6 -> 6; matrix products, arithmetic and copies ran while one was open for 1% -> 1% of each run, Pallas kernels for 2% -> 1%
where the time goes in v4:
time: 124 us; the launch traced here: 123 us
  starting transfers between devices  46 us (37%)
  blocking collectives  31.1 us (25%)
  waiting for transfers between devices  28.2 us (23%)
  Pallas kernels  12.6 us (10%)
  local copies, waits for them, and re-layouts  1.91 us (2%)
  between operations  1.86 us (2%)
  other arithmetic  1.43 us (1%)
    ppermute x15, starting transfers between devices, swapped(): return lax.ppermute(x, axis, pairs)  39.2 us
    all_to_all x1, blocking collectives, shards(): parts = lax.all_to_all(part, SEC_TILE, 0, 0, tiled=True)  31.1 us
    ppermute x15, waiting for transfers between devices, swapped(): return lax.ppermute(x, axis, pairs)  28.2 us
    all_to_all x1, starting transfers between devices, shards(): pieces = lax.all_to_all(moved, SEC, 0, 0, tiled=True)  6.82 us
    pallas_call x2, Pallas kernels, near(): call(lambda *refs: near_body(affine, *refs), f32(*x.shape), [SMEM] * 2 +...  2.86 us
  transfers between devices with their start and end apart: 16, of which 6 were waited for; matrix products, arithmetic and copies ran while one was open for 1% of the time, Pallas kernels for 1%

profile of v4, /device:TPU:1, one launch (start us, length us, event | category | flops | bytes accessed | tf_op | source)
XLA Modules:
  0.0 123.1 jit_solution(9261652773714824381)
XLA Ops:
  0.6 0.8 reduce_sum.72
  2.0 6.8 %all-to-all-start = ((f32[16,1,2]{2,1,0:T(1,128)}), f32[16,1,2]{2,1,0:T(1,128)S(1)}, u32[]{:S(2)}, u32[]{:S(2)}) async-start(f32[16,1,2]{2,1,0:T(1,128)} %broadcast_in_dim.20), calls=%async_computation | async-start | bytes 16384 | tf_op jit(solution)/shard_map/all_to_all | solution.py:378
  8.8 0.9 copy-done.2
  9.9 0.7 collective-permute-start.1
  10.6 4.6 %collective-permute-start = (f32[1,2,2,3,16,128]{5,4,3,2,1,0:T(8,128)S(1)}, f32[1,2,2,3,16,128]{5,4,3,2,1,0:T(8,128)S(1)}, u32[]{:S(2)}, u32[]{:S(2)}) collective-permute-start(f32[1,2,2,3,16,128]{5,4,3,2,1,0:T(8,128)S(1)} %get-tuple-element.54), channel_id=1, source_target_pairs={{0,1},{1,0},{2,3},{3,2},{4,5},{5,4},{6,7},{7,6},{8,9},{9,8},{10,11... | collective-permute-start | bytes 294920 | tf_op jit(solution)/shard_map/ppermute | solution.py:335
  15.4 2.6 %collective-permute-done = f32[1,2,2,3,16,128]{5,4,3,2,1,0:T(8,128)S(1)} collective-permute-done((f32[1,2,2,3,16,128]{5,4,3,2,1,0:T(8,128)S(1)}, f32[1,2,2,3,16,128]{5,4,3,2,1,0:T(8,128)S(1)}, u32[]{:S(2)}, u32[]{:S(2)}) %collective-permute-start) | collective-permute-done | bytes 98336 | tf_op jit(solution)/shard_map/ppermute | solution.py:335
  18.0 1.1 collective-permute-start.2
  19.2 3.2 %collective-permute-start.4 = (f32[1,2,2,8,16,128]{5,4,3,2,1,0:T(8,128)S(1)}, f32[1,2,2,8,16,128]{5,4,3,2,1,0:T(8,128)S(1)}, u32[]{:S(2)}, u32[]{:S(2)}) collective-permute-start(f32[1,2,2,8,16,128]{5,4,3,2,1,0:T(8,128)S(1)} %bitcast.173), channel_id=1, source_target_pairs={{16,32},{32,16},{48,64},{64,48},{80,96},{96,80},{112,128},{128,112... | collective-permute-start | bytes 786440 | tf_op jit(solution)/shard_map/ppermute | solution.py:335
  22.4 2.4 %collective-permute-start.3 = (f32[1,2,2,5,16,128]{5,4,3,2,1,0:T(8,128)S(1)}, f32[1,2,2,5,16,128]{5,4,3,2,1,0:T(8,128)S(1)}, u32[]{:S(2)}, u32[]{:S(2)}) collective-permute-start(f32[1,2,2,5,16,128]{5,4,3,2,1,0:T(8,128)S(1)} %pad_maximum_fusion.8), channel_id=1, source_target_pairs={{16,32},{32,16},{48,64},{64,48},{80,96},{96,80},{112,128},{128,112... | collective-permute-start | bytes 491528 | tf_op jit(solution)/shard_map/ppermute | solution.py:335
  24.8 1.4 %shard_map.78 = (f32[2,4,4,128,128]{4,3,2,1,0:T(8,128)S(1)}, f32[2,128,128]{2,1,0:T(8,128)S(1)}, f32[2,128,128]{2,1,0:T(8,128)S(1)}, f32[2,2,128,128]{3,2,1,0:T(8,128)S(1)}) custom-call(s32[5]{0:T(128)S(1)} %stack.51.place_ref.refs_0_.place, s32[2,2,4]{2,1,0:T(2,128)S(1)} %bitcast.175, bf16[2,4,2,8,2048]{4,3,2,1,0:T(8,128)(2,1)S(1)} %copy-done, ...), custom_call_target="tpu_custom_call" | custom-call | flops 4000000 | bytes 4000000 | tf_op jit(solution)/shard_map/pallas_call | solution.py:382
  26.4 2.7 %collective-permute-done.3 = f32[1,2,2,5,16,128]{5,4,3,2,1,0:T(8,128)S(1)} collective-permute-done((f32[1,2,2,5,16,128]{5,4,3,2,1,0:T(8,128)S(1)}, f32[1,2,2,5,16,128]{5,4,3,2,1,0:T(8,128)S(1)}, u32[]{:S(2)}, u32[]{:S(2)}) %collective-permute-start.3) | collective-permute-done | bytes 163872 | tf_op jit(solution)/shard_map/ppermute | solution.py:335
  29.1 1.2 shard_map.79.part
  30.3 0.9 shard_map.81.refs_8_.force
  31.3 0.7 collective-permute-start.6
  32.0 5.8 %collective-permute-start.5 = (f32[2,2,2,3,16,128]{5,4,3,2,1,0:T(8,128)S(1)}, f32[2,2,2,3,16,128]{5,4,3,2,1,0:T(8,128)S(1)}, u32[]{:S(2)}, u32[]{:S(2)}) collective-permute-start(f32[2,2,2,3,16,128]{5,4,3,2,1,0:T(8,128)S(1)} %get-tuple-element.52), channel_id=1, source_target_pairs={{0,1},{1,0},{2,3},{3,2},{4,5},{5,4},{6,7},{7,6},{8,9},{9,8},{10,11... | collective-permute-start | bytes 589832 | tf_op jit(solution)/shard_map/ppermute | solution.py:335
  37.8 3.1 %collective-permute-done.5 = f32[2,2,2,3,16,128]{5,4,3,2,1,0:T(8,128)S(1)} collective-permute-done((f32[2,2,2,3,16,128]{5,4,3,2,1,0:T(8,128)S(1)}, f32[2,2,2,3,16,128]{5,4,3,2,1,0:T(8,128)S(1)}, u32[]{:S(2)}, u32[]{:S(2)}) %collective-permute-start.5) | collective-permute-done | bytes 196640 | tf_op jit(solution)/shard_map/ppermute | solution.py:335
  41.1 5.8 %collective-permute-start.9 = (f32[2,2,2,8,16,128]{5,4,3,2,1,0:T(8,128)S(1)}, f32[2,2,2,8,16,128]{5,4,3,2,1,0:T(8,128)S(1)}, u32[]{:S(2)}, u32[]{:S(2)}) collective-permute-start(f32[2,2,2,8,16,128]{5,4,3,2,1,0:T(8,128)S(1)} %shard_map.81.refs_8_.force), channel_id=1, source_target_pairs={{16,32},{32,16},{48,64},{64,48},{80,96},{96,80},{112,128},{128,112... | collective-permute-start | bytes 1572872 | tf_op jit(solution)/shard_map/ppermute | solution.py:335
  46.9 1.9 %collective-permute-start.8 = (f32[2,2,2,5,16,128]{5,4,3,2,1,0:T(8,128)S(1)}, f32[2,2,2,5,16,128]{5,4,3,2,1,0:T(8,128)S(1)}, u32[]{:S(2)}, u32[]{:S(2)}) collective-permute-start(f32[2,2,2,5,16,128]{5,4,3,2,1,0:T(8,128)S(1)} %pad_maximum_fusion.6), channel_id=1, source_target_pairs={{16,32},{32,16},{48,64},{64,48},{80,96},{96,80},{112,128},{128,112... | collective-permute-start | bytes 983048 | tf_op jit(solution)/shard_map/ppermute | solution.py:335
  48.8 8.4 %collective-permute-done.8 = f32[2,2,2,5,16,128]{5,4,3,2,1,0:T(8,128)S(1)} collective-permute-done((f32[2,2,2,5,16,128]{5,4,3,2,1,0:T(8,128)S(1)}, f32[2,2,2,5,16,128]{5,4,3,2,1,0:T(8,128)S(1)}, u32[]{:S(2)}, u32[]{:S(2)}) %collective-permute-start.8) | collective-permute-done | bytes 327712 | tf_op jit(solution)/shard_map/ppermute | solution.py:335
  57.4 1.7 %shard_map.82.part = f32[2,2,2,8,16,128]{5,4,3,2,1,0:T(8,128)S(1)} custom-call(s32[5]{0:T(128)S(1)} %stack.51.place_ref.refs_0_.place, s32[2,2,4]{2,1,0:T(2,128)S(1)} %bitcast.178, f32[2,2,2,13,16,128]{5,4,3,2,1,0:T(8,128)S(1)} %pad_maximum_fusion.refs_2_, f32[2,2,2,13,16,128]{5,4,3,2,1,0:T(8,128)S(1)} %collective-permute-done.7.refs_3_, ...), custom_call_target="tpu_custom_call" | custom-call | flops 4000000 | bytes 4000000 | tf_op jit(solution)/shard_map/pallas_call | solution.py:395
  59.1 1.1 shard_map.83.refs_9_.second
  60.2 0.7 collective-permute-start.11
  60.9 3.9 %collective-permute-start.10 = (f32[2,2,2,3,16,128]{5,4,3,2,1,0:T(8,128)S(1)}, f32[2,2,2,3,16,128]{5,4,3,2,1,0:T(8,128)S(1)}, u32[]{:S(2)}, u32[]{:S(2)}) collective-permute-start(f32[2,2,2,3,16,128]{5,4,3,2,1,0:T(8,128)S(1)} %get-tuple-element.50), channel_id=1, source_target_pairs={{0,1},{1,0},{2,3},{3,2},{4,5},{5,4},{6,7},{7,6},{8,9},{9,8},{10,11... | collective-permute-start | bytes 589832 | tf_op jit(solution)/shard_map/ppermute | solution.py:335
  64.8 3.1 %collective-permute-done.10 = f32[2,2,2,3,16,128]{5,4,3,2,1,0:T(8,128)S(1)} collective-permute-done((f32[2,2,2,3,16,128]{5,4,3,2,1,0:T(8,128)S(1)}, f32[2,2,2,3,16,128]{5,4,3,2,1,0:T(8,128)S(1)}, u32[]{:S(2)}, u32[]{:S(2)}) %collective-permute-start.10) | collective-permute-done | bytes 196640 | tf_op jit(solution)/shard_map/ppermute | solution.py:335
  68.1 6.4 %collective-permute-start.14 = (f32[2,2,2,8,16,128]{5,4,3,2,1,0:T(8,128)S(1)}, f32[2,2,2,8,16,128]{5,4,3,2,1,0:T(8,128)S(1)}, u32[]{:S(2)}, u32[]{:S(2)}) collective-permute-start(f32[2,2,2,8,16,128]{5,4,3,2,1,0:T(8,128)S(1)} %shard_map.83.refs_9_.second), channel_id=1, source_target_pairs={{16,32},{32,16},{48,64},{64,48},{80,96},{96,80},{112,128},{128,112... | collective-permute-start | bytes 1572872 | tf_op jit(solution)/shard_map/ppermute | solution.py:335
  74.6 1.9 %collective-permute-start.13 = (f32[2,2,2,5,16,128]{5,4,3,2,1,0:T(8,128)S(1)}, f32[2,2,2,5,16,128]{5,4,3,2,1,0:T(8,128)S(1)}, u32[]{:S(2)}, u32[]{:S(2)}) collective-permute-start(f32[2,2,2,5,16,128]{5,4,3,2,1,0:T(8,128)S(1)} %pad_maximum_fusion.7), channel_id=1, source_target_pairs={{16,32},{32,16},{48,64},{64,48},{80,96},{96,80},{112,128},{128,112... | collective-permute-start | bytes 983048 | tf_op jit(solution)/shard_map/ppermute | solution.py:335
  76.5 8.4 %collective-permute-done.13 = f32[2,2,2,5,16,128]{5,4,3,2,1,0:T(8,128)S(1)} collective-permute-done((f32[2,2,2,5,16,128]{5,4,3,2,1,0:T(8,128)S(1)}, f32[2,2,2,5,16,128]{5,4,3,2,1,0:T(8,128)S(1)}, u32[]{:S(2)}, u32[]{:S(2)}) %collective-permute-start.13) | collective-permute-done | bytes 327712 | tf_op jit(solution)/shard_map/ppermute | solution.py:335
  85.0 2.0 %shard_map.84 = (f32[2,2,2,8,16,128]{5,4,3,2,1,0:T(8,128)S(1)}, f32[1,128]{1,0:T(1,128)S(1)}) custom-call(s32[5]{0:T(128)S(1)} %stack.51.place_ref.refs_0_.place, s32[2,2,4]{2,1,0:T(2,128)S(1)} %bitcast.180, f32[2,2,2,13,16,128]{5,4,3,2,1,0:T(8,128)S(1)} %pad_maximum_fusion.2.refs_2_, f32[2,2,2,13,16,128]{5,4,3,2,1,0:T(8,128)S(1)} %collective-permute-done.12.refs_3_, ...), custom_call_target="tpu_custom_call" | custom-call | flops 4000000 | bytes 4000000 | tf_op jit(solution)/shard_map/pallas_call | solution.py:409
  87.0 1.5 %shard_map.85 = (f32[2,2,2,8,16,128]{5,4,3,2,1,0:T(8,128)S(1)}, f32[256,1,128]{2,1,0:T(1,128)S(1)}) custom-call(s32[5]{0:T(128)S(1)} %stack.51.place_ref.refs_0_.place, s32[2,2,4]{2,1,0:T(2,128)S(1)} %bitcast.181, f32[2,2,2,8,16,128]{5,4,3,2,1,0:T(8,128)S(1)} %get-tuple-element.34.part, f32[2,2,2,13,16,128]{5,4,3,2,1,0:T(8,128)S(1)} %pad_maximum_fusion.3.link, ...), custom_call_target="tpu_custom_call" | custom-call | flops 4000000 | bytes 4000000 | tf_op jit(solution)/shard_map/pallas_call | solution.py:414
  88.5 31.1 %all_to_all.10.parts = f32[256,1,128]{2,1,0:T(1,128)S(1)} all-to-all(f32[256,1,128]{2,1,0:T(1,128)S(1)} %get-tuple-element.36), channel_id=1, replica_groups=mesh['sec_0'=2,'sec_1'=4,'sec_2'=2,'tile_0'=2,'tile_1'=8] {'sec_0','sec_..., dimensions={0} | all-to-all | bytes 262144 | tf_op jit(solution)/shard_map/all_to_all | solution.py:418
  119.7 1.0 shard_map.86
  121.3 1.6 %shard_map.87 = (f32[2,2,8,2048]{3,2,1,0:T(8,128)}, f32[2,2,8,2048]{3,2,1,0:T(8,128)}) custom-call(f32[128]{0:T(128)S(1)} %get-tuple-element.56.coef, f32[1,2,2,128,128]{4,3,2,1,0:T(8,128)S(1)} %shard_map.77.start, f32[2,2,2,128,128]{4,3,2,1,0:T(8,128)S(1)} %bitcast.182, f32[2,2,2,128,128]{4,3,2,1,0:T(8,128)S(1)} %bitcast.183, ...), custom_call_target="tpu_custom_call" | custom-call | flops 4000000 | bytes 4000000 | tf_op jit(solution)/shard_map/pallas_call | solution.py:439
  (55 shorter events, 2.0 us)
Async XLA Ops:
  0.6 24.2 %copy-start = (bf16[2,4,2,8,2048]{4,3,2,1,0:T(8,128)(2,1)S(1)}, bf16[2,4,2,8,2048]{4,3,2,1,0:T(8,128)(2,1)}, u32[]{:S(2)}) copy-start(bf16[2,4,2,8,2048]{4,3,2,1,0:T(8,128)(2,1)} %frac_ref.1) | copy-start | bytes 1572868
  0.6 24.2 %copy-start.1 = (s32[2,8,2048]{2,1,0:T(8,128)S(1)}, s32[2,8,2048]{2,1,0:T(8,128)}, u32[]{:S(2)}) copy-start(s32[2,8,2048]{2,1,0:T(8,128)} %fixed_ref.3) | copy-start | bytes 393220
  2.0 13.3 %all-to-all-start = ((f32[16,1,2]{2,1,0:T(1,128)}), f32[16,1,2]{2,1,0:T(1,128)S(1)}, u32[]{:S(2)}, u32[]{:S(2)}) async-start(f32[16,1,2]{2,1,0:T(1,128)} %broadcast_in_dim.20), calls=%async_computation | async-start | bytes 16384 | tf_op jit(solution)/shard_map/all_to_all | solution.py:378
  8.8 0.9 copy-start.2
  9.8 15.0 %copy-start.4 = (s32[4,2,1,2]{0,3,2,1:T(2,128)S(1)}, s32[4,2,1,2]{0,3,2,1:T(2,128)}, u32[]{:S(2)}) copy-start(s32[4,2,1,2]{0,3,2,1:T(2,128)} %param.11) | copy-start | bytes 196
  9.8 16.5 %copy-start.3 = (f32[2,2,8,2048]{3,2,1,0:T(8,128)S(1)}, f32[2,2,8,2048]{3,2,1,0:T(8,128)}, u32[]{:S(2)}) copy-start(f32[2,2,8,2048]{3,2,1,0:T(8,128)} %vel_ref.1) | copy-start | bytes 786436
  9.9 5.5 %collective-permute-start.1 = (f32[1,2,2,3,16,128]{5,4,3,2,1,0:T(8,128)S(1)}, f32[1,2,2,3,16,128]{5,4,3,2,1,0:T(8,128)S(1)}, u32[]{:S(2)}, u32[]{:S(2)}) collective-permute-start(f32[1,2,2,3,16,128]{5,4,3,2,1,0:T(8,128)S(1)} %get-tuple-element.55), channel_id=1, source_target_pairs={{1,2},{2,1},{3,4},{4,3},{5,6},{6,5},{7,8},{8,7},{9,10},{10,9},{11,... | collective-permute-start | bytes 294920 | tf_op jit(solution)/shard_map/ppermute | solution.py:335
  10.6 7.4 %collective-permute-start = (f32[1,2,2,3,16,128]{5,4,3,2,1,0:T(8,128)S(1)}, f32[1,2,2,3,16,128]{5,4,3,2,1,0:T(8,128)S(1)}, u32[]{:S(2)}, u32[]{:S(2)}) collective-permute-start(f32[1,2,2,3,16,128]{5,4,3,2,1,0:T(8,128)S(1)} %get-tuple-element.54), channel_id=1, source_target_pairs={{0,1},{1,0},{2,3},{3,2},{4,5},{5,4},{6,7},{7,6},{8,9},{9,8},{10,11... | collective-permute-start | bytes 294920 | tf_op jit(solution)/shard_map/ppermute | solution.py:335
  18.0 11.1 %collective-permute-start.2 = (f32[1,2,2,13,16,128]{5,4,3,2,1,0:T(8,128)S(1)}, f32[1,2,2,13,16,128]{5,4,3,2,1,0:T(8,128)S(1)}, u32[]{:S(2)}, u32[]{:S(2)}) collective-permute-start(f32[1,2,2,13,16,128]{5,4,3,2,1,0:T(8,128)S(1)} %pad_maximum_fusion.4.refs_2_), channel_id=1, source_target_pairs={{0,16},{16,0},{32,48},{48,32},{64,80},{80,64},{96,112},{112,96},{1... | collective-permute-start | bytes 1277960 | tf_op jit(solution)/shard_map/ppermute | solution.py:335
  19.2 9.9 %collective-permute-start.4 = (f32[1,2,2,8,16,128]{5,4,3,2,1,0:T(8,128)S(1)}, f32[1,2,2,8,16,128]{5,4,3,2,1,0:T(8,128)S(1)}, u32[]{:S(2)}, u32[]{:S(2)}) collective-permute-start(f32[1,2,2,8,16,128]{5,4,3,2,1,0:T(8,128)S(1)} %bitcast.173), channel_id=1, source_target_pairs={{16,32},{32,16},{48,64},{64,48},{80,96},{96,80},{112,128},{128,112... | collective-permute-start | bytes 786440 | tf_op jit(solution)/shard_map/ppermute | solution.py:335
  22.4 6.6 %collective-permute-start.3 = (f32[1,2,2,5,16,128]{5,4,3,2,1,0:T(8,128)S(1)}, f32[1,2,2,5,16,128]{5,4,3,2,1,0:T(8,128)S(1)}, u32[]{:S(2)}, u32[]{:S(2)}) collective-permute-start(f32[1,2,2,5,16,128]{5,4,3,2,1,0:T(8,128)S(1)} %pad_maximum_fusion.8), channel_id=1, source_target_pairs={{16,32},{32,16},{48,64},{64,48},{80,96},{96,80},{112,128},{128,112... | collective-permute-start | bytes 491528 | tf_op jit(solution)/shard_map/ppermute | solution.py:335
  29.1 1.3 %copy-start.5 = (f32[2,2]{1,0:T(2,128)S(1)}, f32[2,2]{1,0:T(2,128)}, u32[]{:S(2)}) copy-start(f32[2,2]{1,0:T(2,128)} %trans.1) | copy-start | bytes 52
  31.3 6.5 %collective-permute-start.6 = (f32[2,2,2,3,16,128]{5,4,3,2,1,0:T(8,128)S(1)}, f32[2,2,2,3,16,128]{5,4,3,2,1,0:T(8,128)S(1)}, u32[]{:S(2)}, u32[]{:S(2)}) collective-permute-start(f32[2,2,2,3,16,128]{5,4,3,2,1,0:T(8,128)S(1)} %get-tuple-element.53), channel_id=1, source_target_pairs={{1,2},{2,1},{3,4},{4,3},{5,6},{6,5},{7,8},{8,7},{9,10},{10,9},{11,... | collective-permute-start | bytes 589832 | tf_op jit(solution)/shard_map/ppermute | solution.py:335
  32.0 8.9 %collective-permute-start.5 = (f32[2,2,2,3,16,128]{5,4,3,2,1,0:T(8,128)S(1)}, f32[2,2,2,3,16,128]{5,4,3,2,1,0:T(8,128)S(1)}, u32[]{:S(2)}, u32[]{:S(2)}) collective-permute-start(f32[2,2,2,3,16,128]{5,4,3,2,1,0:T(8,128)S(1)} %get-tuple-element.52), channel_id=1, source_target_pairs={{0,1},{1,0},{2,3},{3,2},{4,5},{5,4},{6,7},{7,6},{8,9},{9,8},{10,11... | collective-permute-start | bytes 589832 | tf_op jit(solution)/shard_map/ppermute | solution.py:335
  41.0 16.4 %collective-permute-start.7 = (f32[2,2,2,13,16,128]{5,4,3,2,1,0:T(8,128)S(1)}, f32[2,2,2,13,16,128]{5,4,3,2,1,0:T(8,128)S(1)}, u32[]{:S(2)}, u32[]{:S(2)}) collective-permute-start(f32[2,2,2,13,16,128]{5,4,3,2,1,0:T(8,128)S(1)} %pad_maximum_fusion.refs_2_), channel_id=1, source_target_pairs={{0,16},{16,0},{32,48},{48,32},{64,80},{80,64},{96,112},{112,96},{1... | collective-permute-start | bytes 2555912 | tf_op jit(solution)/shard_map/ppermute | solution.py:335
  41.1 16.2 %collective-permute-start.9 = (f32[2,2,2,8,16,128]{5,4,3,2,1,0:T(8,128)S(1)}, f32[2,2,2,8,16,128]{5,4,3,2,1,0:T(8,128)S(1)}, u32[]{:S(2)}, u32[]{:S(2)}) collective-permute-start(f32[2,2,2,8,16,128]{5,4,3,2,1,0:T(8,128)S(1)} %shard_map.81.refs_8_.force), channel_id=1, source_target_pairs={{16,32},{32,16},{48,64},{64,48},{80,96},{96,80},{112,128},{128,112... | collective-permute-start | bytes 1572872 | tf_op jit(solution)/shard_map/ppermute | solution.py:335
  46.9 10.3 %collective-permute-start.8 = (f32[2,2,2,5,16,128]{5,4,3,2,1,0:T(8,128)S(1)}, f32[2,2,2,5,16,128]{5,4,3,2,1,0:T(8,128)S(1)}, u32[]{:S(2)}, u32[]{:S(2)}) collective-permute-start(f32[2,2,2,5,16,128]{5,4,3,2,1,0:T(8,128)S(1)} %pad_maximum_fusion.6), channel_id=1, source_target_pairs={{16,32},{32,16},{48,64},{64,48},{80,96},{96,80},{112,128},{128,112... | collective-permute-start | bytes 983048 | tf_op jit(solution)/shard_map/ppermute | solution.py:335
  60.2 4.6 %collective-permute-start.11 = (f32[2,2,2,3,16,128]{5,4,3,2,1,0:T(8,128)S(1)}, f32[2,2,2,3,16,128]{5,4,3,2,1,0:T(8,128)S(1)}, u32[]{:S(2)}, u32[]{:S(2)}) collective-permute-start(f32[2,2,2,3,16,128]{5,4,3,2,1,0:T(8,128)S(1)} %get-tuple-element.51), channel_id=1, source_target_pairs={{1,2},{2,1},{3,4},{4,3},{5,6},{6,5},{7,8},{8,7},{9,10},{10,9},{11,... | collective-permute-start | bytes 589832 | tf_op jit(solution)/shard_map/ppermute | solution.py:335
  60.9 6.9 %collective-permute-start.10 = (f32[2,2,2,3,16,128]{5,4,3,2,1,0:T(8,128)S(1)}, f32[2,2,2,3,16,128]{5,4,3,2,1,0:T(8,128)S(1)}, u32[]{:S(2)}, u32[]{:S(2)}) collective-permute-start(f32[2,2,2,3,16,128]{5,4,3,2,1,0:T(8,128)S(1)} %get-tuple-element.50), channel_id=1, source_target_pairs={{0,1},{1,0},{2,3},{3,2},{4,5},{5,4},{6,7},{7,6},{8,9},{9,8},{10,11... | collective-permute-start | bytes 589832 | tf_op jit(solution)/shard_map/ppermute | solution.py:335
  68.0 17.0 %collective-permute-start.12 = (f32[2,2,2,13,16,128]{5,4,3,2,1,0:T(8,128)S(1)}, f32[2,2,2,13,16,128]{5,4,3,2,1,0:T(8,128)S(1)}, u32[]{:S(2)}, u32[]{:S(2)}) collective-permute-start(f32[2,2,2,13,16,128]{5,4,3,2,1,0:T(8,128)S(1)} %pad_maximum_fusion.2.refs_2_), channel_id=1, source_target_pairs={{0,16},{16,0},{32,48},{48,32},{64,80},{80,64},{96,112},{112,96},{1... | collective-permute-start | bytes 2555912 | tf_op jit(solution)/shard_map/ppermute | solution.py:335
  68.1 16.8 %collective-permute-start.14 = (f32[2,2,2,8,16,128]{5,4,3,2,1,0:T(8,128)S(1)}, f32[2,2,2,8,16,128]{5,4,3,2,1,0:T(8,128)S(1)}, u32[]{:S(2)}, u32[]{:S(2)}) collective-permute-start(f32[2,2,2,8,16,128]{5,4,3,2,1,0:T(8,128)S(1)} %shard_map.83.refs_9_.second), channel_id=1, source_target_pairs={{16,32},{32,16},{48,64},{64,48},{80,96},{96,80},{112,128},{128,112... | collective-permute-start | bytes 1572872 | tf_op jit(solution)/shard_map/ppermute | solution.py:335
  74.6 10.3 %collective-permute-start.13 = (f32[2,2,2,5,16,128]{5,4,3,2,1,0:T(8,128)S(1)}, f32[2,2,2,5,16,128]{5,4,3,2,1,0:T(8,128)S(1)}, u32[]{:S(2)}, u32[]{:S(2)}) collective-permute-start(f32[2,2,2,5,16,128]{5,4,3,2,1,0:T(8,128)S(1)} %pad_maximum_fusion.7), channel_id=1, source_target_pairs={{16,32},{32,16},{48,64},{64,48},{80,96},{96,80},{112,128},{128,112... | collective-permute-start | bytes 983048 | tf_op jit(solution)/shard_map/ppermute | solution.py:335

commit v5 on v4

--- a/solution.py
+++ b/solution.py
@@ -46,8 +46,16 @@
     return jax.ShapeDtypeStruct(shape, jnp.float32)
 
 
-def relayout(u_ref, out_ref):
+def relayout(trans_ref, u_ref, out_ref, moved_ref):
     comps, count, height, width = u_ref.shape
+    comp = lax.broadcasted_iota(jnp.int32, moved_ref.shape, 2)
+    moved = []
+    for c in range(comps):
+        total = trans_ref[0, c]
+        for s in range(1, count):
+            total = total + trans_ref[s, c]
+        moved.append(total)
+    moved_ref[...] = jnp.where(comp == 0, moved[0], moved[1])
     q = width // 128
     for s in range(count):
         for j in range(q):
@@ -280,7 +288,7 @@
 
 def solve_body(parts, out, lost):
     lanes = parts.shape[-1]
-    total = jnp.sum(parts[...], axis=0)
+    total = jnp.sum(jnp.sum(parts[...], axis=0), axis=0, keepdims=True)
     lane = lax.broadcasted_iota(jnp.int32, (1, lanes), 1)
     gram = {
         pair: jnp.sum(jnp.where(lane == n, total, 0.0), axis=1, keepdims=True)
@@ -367,14 +375,15 @@
     ).astype(jnp.int32)
     shifts = jnp.transpose(offsets[:, :, 0], (1, 2, 0))
 
-    start = call(relayout, f32(1, comps, count, height * q, 128), [VMEM])(displacement)
+    group = lax.axis_size(SEC)
+    start, moved = call(
+        relayout, [f32(1, comps, count, height * q, 128), f32(group, 1, comps)], [SMEM, VMEM]
+    )(trans, displacement)
     by_row = start.reshape(1, comps, count, height, q, 128)
     moving = call(
         relayout_moving, f32(*start.shape), [VMEM] * 2
     )(velocity, fixed).reshape(by_row.shape)
 
-    group = lax.axis_size(SEC)
-    moved = jnp.broadcast_to(jnp.sum(trans, 0)[None, None], (group, 1, 2))
     pieces = lax.all_to_all(moved, SEC, 0, 0, tiled=True)
     passed = jnp.arange(group) < lax.axis_index(SEC)
     before = jnp.sum(jnp.where(passed[:, None], pieces[:, 0], 0.0), 0)
@@ -412,13 +421,13 @@
         [SMEM] * 2 + [VMEM] * 8,
     )(place, shifts, ext, chip, w, diag, keep, base, force, second)
     third, part = call(
-        far_last_body, [both, f32(devices, 1, 128)], [SMEM] * 2 + [VMEM] * 6
+        far_last_body, [both, f32(devices // 8, 8, 128)], [SMEM] * 2 + [VMEM] * 6
     )(place, shifts, third, link, w, early, force, second)
 
-    parts = lax.all_to_all(part, SEC_TILE, 0, 0, tiled=True)
+    parts = lax.all_to_all(part.reshape(devices, 1, 128), SEC_TILE, 0, 0, tiled=True)
     coef, lost = call(
         solve_body, [f32(1, 128), jax.ShapeDtypeStruct((1, 1), jnp.int32)], [VMEM]
-    )(parts)
+    )(parts.reshape(part.shape))
     coef = coef[0]
 
     def measured(coef):

time: 124 us -> 124 us (level)
  transfers between devices with their start and end apart: 16 -> 16, of which waited for: 6 -> 7; matrix products, arithmetic and copies ran while one was open for 1% -> 0% of each run, Pallas kernels for 1% -> 1%
where the time goes in v5:
time: 124 us; the launch traced here: 123 us
  starting transfers between devices  46 us (37%)
  blocking collectives  31.1 us (25%)
  waiting for transfers between devices  28.2 us (23%)
  Pallas kernels  13.5 us (11%)
  local copies, waits for them, and re-layouts  2.04 us (2%)
  between operations  1.85 us (1%)
    ppermute x15, starting transfers between devices, swapped(): return lax.ppermute(x, axis, pairs)  39.2 us
    all_to_all x1, blocking collectives, shards(): lax.all_to_all(part.reshape(devices, 1, 128), SEC_TILE, 0, 0, tiled=True)  31.1 us
    ppermute x15, waiting for transfers between devices, swapped(): return lax.ppermute(x, axis, pairs)  28.1 us
    all_to_all x1, starting transfers between devices, shards(): pieces = lax.all_to_all(moved, SEC, 0, 0, tiled=True)  6.82 us
    pallas_call x2, Pallas kernels, near(): call(lambda *refs: near_body(affine, *refs), f32(*x.shape), [SMEM] * 2 +...  2.86 us
  transfers between devices with their start and end apart: 16, of which 7 were waited for; matrix products, arithmetic and copies ran while one was open for 0% of the time, Pallas kernels for 1%

profile of v5, /device:TPU:1, one launch (start us, length us, event | category | flops | bytes accessed | tf_op | source)
XLA Modules:
  0.0 123.3 jit_solution(7984817997626410047)
XLA Ops:
  0.7 1.0 copy-done.2
  1.7 0.7 copy-done.5
  2.3 1.2 %shard_map.77 = (f32[1,2,2,128,128]{4,3,2,1,0:T(8,128)S(1)}, f32[16,1,2]{2,1,0:T(1,128)}) custom-call(f32[2,2]{1,0:T(2,128)S(1)} %copy-done.5, f32[2,2,8,2048]{3,2,1,0:T(8,128)S(1)} %copy-done.2), custom_call_target="tpu_custom_call" | custom-call | flops 4000000 | bytes 4000000 | tf_op jit(solution)/shard_map/pallas_call | solution.py:379
  3.6 6.8 %all-to-all-start = ((f32[16,1,2]{2,1,0:T(1,128)}), f32[16,1,2]{2,1,0:T(1,128)S(1)}, u32[]{:S(2)}, u32[]{:S(2)}) async-start(f32[16,1,2]{2,1,0:T(1,128)} %get-tuple-element.31), calls=%async_computation | async-start | bytes 16384 | tf_op jit(solution)/shard_map/all_to_all | solution.py:387
  11.1 4.6 %collective-permute-start = (f32[1,2,2,3,16,128]{5,4,3,2,1,0:T(8,128)S(1)}, f32[1,2,2,3,16,128]{5,4,3,2,1,0:T(8,128)S(1)}, u32[]{:S(2)}, u32[]{:S(2)}) collective-permute-start(f32[1,2,2,3,16,128]{5,4,3,2,1,0:T(8,128)S(1)} %get-tuple-element.58), channel_id=1, source_target_pairs={{0,1},{1,0},{2,3},{3,2},{4,5},{5,4},{6,7},{7,6},{8,9},{9,8},{10,11... | collective-permute-start | bytes 294920 | tf_op jit(solution)/shard_map/ppermute | solution.py:343
  15.9 2.5 %collective-permute-done = f32[1,2,2,3,16,128]{5,4,3,2,1,0:T(8,128)S(1)} collective-permute-done((f32[1,2,2,3,16,128]{5,4,3,2,1,0:T(8,128)S(1)}, f32[1,2,2,3,16,128]{5,4,3,2,1,0:T(8,128)S(1)}, u32[]{:S(2)}, u32[]{:S(2)}) %collective-permute-start) | collective-permute-done | bytes 98336 | tf_op jit(solution)/shard_map/ppermute | solution.py:343
  18.5 1.1 collective-permute-start.2
  19.7 3.2 %collective-permute-start.4 = (f32[1,2,2,8,16,128]{5,4,3,2,1,0:T(8,128)S(1)}, f32[1,2,2,8,16,128]{5,4,3,2,1,0:T(8,128)S(1)}, u32[]{:S(2)}, u32[]{:S(2)}) collective-permute-start(f32[1,2,2,8,16,128]{5,4,3,2,1,0:T(8,128)S(1)} %bitcast.177), channel_id=1, source_target_pairs={{16,32},{32,16},{48,64},{64,48},{80,96},{96,80},{112,128},{128,112... | collective-permute-start | bytes 786440 | tf_op jit(solution)/shard_map/ppermute | solution.py:343
  22.9 2.4 %collective-permute-start.3 = (f32[1,2,2,5,16,128]{5,4,3,2,1,0:T(8,128)S(1)}, f32[1,2,2,5,16,128]{5,4,3,2,1,0:T(8,128)S(1)}, u32[]{:S(2)}, u32[]{:S(2)}) collective-permute-start(f32[1,2,2,5,16,128]{5,4,3,2,1,0:T(8,128)S(1)} %pad_maximum_fusion.8), channel_id=1, source_target_pairs={{16,32},{32,16},{48,64},{64,48},{80,96},{96,80},{112,128},{128,112... | collective-permute-start | bytes 491528 | tf_op jit(solution)/shard_map/ppermute | solution.py:343
  25.3 1.4 %shard_map.78 = (f32[2,4,4,128,128]{4,3,2,1,0:T(8,128)S(1)}, f32[2,128,128]{2,1,0:T(8,128)S(1)}, f32[2,128,128]{2,1,0:T(8,128)S(1)}, f32[2,2,128,128]{3,2,1,0:T(8,128)S(1)}) custom-call(s32[5]{0:T(128)S(1)} %stack.51.place_ref.refs_0_.place, s32[2,2,4]{2,1,0:T(2,128)S(1)} %bitcast.181, bf16[2,4,2,8,2048]{4,3,2,1,0:T(8,128)(2,1)S(1)} %copy-done, ...), custom_call_target="tpu_custom_call" | custom-call | flops 4000000 | bytes 4000000 | tf_op jit(solution)/shard_map/pallas_call | solution.py:391
  26.9 2.7 %collective-permute-done.3 = f32[1,2,2,5,16,128]{5,4,3,2,1,0:T(8,128)S(1)} collective-permute-done((f32[1,2,2,5,16,128]{5,4,3,2,1,0:T(8,128)S(1)}, f32[1,2,2,5,16,128]{5,4,3,2,1,0:T(8,128)S(1)}, u32[]{:S(2)}, u32[]{:S(2)}) %collective-permute-start.3) | collective-permute-done | bytes 163872 | tf_op jit(solution)/shard_map/ppermute | solution.py:343
  29.6 1.2 shard_map.79.part
  30.8 0.9 shard_map.81.refs_8_.force
  31.8 0.7 collective-permute-start.6
  32.5 5.8 %collective-permute-start.5 = (f32[2,2,2,3,16,128]{5,4,3,2,1,0:T(8,128)S(1)}, f32[2,2,2,3,16,128]{5,4,3,2,1,0:T(8,128)S(1)}, u32[]{:S(2)}, u32[]{:S(2)}) collective-permute-start(f32[2,2,2,3,16,128]{5,4,3,2,1,0:T(8,128)S(1)} %get-tuple-element.56), channel_id=1, source_target_pairs={{0,1},{1,0},{2,3},{3,2},{4,5},{5,4},{6,7},{7,6},{8,9},{9,8},{10,11... | collective-permute-start | bytes 589832 | tf_op jit(solution)/shard_map/ppermute | solution.py:343
  38.3 3.1 %collective-permute-done.5 = f32[2,2,2,3,16,128]{5,4,3,2,1,0:T(8,128)S(1)} collective-permute-done((f32[2,2,2,3,16,128]{5,4,3,2,1,0:T(8,128)S(1)}, f32[2,2,2,3,16,128]{5,4,3,2,1,0:T(8,128)S(1)}, u32[]{:S(2)}, u32[]{:S(2)}) %collective-permute-start.5) | collective-permute-done | bytes 196640 | tf_op jit(solution)/shard_map/ppermute | solution.py:343
  41.6 5.8 %collective-permute-start.9 = (f32[2,2,2,8,16,128]{5,4,3,2,1,0:T(8,128)S(1)}, f32[2,2,2,8,16,128]{5,4,3,2,1,0:T(8,128)S(1)}, u32[]{:S(2)}, u32[]{:S(2)}) collective-permute-start(f32[2,2,2,8,16,128]{5,4,3,2,1,0:T(8,128)S(1)} %shard_map.81.refs_8_.force), channel_id=1, source_target_pairs={{16,32},{32,16},{48,64},{64,48},{80,96},{96,80},{112,128},{128,112... | collective-permute-start | bytes 1572872 | tf_op jit(solution)/shard_map/ppermute | solution.py:343
  47.4 1.9 %collective-permute-start.8 = (f32[2,2,2,5,16,128]{5,4,3,2,1,0:T(8,128)S(1)}, f32[2,2,2,5,16,128]{5,4,3,2,1,0:T(8,128)S(1)}, u32[]{:S(2)}, u32[]{:S(2)}) collective-permute-start(f32[2,2,2,5,16,128]{5,4,3,2,1,0:T(8,128)S(1)} %pad_maximum_fusion.6), channel_id=1, source_target_pairs={{16,32},{32,16},{48,64},{64,48},{80,96},{96,80},{112,128},{128,112... | collective-permute-start | bytes 983048 | tf_op jit(solution)/shard_map/ppermute | solution.py:343
  49.3 8.4 %collective-permute-done.8 = f32[2,2,2,5,16,128]{5,4,3,2,1,0:T(8,128)S(1)} collective-permute-done((f32[2,2,2,5,16,128]{5,4,3,2,1,0:T(8,128)S(1)}, f32[2,2,2,5,16,128]{5,4,3,2,1,0:T(8,128)S(1)}, u32[]{:S(2)}, u32[]{:S(2)}) %collective-permute-start.8) | collective-permute-done | bytes 327712 | tf_op jit(solution)/shard_map/ppermute | solution.py:343
  57.9 1.7 %shard_map.82.part = f32[2,2,2,8,16,128]{5,4,3,2,1,0:T(8,128)S(1)} custom-call(s32[5]{0:T(128)S(1)} %stack.51.place_ref.refs_0_.place, s32[2,2,4]{2,1,0:T(2,128)S(1)} %bitcast.184, f32[2,2,2,13,16,128]{5,4,3,2,1,0:T(8,128)S(1)} %pad_maximum_fusion.refs_2_, f32[2,2,2,13,16,128]{5,4,3,2,1,0:T(8,128)S(1)} %collective-permute-done.7.refs_3_, ...), custom_call_target="tpu_custom_call" | custom-call | flops 4000000 | bytes 4000000 | tf_op jit(solution)/shard_map/pallas_call | solution.py:404
  59.6 1.1 shard_map.83.refs_9_.second
  60.7 0.7 collective-permute-start.11
  61.4 3.9 %collective-permute-start.10 = (f32[2,2,2,3,16,128]{5,4,3,2,1,0:T(8,128)S(1)}, f32[2,2,2,3,16,128]{5,4,3,2,1,0:T(8,128)S(1)}, u32[]{:S(2)}, u32[]{:S(2)}) collective-permute-start(f32[2,2,2,3,16,128]{5,4,3,2,1,0:T(8,128)S(1)} %get-tuple-element.54), channel_id=1, source_target_pairs={{0,1},{1,0},{2,3},{3,2},{4,5},{5,4},{6,7},{7,6},{8,9},{9,8},{10,11... | collective-permute-start | bytes 589832 | tf_op jit(solution)/shard_map/ppermute | solution.py:343
  65.3 3.1 %collective-permute-done.10 = f32[2,2,2,3,16,128]{5,4,3,2,1,0:T(8,128)S(1)} collective-permute-done((f32[2,2,2,3,16,128]{5,4,3,2,1,0:T(8,128)S(1)}, f32[2,2,2,3,16,128]{5,4,3,2,1,0:T(8,128)S(1)}, u32[]{:S(2)}, u32[]{:S(2)}) %collective-permute-start.10) | collective-permute-done | bytes 196640 | tf_op jit(solution)/shard_map/ppermute | solution.py:343
  68.6 6.4 %collective-permute-start.14 = (f32[2,2,2,8,16,128]{5,4,3,2,1,0:T(8,128)S(1)}, f32[2,2,2,8,16,128]{5,4,3,2,1,0:T(8,128)S(1)}, u32[]{:S(2)}, u32[]{:S(2)}) collective-permute-start(f32[2,2,2,8,16,128]{5,4,3,2,1,0:T(8,128)S(1)} %shard_map.83.refs_9_.second), channel_id=1, source_target_pairs={{16,32},{32,16},{48,64},{64,48},{80,96},{96,80},{112,128},{128,112... | collective-permute-start | bytes 1572872 | tf_op jit(solution)/shard_map/ppermute | solution.py:343
  75.1 1.9 %collective-permute-start.13 = (f32[2,2,2,5,16,128]{5,4,3,2,1,0:T(8,128)S(1)}, f32[2,2,2,5,16,128]{5,4,3,2,1,0:T(8,128)S(1)}, u32[]{:S(2)}, u32[]{:S(2)}) collective-permute-start(f32[2,2,2,5,16,128]{5,4,3,2,1,0:T(8,128)S(1)} %pad_maximum_fusion.7), channel_id=1, source_target_pairs={{16,32},{32,16},{48,64},{64,48},{80,96},{96,80},{112,128},{128,112... | collective-permute-start | bytes 983048 | tf_op jit(solution)/shard_map/ppermute | solution.py:343
  77.0 8.4 %collective-permute-done.13 = f32[2,2,2,5,16,128]{5,4,3,2,1,0:T(8,128)S(1)} collective-permute-done((f32[2,2,2,5,16,128]{5,4,3,2,1,0:T(8,128)S(1)}, f32[2,2,2,5,16,128]{5,4,3,2,1,0:T(8,128)S(1)}, u32[]{:S(2)}, u32[]{:S(2)}) %collective-permute-start.13) | collective-permute-done | bytes 327712 | tf_op jit(solution)/shard_map/ppermute | solution.py:343
  85.6 2.0 %shard_map.84 = (f32[2,2,2,8,16,128]{5,4,3,2,1,0:T(8,128)S(1)}, f32[1,128]{1,0:T(1,128)S(1)}) custom-call(s32[5]{0:T(128)S(1)} %stack.51.place_ref.refs_0_.place, s32[2,2,4]{2,1,0:T(2,128)S(1)} %bitcast.186, f32[2,2,2,13,16,128]{5,4,3,2,1,0:T(8,128)S(1)} %pad_maximum_fusion.2.refs_2_, f32[2,2,2,13,16,128]{5,4,3,2,1,0:T(8,128)S(1)} %collective-permute-done.12.refs_3_, ...), custom_call_target="tpu_custom_call" | custom-call | flops 4000000 | bytes 4000000 | tf_op jit(solution)/shard_map/pallas_call | solution.py:418
  87.5 1.5 %shard_map.85 = (f32[2,2,2,8,16,128]{5,4,3,2,1,0:T(8,128)S(1)}, f32[32,8,128]{2,1,0:T(8,128)S(1)}) custom-call(s32[5]{0:T(128)S(1)} %stack.51.place_ref.refs_0_.place, s32[2,2,4]{2,1,0:T(2,128)S(1)} %bitcast.187, f32[2,2,2,8,16,128]{5,4,3,2,1,0:T(8,128)S(1)} %get-tuple-element.38.part, f32[2,2,2,13,16,128]{5,4,3,2,1,0:T(8,128)S(1)} %pad_maximum_fusion.3.link, ...), custom_call_target="tpu_custom_call" | custom-call | flops 4000000 | bytes 4000000 | tf_op jit(solution)/shard_map/pallas_call | solution.py:423
  89.0 31.1 %all_to_all.10 = f32[256,1,128]{2,1,0:T(1,128)S(1)} all-to-all(f32[256,1,128]{2,1,0:T(1,128)S(1)} %bitcast.180), channel_id=1, replica_groups=mesh['sec_0'=2,'sec_1'=4,'sec_2'=2,'tile_0'=2,'tile_1'=8] {'sec_0','sec_..., dimensions={0} | all-to-all | bytes 262144 | tf_op jit(solution)/shard_map/all_to_all | solution.py:427
  120.1 0.8 shard_map.86
  121.5 1.6 %shard_map.87 = (f32[2,2,8,2048]{3,2,1,0:T(8,128)}, f32[2,2,8,2048]{3,2,1,0:T(8,128)}) custom-call(f32[128]{0:T(128)S(1)} %get-tuple-element.60.coef, f32[1,2,2,128,128]{4,3,2,1,0:T(8,128)S(1)} %get-tuple-element.32.start, f32[2,2,2,128,128]{4,3,2,1,0:T(8,128)S(1)} %bitcast.188, f32[2,2,2,128,128]{4,3,2,1,0:T(8,128)S(1)} %bitcast.189, ...), custom_call_target="tpu_custom_call" | custom-call | flops 4000000 | bytes 4000000 | tf_op jit(solution)/shard_map/pallas_call | solution.py:448
  (55 shorter events, 2.0 us)
Async XLA Ops:
  0.6 24.7 %copy-start = (bf16[2,4,2,8,2048]{4,3,2,1,0:T(8,128)(2,1)S(1)}, bf16[2,4,2,8,2048]{4,3,2,1,0:T(8,128)(2,1)}, u32[]{:S(2)}) copy-start(bf16[2,4,2,8,2048]{4,3,2,1,0:T(8,128)(2,1)} %frac_ref.1) | copy-start | bytes 1572868
  0.6 24.7 %copy-start.1 = (s32[2,8,2048]{2,1,0:T(8,128)S(1)}, s32[2,8,2048]{2,1,0:T(8,128)}, u32[]{:S(2)}) copy-start(s32[2,8,2048]{2,1,0:T(8,128)} %fixed_ref.3) | copy-start | bytes 393220
  0.7 1.0 copy-start.2
  1.7 0.7 copy-start.5
  2.3 23.0 %copy-start.4 = (s32[4,2,1,2]{0,3,2,1:T(2,128)S(1)}, s32[4,2,1,2]{0,3,2,1:T(2,128)}, u32[]{:S(2)}) copy-start(s32[4,2,1,2]{0,3,2,1:T(2,128)} %param.11) | copy-start | bytes 196
  2.3 24.4 %copy-start.3 = (f32[2,2,8,2048]{3,2,1,0:T(8,128)S(1)}, f32[2,2,8,2048]{3,2,1,0:T(8,128)}, u32[]{:S(2)}) copy-start(f32[2,2,8,2048]{3,2,1,0:T(8,128)} %vel_ref.1) | copy-start | bytes 786436
  3.6 12.3 %all-to-all-start = ((f32[16,1,2]{2,1,0:T(1,128)}), f32[16,1,2]{2,1,0:T(1,128)S(1)}, u32[]{:S(2)}, u32[]{:S(2)}) async-start(f32[16,1,2]{2,1,0:T(1,128)} %get-tuple-element.31), calls=%async_computation | async-start | bytes 16384 | tf_op jit(solution)/shard_map/all_to_all | solution.py:387
  10.4 5.5 %collective-permute-start.1 = (f32[1,2,2,3,16,128]{5,4,3,2,1,0:T(8,128)S(1)}, f32[1,2,2,3,16,128]{5,4,3,2,1,0:T(8,128)S(1)}, u32[]{:S(2)}, u32[]{:S(2)}) collective-permute-start(f32[1,2,2,3,16,128]{5,4,3,2,1,0:T(8,128)S(1)} %get-tuple-element.59), channel_id=1, source_target_pairs={{1,2},{2,1},{3,4},{4,3},{5,6},{6,5},{7,8},{8,7},{9,10},{10,9},{11,... | collective-permute-start | bytes 294920 | tf_op jit(solution)/shard_map/ppermute | solution.py:343
  11.1 7.4 %collective-permute-start = (f32[1,2,2,3,16,128]{5,4,3,2,1,0:T(8,128)S(1)}, f32[1,2,2,3,16,128]{5,4,3,2,1,0:T(8,128)S(1)}, u32[]{:S(2)}, u32[]{:S(2)}) collective-permute-start(f32[1,2,2,3,16,128]{5,4,3,2,1,0:T(8,128)S(1)} %get-tuple-element.58), channel_id=1, source_target_pairs={{0,1},{1,0},{2,3},{3,2},{4,5},{5,4},{6,7},{7,6},{8,9},{9,8},{10,11... | collective-permute-start | bytes 294920 | tf_op jit(solution)/shard_map/ppermute | solution.py:343
  18.5 11.1 %collective-permute-start.2 = (f32[1,2,2,13,16,128]{5,4,3,2,1,0:T(8,128)S(1)}, f32[1,2,2,13,16,128]{5,4,3,2,1,0:T(8,128)S(1)}, u32[]{:S(2)}, u32[]{:S(2)}) collective-permute-start(f32[1,2,2,13,16,128]{5,4,3,2,1,0:T(8,128)S(1)} %pad_maximum_fusion.4.refs_2_), channel_id=1, source_target_pairs={{0,16},{16,0},{32,48},{48,32},{64,80},{80,64},{96,112},{112,96},{1... | collective-permute-start | bytes 1277960 | tf_op jit(solution)/shard_map/ppermute | solution.py:343
  19.7 9.9 %collective-permute-start.4 = (f32[1,2,2,8,16,128]{5,4,3,2,1,0:T(8,128)S(1)}, f32[1,2,2,8,16,128]{5,4,3,2,1,0:T(8,128)S(1)}, u32[]{:S(2)}, u32[]{:S(2)}) collective-permute-start(f32[1,2,2,8,16,128]{5,4,3,2,1,0:T(8,128)S(1)} %bitcast.177), channel_id=1, source_target_pairs={{16,32},{32,16},{48,64},{64,48},{80,96},{96,80},{112,128},{128,112... | collective-permute-start | bytes 786440 | tf_op jit(solution)/shard_map/ppermute | solution.py:343
  22.9 6.6 %collective-permute-start.3 = (f32[1,2,2,5,16,128]{5,4,3,2,1,0:T(8,128)S(1)}, f32[1,2,2,5,16,128]{5,4,3,2,1,0:T(8,128)S(1)}, u32[]{:S(2)}, u32[]{:S(2)}) collective-permute-start(f32[1,2,2,5,16,128]{5,4,3,2,1,0:T(8,128)S(1)} %pad_maximum_fusion.8), channel_id=1, source_target_pairs={{16,32},{32,16},{48,64},{64,48},{80,96},{96,80},{112,128},{128,112... | collective-permute-start | bytes 491528 | tf_op jit(solution)/shard_map/ppermute | solution.py:343
  29.6 1.3 %copy-start.6 = (f32[2,2]{1,0:T(2,128)S(1)}, f32[2,2]{1,0:T(2,128)}, u32[]{:S(2)}) copy-start(f32[2,2]{1,0:T(2,128)} %trans.1) | copy-start | bytes 52
  31.8 6.5 %collective-permute-start.6 = (f32[2,2,2,3,16,128]{5,4,3,2,1,0:T(8,128)S(1)}, f32[2,2,2,3,16,128]{5,4,3,2,1,0:T(8,128)S(1)}, u32[]{:S(2)}, u32[]{:S(2)}) collective-permute-start(f32[2,2,2,3,16,128]{5,4,3,2,1,0:T(8,128)S(1)} %get-tuple-element.57), channel_id=1, source_target_pairs={{1,2},{2,1},{3,4},{4,3},{5,6},{6,5},{7,8},{8,7},{9,10},{10,9},{11,... | collective-permute-start | bytes 589832 | tf_op jit(solution)/shard_map/ppermute | solution.py:343
  32.5 8.9 %collective-permute-start.5 = (f32[2,2,2,3,16,128]{5,4,3,2,1,0:T(8,128)S(1)}, f32[2,2,2,3,16,128]{5,4,3,2,1,0:T(8,128)S(1)}, u32[]{:S(2)}, u32[]{:S(2)}) collective-permute-start(f32[2,2,2,3,16,128]{5,4,3,2,1,0:T(8,128)S(1)} %get-tuple-element.56), channel_id=1, source_target_pairs={{0,1},{1,0},{2,3},{3,2},{4,5},{5,4},{6,7},{7,6},{8,9},{9,8},{10,11... | collective-permute-start | bytes 589832 | tf_op jit(solution)/shard_map/ppermute | solution.py:343
  41.5 16.4 %collective-permute-start.7 = (f32[2,2,2,13,16,128]{5,4,3,2,1,0:T(8,128)S(1)}, f32[2,2,2,13,16,128]{5,4,3,2,1,0:T(8,128)S(1)}, u32[]{:S(2)}, u32[]{:S(2)}) collective-permute-start(f32[2,2,2,13,16,128]{5,4,3,2,1,0:T(8,128)S(1)} %pad_maximum_fusion.refs_2_), channel_id=1, source_target_pairs={{0,16},{16,0},{32,48},{48,32},{64,80},{80,64},{96,112},{112,96},{1... | collective-permute-start | bytes 2555912 | tf_op jit(solution)/shard_map/ppermute | solution.py:343
  41.6 16.2 %collective-permute-start.9 = (f32[2,2,2,8,16,128]{5,4,3,2,1,0:T(8,128)S(1)}, f32[2,2,2,8,16,128]{5,4,3,2,1,0:T(8,128)S(1)}, u32[]{:S(2)}, u32[]{:S(2)}) collective-permute-start(f32[2,2,2,8,16,128]{5,4,3,2,1,0:T(8,128)S(1)} %shard_map.81.refs_8_.force), channel_id=1, source_target_pairs={{16,32},{32,16},{48,64},{64,48},{80,96},{96,80},{112,128},{128,112... | collective-permute-start | bytes 1572872 | tf_op jit(solution)/shard_map/ppermute | solution.py:343
  47.4 10.3 %collective-permute-start.8 = (f32[2,2,2,5,16,128]{5,4,3,2,1,0:T(8,128)S(1)}, f32[2,2,2,5,16,128]{5,4,3,2,1,0:T(8,128)S(1)}, u32[]{:S(2)}, u32[]{:S(2)}) collective-permute-start(f32[2,2,2,5,16,128]{5,4,3,2,1,0:T(8,128)S(1)} %pad_maximum_fusion.6), channel_id=1, source_target_pairs={{16,32},{32,16},{48,64},{64,48},{80,96},{96,80},{112,128},{128,112... | collective-permute-start | bytes 983048 | tf_op jit(solution)/shard_map/ppermute | solution.py:343
  60.7 4.6 %collective-permute-start.11 = (f32[2,2,2,3,16,128]{5,4,3,2,1,0:T(8,128)S(1)}, f32[2,2,2,3,16,128]{5,4,3,2,1,0:T(8,128)S(1)}, u32[]{:S(2)}, u32[]{:S(2)}) collective-permute-start(f32[2,2,2,3,16,128]{5,4,3,2,1,0:T(8,128)S(1)} %get-tuple-element.55), channel_id=1, source_target_pairs={{1,2},{2,1},{3,4},{4,3},{5,6},{6,5},{7,8},{8,7},{9,10},{10,9},{11,... | collective-permute-start | bytes 589832 | tf_op jit(solution)/shard_map/ppermute | solution.py:343
  61.4 6.9 %collective-permute-start.10 = (f32[2,2,2,3,16,128]{5,4,3,2,1,0:T(8,128)S(1)}, f32[2,2,2,3,16,128]{5,4,3,2,1,0:T(8,128)S(1)}, u32[]{:S(2)}, u32[]{:S(2)}) collective-permute-start(f32[2,2,2,3,16,128]{5,4,3,2,1,0:T(8,128)S(1)} %get-tuple-element.54), channel_id=1, source_target_pairs={{0,1},{1,0},{2,3},{3,2},{4,5},{5,4},{6,7},{7,6},{8,9},{9,8},{10,11... | collective-permute-start | bytes 589832 | tf_op jit(solution)/shard_map/ppermute | solution.py:343
  68.5 17.0 %collective-permute-start.12 = (f32[2,2,2,13,16,128]{5,4,3,2,1,0:T(8,128)S(1)}, f32[2,2,2,13,16,128]{5,4,3,2,1,0:T(8,128)S(1)}, u32[]{:S(2)}, u32[]{:S(2)}) collective-permute-start(f32[2,2,2,13,16,128]{5,4,3,2,1,0:T(8,128)S(1)} %pad_maximum_fusion.2.refs_2_), channel_id=1, source_target_pairs={{0,16},{16,0},{32,48},{48,32},{64,80},{80,64},{96,112},{112,96},{1... | collective-permute-start | bytes 2555912 | tf_op jit(solution)/shard_map/ppermute | solution.py:343
  68.6 16.8 %collective-permute-start.14 = (f32[2,2,2,8,16,128]{5,4,3,2,1,0:T(8,128)S(1)}, f32[2,2,2,8,16,128]{5,4,3,2,1,0:T(8,128)S(1)}, u32[]{:S(2)}, u32[]{:S(2)}) collective-permute-start(f32[2,2,2,8,16,128]{5,4,3,2,1,0:T(8,128)S(1)} %shard_map.83.refs_9_.second), channel_id=1, source_target_pairs={{16,32},{32,16},{48,64},{64,48},{80,96},{96,80},{112,128},{128,112... | collective-permute-start | bytes 1572872 | tf_op jit(solution)/shard_map/ppermute | solution.py:343
  75.1 10.3 %collective-permute-start.13 = (f32[2,2,2,5,16,128]{5,4,3,2,1,0:T(8,128)S(1)}, f32[2,2,2,5,16,128]{5,4,3,2,1,0:T(8,128)S(1)}, u32[]{:S(2)}, u32[]{:S(2)}) collective-permute-start(f32[2,2,2,5,16,128]{5,4,3,2,1,0:T(8,128)S(1)} %pad_maximum_fusion.7), channel_id=1, source_target_pairs={{16,32},{32,16},{48,64},{64,48},{80,96},{96,80},{112,128},{128,112... | collective-permute-start | bytes 983048 | tf_op jit(solution)/shard_map/ppermute | solution.py:343
